TPU v7x, 32 devices: a whole 2x2x4 slice. The times are simulated.
32 devices in a mesh: dp: 8 (over z, y), tensor: 4 (over x, core).
Axes of the slice: x: 2, y: 2, z: 4, core: 2. Of those that a mesh axis runs over, the one named last changes fastest.
Arguments:
- tokens: bfloat16 [32768, 768], P(('dp', 'tensor')), may hold values from -6 to 6
- segment_ids: int32 [16, 2048], P('dp'), may hold values from 0 to 15, never falling along the last dimension, each value on 1 to 1024 neighbouring positions
- qkv_weight: bfloat16 [768, 3, 768], P('dp', None, 'tensor'), may hold values from -0.21875 to 0.21875
- qv_bias: bfloat16 [2, 768], P(None, 'tensor'), may hold values from -2 to 2
- out_weight: bfloat16 [768, 768], P('dp', 'tensor'), may hold values from -0.4375 to 0.4375
- out_bias: bfloat16 [768], replicated, may hold values from -2 to 2
- first_gain: bfloat16 [768], replicated, may hold values from 0.25 to 1.75
- first_shift: bfloat16 [768], replicated, may hold values from -2 to 2
- up_weight: bfloat16 [768, 3072], P('dp', 'tensor'), may hold values from -0.21875 to 0.21875
- up_bias: bfloat16 [3072], P('tensor'), may hold values from -3 to 3
- down_weight: bfloat16 [768, 3072], P('dp', 'tensor'), may hold values from -0.109375 to 0.109375
- down_bias: bfloat16 [768], replicated, may hold values from -2 to 2
- second_gain: bfloat16 [768], replicated, may hold values from 0.25 to 1.75
- second_shift: bfloat16 [768], replicated, may hold values from -2 to 2
- output_grad: bfloat16 [32768, 768], P(('dp', 'tensor')), may hold values from -6 to 6
Outputs:
- output: bfloat16 [32768, 768], P(('dp', 'tensor'))
- input_grad: float32 [32768, 768], P(('dp', 'tensor'))
- qkv_grad: float32 [768, 3, 768], P('dp', None, 'tensor')
- qv_bias_grad: float32 [2, 768], P(None, 'tensor')
- out_weight_grad: float32 [768, 768], P('dp', 'tensor')
- up_weight_grad: float32 [768, 3072], P('dp', 'tensor')
- up_bias_grad: float32 [3072], P('tensor')
- down_weight_grad: float32 [768, 3072], P('dp', 'tensor')
- vector_grads: float32 [6, 768], replicated
Inputs may be any that keep to these rules, and one draw needn't show every extreme that they name: `segment_ids`: document ids never fall along a sequence; each document has at most 1024 tokens.
All inputs are finite; a program needn't handle non-finite values.
Results may differ from a plain program's by a relative error of at most 0.015.
Values may be sent and summed in bfloat16 or wider, within the bound.
No kernel may reach another device: no remote copies, remote signals or barrier semaphores. Data moves between devices by JAX's collectives and lax.ppermute only.
A program may use at most 192 MiB of HBM per device.

v0:
```python
from functools import partial

import jax
import jax.numpy as jnp
from jax import lax
from jax.sharding import PartitionSpec as P

HEAD_DIM = 64


EPSILON = 1e-12
MASKED = -1e30


def matmul_plain(left, right):
    return jnp.dot(left, right, preferred_element_type=jnp.float32)


def times_transposed(left, right):
    return lax.dot_general(
        left, right, (((1,), (1,)), ((), ())), preferred_element_type=jnp.float32
    )


def over_rows(left, right):
    return lax.dot_general(
        left, right, (((0,), (0,)), ((), ())), preferred_element_type=jnp.float32
    )


def normalize(values, gain, shift):
    center = jnp.mean(values, axis=-1, keepdims=True)
    offset = values - center
    spread = jnp.mean(offset * offset, axis=-1, keepdims=True)
    inverse = lax.rsqrt(spread + EPSILON)
    normed = offset * inverse
    return (normed * gain + shift, normed, inverse)


def normalize_back(incoming, normed, inverse, gain):
    weighted = incoming * gain
    centered = weighted - jnp.mean(weighted, axis=-1, keepdims=True)
    centered = centered - normed * jnp.mean(weighted * normed, axis=-1, keepdims=True)
    return (centered * inverse, jnp.sum(incoming * normed, axis=0), jnp.sum(incoming, axis=0))


def masked_scores(query_rows, seg_rows, key_seq, seg_seq):
    scores = jnp.einsum(
        "qhd,khd->hqk", query_rows, key_seq, preferred_element_type=jnp.float32
    ) * HEAD_DIM ** (-0.5)
    same_doc = (seg_rows[:, None] == seg_seq[None, :])[None]
    return jnp.where(same_doc, scores, MASKED)


def attend_forward(query_seq, key_seq, value_seq, seg_seq, block_rows):
    block_count = query_seq.shape[0] // block_rows

    def one_block(block_index):
        first_row = block_index * block_rows
        query_rows = lax.dynamic_slice_in_dim(query_seq, first_row, block_rows, 0)
        seg_rows = lax.dynamic_slice_in_dim(seg_seq, first_row, block_rows, 0)
        scores = masked_scores(query_rows, seg_rows, key_seq, seg_seq)
        row_max = jnp.max(scores, axis=-1, keepdims=True)
        powers = jnp.exp(scores - row_max)
        row_total = jnp.sum(powers, axis=-1, keepdims=True)
        weights = (powers / row_total).astype(jnp.bfloat16)
        context = jnp.einsum("hqk,khd->qhd", weights, value_seq, preferred_element_type=jnp.float32)
        return (context, (row_max + jnp.log(row_total))[..., 0])

    contexts, log_sums = lax.map(one_block, jnp.arange(block_count, dtype=jnp.int32))
    return (contexts.reshape(query_seq.shape), log_sums)


def attend_backward(query_seq, key_seq, value_seq, seg_seq, log_sums, grad_seq, block_rows):
    block_count = query_seq.shape[0] // block_rows
    score_scale = HEAD_DIM ** (-0.5)

    def one_block(running, block_index):
        key_grad, value_grad = running
        first_row = block_index * block_rows
        query_rows = lax.dynamic_slice_in_dim(query_seq, first_row, block_rows, 0)
        seg_rows = lax.dynamic_slice_in_dim(seg_seq, first_row, block_rows, 0)
        grad_rows = lax.dynamic_slice_in_dim(grad_seq, first_row, block_rows, 0)
        scores = masked_scores(query_rows, seg_rows, key_seq, seg_seq)
        probs = jnp.exp(scores - log_sums[block_index][..., None])
        weights = probs.astype(jnp.bfloat16)
        prob_grad = jnp.einsum(
            "qhd,khd->hqk", grad_rows, value_seq, preferred_element_type=jnp.float32
        )
        inner = jnp.sum(probs * prob_grad, axis=-1, keepdims=True)
        score_grad = (probs * (prob_grad - inner)).astype(jnp.bfloat16)
        query_grad = (
            jnp.einsum("hqk,khd->qhd", score_grad, key_seq, preferred_element_type=jnp.float32)
            * score_scale
        )
        key_grad = (
            key_grad
            + jnp.einsum("hqk,qhd->khd", score_grad, query_rows, preferred_element_type=jnp.float32)
            * score_scale
        )
        value_grad = value_grad + jnp.einsum(
            "hqk,qhd->khd", weights, grad_rows, preferred_element_type=jnp.float32
        )
        return ((key_grad, value_grad), query_grad)

    empty_grad = jnp.zeros(key_seq.shape, jnp.float32)
    (key_grad, value_grad), query_grads = lax.scan(
        one_block, (empty_grad, empty_grad), jnp.arange(block_count, dtype=jnp.int32)
    )
    return (query_grads.reshape(query_seq.shape), key_grad, value_grad)


def local(
    tokens,
    segment_ids,
    qkv_weight,
    qv_bias,
    out_weight,
    out_bias,
    first_gain,
    first_shift,
    up_weight,
    up_bias,
    down_weight,
    down_bias,
    second_gain,
    second_shift,
    output_grad,
):
    row_count, model_width = tokens.shape
    sequences, seq_length = segment_ids.shape
    block_rows = min(512, seq_length)
    gathered = lax.all_gather(tokens, "tensor", axis=0, tiled=True)
    qkv_full, out_full, up_full, down_full = (
        lax.all_gather(qkv_weight, "dp", axis=0, tiled=True),
        lax.all_gather(out_weight, "dp", axis=0, tiled=True),
        lax.all_gather(up_weight, "dp", axis=0, tiled=True),
        lax.all_gather(down_weight, "dp", axis=0, tiled=True),
    )
    local_width = qkv_full.shape[2]
    shape_four = (sequences, seq_length, local_width // HEAD_DIM, HEAD_DIM)
    qkv_flat = qkv_full.reshape(model_width, 3 * local_width)
    bias_pair = qv_bias.astype(jnp.float32)
    projected = matmul_plain(gathered, qkv_flat)
    queries = (projected[:, :local_width] + bias_pair[0]).astype(jnp.bfloat16).reshape(shape_four)
    keys_all = projected[:, local_width : 2 * local_width].astype(jnp.bfloat16).reshape(shape_four)
    values_all = (
        (projected[:, 2 * local_width :] + bias_pair[1]).astype(jnp.bfloat16).reshape(shape_four)
    )

    def forward_sequence(packed):
        return attend_forward(packed[0], packed[1], packed[2], packed[3], block_rows)

    contexts, log_sums = lax.map(forward_sequence, (queries, keys_all, values_all, segment_ids))
    context = contexts.reshape(-1, local_width).astype(jnp.bfloat16)
    attended = lax.psum_scatter(
        times_transposed(context, out_full), "tensor", scatter_dimension=0, tiled=True
    )
    gain_one = first_gain.astype(jnp.float32)
    gain_two = second_gain.astype(jnp.float32)
    first, normed_one, inverse_one = normalize(
        tokens.astype(jnp.float32) + attended + out_bias.astype(jnp.float32),
        gain_one,
        first_shift.astype(jnp.float32),
    )
    first_low = first.astype(jnp.bfloat16)
    spread_rows = lax.all_gather(first_low, "tensor", axis=0, tiled=True)
    up_used, down_used = (up_full, down_full)
    hidden_bias = up_bias.astype(jnp.float32)
    hidden_pre = matmul_plain(spread_rows, up_used) + hidden_bias
    activated, gelu_back = jax.vjp(partial(jax.nn.gelu, approximate=False), hidden_pre)
    act_low = activated.astype(jnp.bfloat16)
    fed = lax.psum_scatter(
        times_transposed(
            lax.slice_in_dim(act_low, 0, lax.axis_size("tensor") * row_count, axis=0), down_used
        ).astype(jnp.bfloat16),
        "tensor",
        scatter_dimension=0,
        tiled=True,
    ).astype(jnp.float32)
    second, normed_two, inverse_two = normalize(
        first + fed + down_bias.astype(jnp.float32), gain_two, second_shift.astype(jnp.float32)
    )
    output = second.astype(jnp.bfloat16)
    grad_second, gain_two_g, shift_two_g = normalize_back(
        output_grad.astype(jnp.float32), normed_two, inverse_two, gain_two
    )
    fed_low = grad_second.astype(jnp.bfloat16)
    down_bias_g = jnp.sum(fed_low.astype(jnp.float32), axis=0)
    fed_rows = lax.all_gather(fed_low, "tensor", axis=0, tiled=True)
    act_grad = matmul_plain(fed_rows, down_used)
    pre_grad = gelu_back(act_grad)[0].astype(jnp.bfloat16)
    down_grad = over_rows(fed_rows, act_low)
    up_grad = over_rows(spread_rows, pre_grad)
    up_bias_g = jnp.sum(pre_grad.astype(jnp.float32), axis=0)
    first_grad = lax.psum_scatter(
        times_transposed(pre_grad, up_used).astype(jnp.bfloat16),
        "tensor",
        scatter_dimension=0,
        tiled=True,
    ).astype(jnp.float32)
    grad_first, gain_one_g, shift_one_g = normalize_back(
        grad_second + first_grad, normed_one, inverse_one, gain_one
    )
    attn_low = grad_first.astype(jnp.bfloat16)
    out_bias_g = jnp.sum(attn_low.astype(jnp.float32), axis=0)
    attn_rows = lax.all_gather(attn_low, "tensor", axis=0, tiled=True)
    context_grad = matmul_plain(attn_rows, out_full).astype(jnp.bfloat16).reshape(shape_four)
    out_weight_g = over_rows(attn_rows, context)

    def backward_sequence(packed):
        return attend_backward(
            packed[0], packed[1], packed[2], packed[3], packed[4], packed[5], block_rows
        )

    query_g, key_g, value_g = lax.map(
        backward_sequence, (queries, keys_all, values_all, segment_ids, log_sums, context_grad)
    )
    mixed_grad = jnp.concatenate(
        [
            query_g.reshape(-1, local_width),
            key_g.reshape(-1, local_width),
            value_g.reshape(-1, local_width),
        ],
        axis=1,
    ).astype(jnp.bfloat16)
    qkv_g = over_rows(gathered, mixed_grad).reshape(model_width, 3, local_width)
    mixed_wide = mixed_grad.astype(jnp.float32)
    qv_g = jnp.stack(
        [
            jnp.sum(mixed_wide[:, :local_width], axis=0),
            jnp.sum(mixed_wide[:, 2 * local_width :], axis=0),
        ]
    )
    input_grad = grad_first + lax.psum_scatter(
        times_transposed(mixed_grad, qkv_flat).astype(jnp.bfloat16),
        "tensor",
        scatter_dimension=0,
        tiled=True,
    ).astype(jnp.float32)
    qkv_share, out_share, up_share, down_share = (
        lax.psum_scatter(qkv_g, "dp", scatter_dimension=0, tiled=True),
        lax.psum_scatter(out_weight_g, "dp", scatter_dimension=0, tiled=True),
        lax.psum_scatter(up_grad, "dp", scatter_dimension=0, tiled=True),
        lax.psum_scatter(down_grad, "dp", scatter_dimension=0, tiled=True),
    )
    qv_share, up_bias_share = lax.psum((qv_g, up_bias_g), "dp")
    vectors = lax.psum(
        jnp.stack([out_bias_g, gain_one_g, shift_one_g, down_bias_g, gain_two_g, shift_two_g]),
        ("dp", "tensor"),
    )
    return (
        output,
        input_grad,
        qkv_share,
        qv_share,
        out_share,
        up_share,
        up_bias_share,
        down_share,
        vectors,
    )


def solution(mesh):
    in_specs = (
        P(("dp", "tensor"), None),
        P("dp", None),
        P("dp", None, "tensor"),
        P(None, "tensor"),
        P("dp", "tensor"),
        P(),
        P(),
        P(),
        P("dp", "tensor"),
        P("tensor"),
        P("dp", "tensor"),
        P(),
        P(),
        P(),
        P(("dp", "tensor"), None),
    )
    out_specs = (
        P(("dp", "tensor"), None),
        P(("dp", "tensor"), None),
        P("dp", None, "tensor"),
        P(None, "tensor"),
        P("dp", "tensor"),
        P("dp", "tensor"),
        P("tensor"),
        P("dp", "tensor"),
        P(),
    )
    return jax.shard_map(local, mesh=mesh, in_specs=in_specs, out_specs=out_specs, check_vma=False)
```

profile of v0, /device:TPU:0, one launch (start us, length us, event | category | flops | bytes accessed | tf_op | source)
XLA Modules:
  0.0 1469.8 jit_solution(13262983610031420961)
XLA Ops:
  9.9 38.8 %all_gather.25 = bf16[768,3,192]{2,1,0:T(4,128)(2,1)S(1)} all-gather(bf16[96,3,192]{2,1,0:T(4,128)(2,1)S(1)} %copy.55), channel_id=1, replica_groups=mesh['dp'=8,'tensor'=4] {'dp'}, dimensions={0}, use_global_device_ids=true | all-gather | bytes 995328 | tf_op jit(solution)/shard_map/all_gather | solution.py:135
  49.6 33.1 %all_gather.26 = bf16[768,192]{1,0:T(8,128)(2,1)} all-gather(bf16[96,192]{1,0:T(8,128)(2,1)S(1)} %copy-done.24), channel_id=1, replica_groups=mesh['dp'=8,'tensor'=4] {'dp'}, dimensions={0}, use_global_device_ids=true | all-gather | bytes 331776 | tf_op jit(solution)/shard_map/all_gather | solution.py:136
  109.5 194.5 %while.54 = (s32[]{:T(128)}, bf16[2,2048,3,64]{3,2,1,0:T(4,128)(2,1)}, f32[2,4,3,512]{3,2,1,0:T(4,128)S(1)}, bf16[2,2048,3,64]{1,3,2,0:T(8,128)(2,1)}, s32[2,204...) while((s32[]{:T(128)}, ...), condition=%wide.region_5.6_spmd, body=%wide.region_0.5_spmd.sunk | while | flops 844102144 | bytes 53436884 | solution.py:154
  113.1 90.5 %while.57 = (s32[]{:T(128)}, bf16[4,512,3,64]{1,3,2,0:T(8,128)(2,1)S(1)}, f32[4,3,512]{2,1,0:T(4,128)S(1)}, s32[4]{0:T(128)S(1)}, s32[2048]{0:T(1024)S(1)}, /*in...) while((s32[]{:T(128)}, ...), condition=%wide.region_4.4_spmd, body=%wide.region_1.3_spmd.sunk | while | flops 844102144 | bytes 44179652 | solution.py:70
  210.4 90.5 %while.57 = (s32[]{:T(128)}, bf16[4,512,3,64]{1,3,2,0:T(8,128)(2,1)S(1)}, f32[4,3,512]{2,1,0:T(4,128)S(1)}, s32[4]{0:T(128)S(1)}, s32[2048]{0:T(1024)S(1)}, /*in...) while((s32[]{:T(128)}, ...), condition=%wide.region_4.4_spmd, body=%wide.region_1.3_spmd.sunk | while | flops 844102144 | bytes 44179652 | solution.py:70
  323.0 97.6 %reduce-scatter.9.cloned.1.call-done = f32[1024,768]{1,0:T(8,128)} async-done(((f32[4096,768]{1,0:T(8,128)}), f32[1024,768]{1,0:T(8,128)}) %reduce-scatter.9.cloned.1.call-update) | async-done | bytes 3145744 | tf_op jit(solution)/shard_map/reduce_scatter | solution.py:156
  426.3 45.7 %all-gather.9.cloned.1.call-done = bf16[4096,768]{1,0:T(8,128)(2,1)} async-done(((bf16[1024,768]{1,0:T(8,128)(2,1)}), bf16[4096,768]{1,0:T(8,128)(2,1)}) %all-gather.9.cloned.1.call-update) | async-done | bytes 6291472 | tf_op jit(solution)/shard_map/all_gather | solution.py:167
  472.0 34.8 %multiply_convert_fusion.1 = (bf16[4096,768]{1,0:T(8,128)(2,1)}, f32[4096,768]{1,0:T(8,128)}, f32[4096,768]{1,0:T(8,128)}) fusion(f32[768]{0:T(1024)S(1)} %convert_element_type.114, bf16[4096,768]{1,0:T(8,128)(2,1)} %all-gather.9.cloned.1.call-done, bf16[768,768]{1,0:T(8,128)(2,1)} %all-gather.11.cloned.1.call-done), kind=kOutput, calls=%fused_computation.62 | convolution fusion | flops 5039456256 | bytes 38931456 | tf_op jit(solution)/shard_map/dot_general | solution.py:16
  524.8 10.3 all-gather.15.cloned.1.call-start
  535.2 46.4 %reduce-scatter.11.cloned.1.call-done = bf16[1024,768]{1,0:T(8,128)(2,1)} async-done(((bf16[4096,768]{1,0:T(8,128)(2,1)}), bf16[1024,768]{1,0:T(8,128)(2,1)}) %reduce-scatter.11.cloned.1.call-update) | async-done | bytes 1572880 | tf_op jit(solution)/shard_map/reduce_scatter | solution.py:173
  591.4 46.3 %all-gather.15.cloned.1.call-done = bf16[4096,768]{1,0:T(8,128)(2,1)} async-done(((bf16[1024,768]{1,0:T(8,128)(2,1)}), bf16[4096,768]{1,0:T(8,128)(2,1)}) %all-gather.15.cloned.1.call-update) | async-done | bytes 6291472 | tf_op jit(solution)/shard_map/all_gather | solution.py:190
  637.7 19.0 %convert_reduce_fusion = (f32[768]{0:T(1024)}, bf16[4096,768]{1,0:T(8,128)(2,1)}) fusion(f32[4096,768]{1,0:T(8,128)} %get-tuple-element.390, f32[4096,768]{1,0:T(8,128)} %get-tuple-element.406, f32[768]{0:T(1024)S(1)} %convert_element_type.114, bf16[4096,768]{1,0:T(8,128)(2,1)} %all-gather.15.cloned.1.call-done, ...), kind=kOutput, calls=%fused_computation.60 | convolution fusion | flops 4885314560 | bytes 38934528 | tf_op jit(solution)/shard_map/dot_general | solution.py:16
  666.5 58.4 %reduce-scatter.13.cloned.1.call-done = bf16[1024,768]{1,0:T(8,128)(2,1)} async-done(((bf16[4096,768]{1,0:T(8,128)(2,1)}), bf16[1024,768]{1,0:T(8,128)(2,1)}) %reduce-scatter.13.cloned.1.call-update) | async-done | bytes 1572880 | tf_op jit(solution)/shard_map/reduce_scatter | solution.py:196
  732.7 46.3 %all-gather.17.cloned.1.call-done = bf16[4096,768]{1,0:T(8,128)(2,1)} async-done(((bf16[1024,768]{1,0:T(8,128)(2,1)}), bf16[4096,768]{1,0:T(8,128)(2,1)}) %all-gather.17.cloned.1.call-update) | async-done | bytes 6291472 | tf_op jit(solution)/shard_map/all_gather | solution.py:207
  789.8 301.9 %while.56 = (s32[]{:T(128)}, bf16[2,2048,3,64]{3,2,1,0:T(4,128)(2,1)}, bf16[2,2048,3,64]{1,3,2,0:T(8,128)(2,1)}, bf16[2,2048,3,64]{1,3,2,0:T(8,128)(2,1)}, bf16[...) while((s32[]{:T(128)}, ...), condition=%wide.region_21.22_spmd, body=%wide.region_17.21_spmd.sunk | while | flops 2063563264 | bytes 193981360 | solution.py:216
  797.4 132.6 %while.58 = (s32[]{:T(128)}, f32[2048,3,64]{0,2,1:T(8,128)}, f32[2048,3,64]{0,2,1:T(8,128)}, bf16[4,512,3,64]{1,3,2,0:T(8,128)(2,1)}, s32[4]{0:T(128)S(1)}, /*in...) while((s32[]{:T(128)}, f32[2048,3,64]{0,2,1:T(8,128)}, ...), condition=%wide.region_20.20_spmd.clone, body=%wide.region_18.19_spmd.clone.sunk | while | flops 2063563264 | bytes 156690960 | solution.py:107
  948.1 132.6 %while.58 = (s32[]{:T(128)}, f32[2048,3,64]{0,2,1:T(8,128)}, f32[2048,3,64]{0,2,1:T(8,128)}, bf16[4,512,3,64]{1,3,2,0:T(8,128)(2,1)}, s32[4]{0:T(128)S(1)}, /*in...) while((s32[]{:T(128)}, f32[2048,3,64]{0,2,1:T(8,128)}, ...), condition=%wide.region_20.20_spmd.clone, body=%wide.region_18.19_spmd.clone.sunk | while | flops 2063563264 | bytes 156690960 | solution.py:107
  1129.1 11.1 fusion.63
  1156.0 41.0 %psum.23 = f32[6,768]{1,0:T(8,128)} all-reduce(f32[6,768]{1,0:T(8,128)S(1)} %stack.39), channel_id=1, replica_groups=mesh['dp'=8,'tensor'=4] {'dp','tensor'}, use_global_device_ids=true, to_apply=%region_38.39 | all-reduce | flops 4608 | bytes 36864 | tf_op jit(solution)/shard_map/psum | solution.py:248
  1201.3 22.6 %all-reduce = (f32[2,192]{1,0:T(2,128)}, f32[768]{0:T(1024)}) all-reduce(f32[2,192]{1,0:T(2,128)S(1)} %pad_maximum_fusion, f32[768]{0:T(1024)S(1)} %copy-done.31), channel_id=1, replica_groups=mesh['dp'=8,'tensor'=4] {'dp'}, use_global_device_ids=true, to_apply=%region_26.27 | all-reduce | flops 1152 | bytes 9216 | tf_op jit(solution)/shard_map/psum | solution.py:247
  1227.2 24.7 %reduce-scatter.21.cloned.1.call-done = f32[96,768]{1,0:T(8,128)} async-done(((f32[768,768]{1,0:T(8,128)}), f32[96,768]{1,0:T(8,128)}) %reduce-scatter.21.cloned.1.call-update) | async-done | bytes 294928 | tf_op jit(solution)/shard_map/reduce_scatter | solution.py:244
  1251.9 72.5 %reduce-scatter.23.cloned.1.call-done = f32[96,768]{1,0:T(8,128)} async-done(((f32[768,768]{1,0:T(8,128)}), f32[96,768]{1,0:T(8,128)}) %reduce-scatter.23.cloned.1.call-update) | async-done | bytes 294928 | tf_op jit(solution)/shard_map/reduce_scatter | solution.py:245
  1324.4 65.9 %reduce-scatter.19.cloned.1.call-done = f32[96,192]{1,0:T(8,128)} async-done(((f32[768,192]{1,0:T(8,128)}), f32[96,192]{1,0:T(8,128)}) %reduce-scatter.19.cloned.1.call-update) | async-done | bytes 73744 | tf_op jit(solution)/shard_map/reduce_scatter | solution.py:243
  1390.2 72.0 %reduce-scatter.17.cloned.1.call-done = f32[96,3,192]{2,0,1:T(8,128)} async-done(((f32[768,3,192]{2,0,1:T(8,128)}), f32[96,3,192]{2,0,1:T(8,128)}) %reduce-scatter.17.cloned.1.call-update) | async-done | bytes 221200 | tf_op jit(solution)/shard_map/reduce_scatter | solution.py:242
  (484 shorter events, 638.9 us)
Async XLA Ops:
  8.0 41.6 %copy-start.24 = (bf16[96,192]{1,0:T(8,128)(2,1)S(1)}, bf16[96,192]{1,0:T(8,128)(2,1)}, u32[]{:S(2)}) copy-start(bf16[96,192]{1,0:T(8,128)(2,1)} %param.27) | copy-start | bytes 110596
  8.0 74.7 %copy-start.32 = (bf16[2,192]{1,0:T(2,128)(2,1)S(1)}, bf16[2,192]{1,0:T(2,128)(2,1)}, u32[]{:S(2)}) copy-start(bf16[2,192]{1,0:T(2,128)(2,1)} %param.26) | copy-start | bytes 2308
  8.0 74.7 %all-gather.7.cloned.1.call-start = ((), (), s32[]{:S(2)}) async-start(), calls=%async_computation.8 | async-start | bytes 7864320 | tf_op jit(solution)/shard_map/all_gather | solution.py:133
  8.8 411.8 %reduce-scatter.9.cloned.1.call-start = ((), (), s32[]{:S(2)}) async-start(), calls=%async_computation.9 | async-start | bytes 15728640 | tf_op jit(solution)/shard_map/reduce_scatter | solution.py:156
  49.6 33.2 %copy-start.20 = (bf16[768,3,192]{0,2,1:T(8,128)(2,1)}, bf16[768,3,192]{0,2,1:T(8,128)(2,1)S(1)}, u32[]{:S(2)}) copy-start(bf16[768,3,192]{0,2,1:T(8,128)(2,1)S(1)} %copy.56) | copy-start | bytes 2654212
  304.0 18.3 %copy-start.22 = (f32[2,4,3,512]{3,2,1,0:T(4,128)}, f32[2,4,3,512]{3,2,1,0:T(4,128)S(1)}, u32[]{:S(2)}) copy-start(f32[2,4,3,512]{3,2,1,0:T(4,128)S(1)} %get-tuple-element.826) | copy-start | bytes 147460
  304.0 11.8 copy-start.16
  322.3 104.0 %all-gather.11.cloned.1.call-start = ((), (), s32[]{:S(2)}) async-start(), calls=%async_computation.11 | async-start | bytes 1327104 | tf_op jit(solution)/shard_map/all_gather | solution.py:137
  322.9 149.1 %all-gather.9.cloned.1.call-start = ((), (), s32[]{:S(2)}) async-start(), calls=%async_computation.10 | async-start | bytes 7864320 | tf_op jit(solution)/shard_map/all_gather | solution.py:167
  425.6 90.0 %all-gather.13.cloned.1.call-start = ((), (), s32[]{:S(2)}) async-start(), calls=%async_computation.12 | async-start | bytes 1327104 | tf_op jit(solution)/shard_map/all_gather | solution.py:138
  426.2 155.4 %reduce-scatter.11.cloned.1.call-start = ((), (), s32[]{:S(2)}) async-start(), calls=%async_computation.13 | async-start | bytes 7864320 | tf_op jit(solution)/shard_map/reduce_scatter | solution.py:173
  524.8 10.4 copy-start.39
  524.8 112.9 %all-gather.15.cloned.1.call-start = ((), (), s32[]{:S(2)}) async-start(), calls=%async_computation.14 | async-start | bytes 7864320 | tf_op jit(solution)/shard_map/all_gather | solution.py:190
  591.3 133.6 %reduce-scatter.13.cloned.1.call-start = ((), (), s32[]{:S(2)}) async-start(), calls=%async_computation.15 | async-start | bytes 7864320 | tf_op jit(solution)/shard_map/reduce_scatter | solution.py:196
  637.7 19.0 %copy-start.40 = (bf16[768,768]{1,0:T(8,128)(2,1)S(1)}, bf16[768,768]{1,0:T(8,128)(2,1)}, u32[]{:S(2)}) copy-start(bf16[768,768]{1,0:T(8,128)(2,1)} %all-gather.11.cloned.1.call-done) | copy-start | bytes 3538948
  666.5 112.5 %all-gather.17.cloned.1.call-start = ((), (), s32[]{:S(2)}) async-start(), calls=%async_computation.16 | async-start | bytes 7864320 | tf_op jit(solution)/shard_map/all_gather | solution.py:207
  729.0 49.9 %copy-start.17 = (bf16[768,192]{1,0:T(8,128)(2,1)S(1)}, bf16[768,192]{1,0:T(8,128)(2,1)}, u32[]{:S(2)}) copy-start(bf16[768,192]{1,0:T(8,128)(2,1)} %all_gather.26) | copy-start | bytes 884740
  732.6 491.2 %reduce-scatter.15.cloned.1.call-start = ((), (), s32[]{:S(2)}) async-start(), calls=%async_computation.17 | async-start | bytes 7864320 | tf_op jit(solution)/shard_map/reduce_scatter | solution.py:235
  1118.9 133.0 %reduce-scatter.21.cloned.1.call-start = ((), (), s32[]{:S(2)}) async-start(), calls=%async_computation.20 | async-start | bytes 2654208 | tf_op jit(solution)/shard_map/reduce_scatter | solution.py:244
  1129.1 11.3 copy-start.13
  1129.1 195.3 %reduce-scatter.23.cloned.1.call-start = ((), (), s32[]{:S(2)}) async-start(), calls=%async_computation.21 | async-start | bytes 2654208 | tf_op jit(solution)/shard_map/reduce_scatter | solution.py:245
  1140.3 249.9 %reduce-scatter.19.cloned.1.call-start = ((), (), s32[]{:S(2)}) async-start(), calls=%async_computation.19 | async-start | bytes 884736 | tf_op jit(solution)/shard_map/reduce_scatter | solution.py:243
  1146.2 316.1 %reduce-scatter.17.cloned.1.call-start = ((), (), s32[]{:S(2)}) async-start(), calls=%async_computation.18 | async-start | bytes 2654208 | tf_op jit(solution)/shard_map/reduce_scatter | solution.py:242
  1200.6 23.3 %copy-start.10 = (f32[1024,768]{1,0:T(8,128)S(1)}, f32[1024,768]{1,0:T(8,128)}, u32[]{:S(2)}) copy-start(f32[1024,768]{1,0:T(8,128)} %get-tuple-element.384) | copy-start | bytes 9437188
  (90 other events, 401.4 us)
Sparse Core Ops, SparseCore 0:
  10.4 49.0 all-gather.6
  322.4 98.1 reduce-scatter.8
  666.6 58.3 reduce-scatter.12
Sparse Core Ops, SparseCore 1:
  324.9 40.6 all-gather.10
  425.7 46.2 all-gather.8
  474.1 41.5 all-gather.12
  524.9 56.7 reduce-scatter.10
  591.4 46.2 all-gather.14
  732.7 46.2 all-gather.16
  1119.0 58.9 reduce-scatter.14
  1182.3 69.5 reduce-scatter.20
  1256.3 68.0 reduce-scatter.22
  1328.6 61.6 reduce-scatter.18
  1394.2 68.0 reduce-scatter.16
where the time goes:
time: 1480 us; the launch traced here: 1470 us
  waiting for transfers between devices  586 us (40%)
  matrix products  424 us (29%)
  other arithmetic  146 us (10%)
  blocking collectives  136 us (9%)
  local copies, waits for them, and re-layouts  122 us (8%)
  loops' own time  28 us (2%)
  between operations  16.4 us (1%)
    reduce_scatter x1, waiting for transfers between devices, local(): lax.psum_scatter(times_transposed(context, out_full), 'tensor', scatter_d...  97.6 us
    reduce_scatter x1, waiting for transfers between devices, local(): lax.psum_scatter(down_grad, 'dp', scatter_dimension=0, tiled=True)  72.5 us
    reduce_scatter x1, waiting for transfers between devices, local(): lax.psum_scatter(qkv_g, 'dp', scatter_dimension=0, tiled=True)  72 us
    dot_general x16, matrix products, masked_scores(): jnp.einsum('qhd,khd->hqk', query_rows, key_seq, preferred_element_type=jn...  71.9 us
    reduce_scatter x1, waiting for transfers between devices, local(): lax.psum_scatter(out_weight_g, 'dp', scatter_dimension=0, tiled=True)  65.9 us
    dot_general x4, matrix products, matmul_plain(): return jnp.dot(left, right, preferred_element_type=jnp.float32)  64.8 us
    reduce_scatter x1, waiting for transfers between devices, local(): lax.psum_scatter(times_transposed(pre_grad, up_used).astype(jnp.bfloat16)...  58.4 us
    reduce_sum x8, other arithmetic, one_block(): row_total = jnp.sum(powers, axis=-1, keepdims=True)  54.1 us
  transfers between devices with their start and end apart: 14, of which 11 were waited for; matrix products, arithmetic and copies ran while one was open for 6% of the time, Pallas kernels for 0%

commit v1 on v0

v1 whole, which is shorter than its diff:
```python
from functools import partial

import jax
import jax.numpy as jnp
from jax import lax
from jax.experimental import pallas as pl
from jax.experimental.pallas import tpu as pltpu
from jax.sharding import Mesh
from jax.sharding import PartitionSpec as P

HEAD_DIM = 64
PAIR = 2 * HEAD_DIM
EPSILON = 1e-12
MASKED = -1e30
BLOCK = 256
F32 = jnp.float32
BF16 = jnp.bfloat16
VMEM_BYTES = 60 << 20


def dot_nn(left, right):
    return jnp.dot(left, right, preferred_element_type=F32)


def dot_nt(left, right):
    return lax.dot_general(left, right, (((1,), (1,)), ((), ())), preferred_element_type=F32)


def call(body, outs, ins, in_specs=None, out_specs=None, scratch=(), grid=(), flops=0, name=None, alias=None):
    whole = pl.BlockSpec(memory_space=pltpu.VMEM)
    moved = sum(a.size * a.dtype.itemsize for a in ins) + sum(o.size * o.dtype.itemsize for o in outs)
    return pl.pallas_call(
        body,
        grid=grid,
        out_shape=outs,
        in_specs=in_specs or [whole] * len(ins),
        out_specs=out_specs or [whole] * len(outs),
        scratch_shapes=list(scratch),
        compiler_params=pltpu.CompilerParams(vmem_limit_bytes=VMEM_BYTES),
        cost_estimate=pl.CostEstimate(flops=int(flops), bytes_accessed=int(moved), transcendentals=0),
        input_output_aliases=alias or {},
        name=name,
    )(*ins)


ANY = pl.BlockSpec(memory_space=pl.ANY)
SMEM = pl.BlockSpec(memory_space=pltpu.SMEM)
VMEM = pl.BlockSpec(memory_space=pltpu.VMEM)


def shape_of(shape, dtype):
    return jax.ShapeDtypeStruct(shape, dtype)


class Grid:
    def __init__(self, mesh):
        n_dp, n_tensor = mesh.devices.shape
        assert n_tensor == 4 and n_dp % 2 == 0
        self.ny = 2
        self.nz = n_dp // 2
        self.n_dp = n_dp
        self.mesh = Mesh(mesh.devices.reshape(self.nz, 2, 2, 2), ("z", "y", "x", "c"))

    def swap(self, array, axis, r=1):
        size = self.nz if axis == "z" else 2
        return lax.ppermute(array, axis, [(i, i ^ r) for i in range(size)])

    def regular(self, rows):
        return rows % 32 == 0 and self.nz & (self.nz - 1) == 0


class Pieces:
    def __init__(self, arrays, entries):
        self.arrays = arrays
        self.entries = entries


def gather(g, shard, both_ends, order):
    rows = shard.shape[0]
    if not g.regular(rows):
        full = lax.all_gather(shard, ("z", "y"), axis=0, tiled=True)[None, None]
        return Pieces([full, g.swap(full, "x")], [(0, 0, 0, 0, 0, 0, full.shape[2]), (1, 0, 0, 1, 0, 0, full.shape[2])])
    near = [shard] + [g.swap(shard, "z", r) for r in range(1, g.nz)]
    arrays, entries = [], []
    parts = [(0, rows // 2, "x"), (rows // 2, rows // 2, "y")] if both_ends else [(0, rows, order)]
    for first, size, axis in parts:
        line = jnp.stack([part[first : first + size] for part in near])
        other = "y" if axis == "x" else "x"
        two = jnp.stack([line, g.swap(line, axis)])
        four = g.swap(two, other)
        for index, array in ((0, two), (1, four)):
            for i in range(2):
                rx, ry = (i, index) if axis == "x" else (index, i)
                for k in range(g.nz):
                    entries.append((len(arrays), i, k, rx, k * 2 + ry, first, size))
            arrays.append(array)
    return Pieces(arrays, entries)


def across_cores(g, pieces):
    count = len(pieces.arrays)
    return Pieces(
        pieces.arrays + [g.swap(a, "c") for a in pieces.arrays],
        [(a, i, k, r * 2, s, f, n) for a, i, k, r, s, f, n in pieces.entries]
        + [(a + count, i, k, r * 2 + 1, s, f, n) for a, i, k, r, s, f, n in pieces.entries],
    )


def load_pieces(entries, refs, offsets, target, sems):
    slots = 1 + max(entry[4] for entry in entries)
    copies = []
    for number, (a, i, k, place, slot, first, size) in enumerate(entries):
        row = pl.multiple_of((slot ^ offsets) * (target.shape[1] // slots) + first, 16)
        copies.append(
            pltpu.make_async_copy(refs[a].at[i, k], target.at[place, pl.ds(row, size)], sems.at[number])
        )
    for copy in copies:
        copy.start()
    for copy in copies:
        copy.wait()


def scatter_layout(g, rows, lanes, order):
    if not g.regular(rows):
        return shape_of((1, 1, rows * g.n_dp, lanes), BF16)
    return shape_of((2, g.nz, rows, lanes), BF16)


def scatter_sum(g, kept, sent, rows, order):
    if not g.regular(rows):
        both = kept[0, 0].astype(F32) + g.swap(sent, "x")[0, 0].astype(F32)
        return lax.psum_scatter(both, ("z", "y"), scatter_dimension=0, tiled=True)
    other = "y" if order == "x" else "x"
    first = g.swap(sent, order)
    away = (kept[1].astype(F32) + first[1].astype(F32)).astype(BF16)
    second = g.swap(away, other)
    line = kept[0].astype(F32) + first[0].astype(F32) + second.astype(F32)
    total = line[0]
    for r in range(1, g.nz):
        total = total + g.swap(line[r].astype(BF16), "z", r).astype(F32)
    return total


def attention_forward(entries, count, meta, lows, highs, *refs):
    pieces = refs[:count]
    own, other, bias, seg_col, seg_row = refs[count : count + 5]
    (q_out, k_out, v_out, ctx_own, ctx_other, lse, w_out, o_out) = refs[count + 5 : count + 13]
    weights, scores, q_masked, sems = refs[count + 13 :]
    rows = own.shape[0]
    core = meta[0]
    load_pieces(entries, pieces, meta[1], weights, sems)
    d = HEAD_DIM
    first, second = weights[0], weights[1]
    pairs = [
        jnp.concatenate([first[:, n * d : (n + 1) * d], second[:, n * d : (n + 1) * d]], axis=1)
        for n in range(4)
    ]
    joined = jnp.concatenate(pairs[:3], axis=1)
    w_out[...] = joined
    o_out[...] = pairs[3]
    lane = lax.broadcasted_iota(jnp.int32, (BLOCK, PAIR), 1)
    left = lane < d
    for source, base in ((own, core * rows), (other, (1 - core) * rows)):
        for r in range(0, rows, BLOCK):
            acc = dot_nn(source[r : r + BLOCK, :], joined)
            at = pl.ds(pl.multiple_of(base + r, BLOCK), BLOCK)
            q = ((acc[:, :PAIR] + bias[0:1, :]).astype(BF16).astype(F32)) * d**-0.5
            q_out[at, :] = q.astype(BF16)
            q_masked[0, at, :] = jnp.where(left, q, 0.0).astype(BF16)
            q_masked[1, at, :] = jnp.where(left, 0.0, q).astype(BF16)
            k_out[at, :] = acc[:, PAIR : 2 * PAIR].astype(BF16)
            v_out[at, :] = (acc[:, 2 * PAIR :] + bias[1:2, :]).astype(BF16)

    def query_block(i, carry):
        at = pl.ds(pl.multiple_of(i * BLOCK, BLOCK), BLOCK)
        seg_q = seg_col[at, :]
        low, high = lows[i], highs[i]
        queries = [q_masked[h, at, :] for h in range(2)]

        def score_block(b, tops):
            keys = k_out[pl.ds(pl.multiple_of(b * BLOCK, BLOCK), BLOCK), :]
            same = seg_q == seg_row[b]
            new = []
            for h in range(2):
                s = jnp.where(same, dot_nt(queries[h], keys), MASKED)
                scores[h, b] = s
                new.append(jnp.maximum(tops[h], jnp.maximum(s[:, :128], s[:, 128:])))
            return tuple(new)

        low_value = jnp.full((BLOCK, 128), MASKED, F32)
        tops = lax.fori_loop(low, high, score_block, (low_value, low_value))
        tops = [jnp.max(t, axis=1, keepdims=True) for t in tops]

        def value_block(b, carry):
            values = v_out[pl.ds(pl.multiple_of(b * BLOCK, BLOCK), BLOCK), :]
            new = []
            for h in range(2):
                total, acc = carry[2 * h], carry[2 * h + 1]
                p = jnp.exp(scores[h, b] - tops[h])
                new.append(total + (p[:, :128] + p[:, 128:]))
                new.append(acc + dot_nn(p.astype(BF16), values))
            return tuple(new)

        zero = jnp.zeros((BLOCK, 128), F32)
        sums = lax.fori_loop(low, high, value_block, (zero,) * 4)
        totals = [jnp.sum(sums[2 * h], axis=1, keepdims=True) for h in range(2)]
        ctx = jnp.where(left, sums[1] / totals[0], sums[3] / totals[1]).astype(BF16)
        for h in range(2):
            column = jnp.broadcast_to(tops[h] + jnp.log(totals[h]), (BLOCK, 128))
            lse[i, h : h + 1, :] = column.T[0:1, :]
        half = i // (rows // BLOCK)
        place = pl.ds(pl.multiple_of((i - half * (rows // BLOCK)) * BLOCK, BLOCK), BLOCK)

        @pl.when(half == core)
        def _():
            ctx_own[place, :] = ctx

        @pl.when(half != core)
        def _():
            ctx_other[place, :] = ctx

        return carry

    lax.fori_loop(0, 2 * rows // BLOCK, query_block, 0)


def attention_backward(
    meta, lows, highs, own, other, da_own, da_other, q, k, v, ctx_own, ctx_other, lse, w, wo, seg_col, seg_row, ig_own,
    ig_other, keep_out, send_out, ig_own_out, ig_other_out, bias_out, q_masked, d_masked, dq_t, k_t, dqkv, delta, token_t,
    da_t, context,
):
    rows = own.shape[0]
    seq = 2 * rows
    core = meta[0]
    d = HEAD_DIM
    lane = lax.broadcasted_iota(jnp.int32, (BLOCK, PAIR), 1)
    left = lane < d
    weights_o = wo[...]
    for source, values, base in ((da_own, ctx_own, core * rows), (da_other, ctx_other, (1 - core) * rows)):
        for r in range(0, rows, BLOCK):
            at = pl.ds(pl.multiple_of(base + r, BLOCK), BLOCK)
            grad = dot_nn(source[r : r + BLOCK, :], weights_o).astype(BF16).astype(F32)
            d_masked[0, at, :] = jnp.where(left, grad, 0.0).astype(BF16)
            d_masked[1, at, :] = jnp.where(left, 0.0, grad).astype(BF16)
            prod = (grad * values[r : r + BLOCK, :].astype(F32)).T
            block = (base + r) // BLOCK
            delta[block, 0:1, :] = jnp.sum(prod[:d], axis=0, keepdims=True)
            delta[block, 1:2, :] = jnp.sum(prod[d:], axis=0, keepdims=True)
            query = q[at, :].astype(F32)
            q_masked[0, at, :] = jnp.where(left, query, 0.0).astype(BF16)
            q_masked[1, at, :] = jnp.where(left, 0.0, query).astype(BF16)
    for r in range(0, seq, BLOCK):
        k_t[:, r : r + BLOCK] = k[r : r + BLOCK, :].T
    dq_t[...] = jnp.zeros_like(dq_t)

    def key_block(b, carry):
        at = pl.ds(pl.multiple_of(b * BLOCK, BLOCK), BLOCK)
        keys, values = k[at, :], v[at, :]
        keys_t = k_t[:, at]
        seg_k = seg_col[at, :]

        def query_block(i, grads):
            dk, dv = grads
            rows_q = pl.ds(pl.multiple_of(i * BLOCK, BLOCK), BLOCK)
            same = seg_k == seg_row[i]
            for h in range(2):
                queries, grad = q_masked[h, rows_q, :], d_masked[h, rows_q, :]
                s = jnp.where(same, dot_nt(keys, queries), MASKED)
                p = jnp.exp(s - lse[i, h : h + 1, :])
                dp = dot_nt(values, grad)
                ds = (p * (dp - delta[i, h : h + 1, :])).astype(BF16)
                dv = dv + dot_nn(p.astype(BF16), grad)
                dk = dk + dot_nn(ds, queries)
                dq_t[h * d : (h + 1) * d, rows_q] += dot_nn(keys_t[h * d : (h + 1) * d, :], ds)
            return dk, dv

        zero = jnp.zeros((BLOCK, PAIR), F32)
        dk, dv = lax.fori_loop(lows[b], highs[b], query_block, (zero, zero))
        dqkv[at, PAIR : 2 * PAIR] = dk.astype(BF16)
        dqkv[at, 2 * PAIR :] = dv.astype(BF16)
        return carry

    lax.fori_loop(0, seq // BLOCK, key_block, 0)
    for r in range(0, seq, BLOCK):
        dqkv[r : r + BLOCK, :PAIR] = (dq_t[:, r : r + BLOCK].T * d**-0.5).astype(BF16)
    total = jnp.zeros((1, 3 * PAIR), F32)
    for r in range(0, seq, BLOCK):
        total = total + jnp.sum(dqkv[r : r + BLOCK, :].astype(F32), axis=0, keepdims=True)
    bias_out[0:1, :] = total
    weights = w[...]
    for base, before, after in ((core * rows, ig_own, ig_own_out), ((1 - core) * rows, ig_other, ig_other_out)):
        for r in range(0, rows, BLOCK):
            at = pl.ds(pl.multiple_of(base + r, BLOCK), BLOCK)
            grad = dot_nt(dqkv[at, :], weights)
            if before is not None:
                grad = grad + before[r : r + BLOCK, :].astype(F32)
            after[r : r + BLOCK, :] = grad.astype(after.dtype)
    for base, source, grads in ((core * rows, own, da_own), ((1 - core) * rows, other, da_other)):
        for r in range(0, rows, BLOCK):
            at = pl.ds(pl.multiple_of(base + r, BLOCK), BLOCK)
            token_t[:, at] = source[r : r + BLOCK, :].T
            da_t[:, at] = grads[r : r + BLOCK, :].T
    context[pl.ds(pl.multiple_of(core * rows, BLOCK), rows), :] = ctx_own[...]
    context[pl.ds(pl.multiple_of((1 - core) * rows, BLOCK), rows), :] = ctx_other[...]
    part = dot_nn(token_t[...], dqkv[...])
    part_o = dot_nn(da_t[...], context[...])
    kinds = [part[:, n * PAIR : (n + 1) * PAIR] for n in range(3)] + [part_o]
    store_blocks(jnp.concatenate([kind[:, :d] for kind in kinds], axis=1), keep_out, meta[1])
    store_blocks(jnp.concatenate([kind[:, d:] for kind in kinds], axis=1), send_out, meta[1])


def store_blocks(value, target, index, lanes=slice(None)):
    ny, nz, size = target.shape[:3]
    for block in range(value.shape[0] // size):
        slot = block ^ index
        target[lax.rem(slot, ny), lax.div(slot, ny), :, lanes] = value[block * size : (block + 1) * size].astype(BF16)


def normalize(values):
    center = jnp.mean(values, axis=-1, keepdims=True)
    offset = values - center
    inverse = lax.rsqrt(jnp.mean(offset * offset, axis=-1, keepdims=True) + EPSILON)
    return offset * inverse, inverse


def normalize_back(incoming, normed, inverse, gain):
    weighted = incoming * gain
    centered = weighted - jnp.mean(weighted, axis=-1, keepdims=True)
    centered = centered - normed * jnp.mean(weighted * normed, axis=-1, keepdims=True)
    return centered * inverse


def column_sum(values):
    return jnp.sum(values, axis=0, keepdims=True)


def accumulate(target, row, value):
    @pl.when(pl.program_id(0) == 0)
    def _():
        target[row : row + 1, :] = value

    @pl.when(pl.program_id(0) != 0)
    def _():
        target[row : row + 1, :] += value


def project_and_norm(tokens, vectors, *refs):
    contexts, weights = refs[:6], refs[6:12]
    normed_out, inverse_out, low_out, weight, context = refs[12:]

    @pl.when(pl.program_id(0) == 0)
    def _():
        for n in range(6):
            weight[:, n * PAIR : (n + 1) * PAIR] = weights[n][...]

    for n in range(6):
        context[:, n * PAIR : (n + 1) * PAIR] = contexts[n][...]
    mixed = dot_nt(context[...], weight[...])
    normed, inverse = normalize(tokens[...].astype(F32) + mixed + vectors[0:1, :])
    normed_out[...] = normed
    inverse_out[...] = inverse
    low_out[...] = (normed * vectors[1:2, :] + vectors[2:3, :]).astype(BF16)


def hidden_forward(entries, count, meta, *refs):
    pieces = refs[:count]
    low, bias, act_out, slope_out, weight, sems = refs[count:]

    @pl.when(pl.program_id(0) == 0)
    def _():
        load_pieces(entries, pieces, meta[1], weight, sems)

    width = weight.shape[2]
    for t in range(4):
        for n in range(0, width, BLOCK):
            at = slice(t * width + n, t * width + n + BLOCK)
            u = dot_nn(low[...], weight[t, :, n : n + BLOCK]) + bias[:, at]
            share = 0.5 + 0.5 * lax.erf(u * 0.5**0.5)
            act_out[:, at] = (u * share).astype(BF16)
            slope_out[:, at] = (share + u * (jnp.exp(-0.5 * u * u) * 0.3989422804014327)).astype(BF16)


def finish_forward(entries, count, meta, *refs):
    pieces = refs[:count]
    act, slope, normed_one, out_grad, vectors = refs[count : count + 5]
    output, dr2_out, df_out, du_out, sums, bias_sums, weight, sems = refs[count + 5 :]

    @pl.when(pl.program_id(0) == 0)
    def _():
        load_pieces(entries, pieces, meta[1], weight, sems)

    width = weight.shape[2]
    fed = vectors[3:4, :]
    for t in range(4):
        fed = fed + dot_nt(act[:, t * width : (t + 1) * width], weight[t])
    first = normed_one[...] * vectors[1:2, :] + vectors[2:3, :]
    normed, inverse = normalize(first + fed)
    output[...] = (normed * vectors[4:5, :] + vectors[5:6, :]).astype(BF16)
    incoming = out_grad[...].astype(F32)
    dr2 = normalize_back(incoming, normed, inverse, vectors[4:5, :])
    dr2_out[...] = dr2
    df = dr2.astype(BF16)
    df_out[...] = df
    accumulate(sums, 0, column_sum(df.astype(F32)))
    accumulate(sums, 1, column_sum(incoming * normed))
    accumulate(sums, 2, column_sum(incoming))
    parts = []
    for t in range(4):
        for n in range(0, width, BLOCK):
            at = slice(t * width + n, t * width + n + BLOCK)
            du = (dot_nn(df, weight[t, :, n : n + BLOCK]) * slope[:, at].astype(F32)).astype(BF16)
            du_out[:, at] = du
            parts.append(column_sum(du.astype(F32)))
    accumulate(bias_sums, 0, jnp.concatenate(parts, axis=1))


def grad_for_partner(left, right, out, left_t):
    @pl.when(pl.program_id(0) == 0)
    def _():
        left_t[...] = left[...].T

    for n in range(0, right.shape[1], BLOCK):
        out[0, :, n : n + BLOCK] = dot_nn(left_t[...], right[:, n : n + BLOCK]).astype(BF16)


def grad_for_chip(order, meta, left, right, received, keep, send, left_t):
    @pl.when(pl.program_id(0) == 0)
    def _():
        left_t[...] = left[...].T

    for place in range(2):
        @pl.when(pl.program_id(0) == place)
        def _():
            for n in range(0, right.shape[1], BLOCK):
                at = slice(n, n + BLOCK)
                value = dot_nn(left_t[...], right[:, at]) + received[0, :, at].astype(F32)
                if order == "x":
                    store_blocks(value, send if place else keep, meta[1], at)
                else:
                    ny, nz, size = keep.shape[:3]
                    for block in range(value.shape[0] // size):
                        rows = value[block * size : (block + 1) * size].astype(BF16)
                        slot = block ^ meta[1]

                        @pl.when(lax.rem(slot, 2) == 0)
                        def _():
                            keep[place, lax.div(slot, 2), :, at] = rows

                        @pl.when(lax.rem(slot, 2) == 1)
                        def _():
                            send[place, lax.div(slot, 2), :, at] = rows


def first_norm_back(entries, count, meta, *refs):
    pieces = refs[:count]
    du, dr2, normed, inverse, vectors, dr1_out, da_out, sums, weight, sems = refs[count:]

    @pl.when(pl.program_id(0) == 0)
    def _():
        load_pieces(entries, pieces, meta[1], weight, sems)

    width = weight.shape[2]
    incoming = dr2[...]
    for t in range(4):
        incoming = incoming + dot_nt(du[:, t * width : (t + 1) * width], weight[t])
    dr1 = normalize_back(incoming, normed[...], inverse[...], vectors[1:2, :])
    dr1_out[...] = dr1
    da = dr1.astype(BF16)
    da_out[...] = da
    accumulate(sums, 0, column_sum(da.astype(F32)))
    accumulate(sums, 1, column_sum(incoming * normed[...]))
    accumulate(sums, 2, column_sum(incoming))


def local(
    g,
    tokens,
    segment_ids,
    qkv_weight,
    qv_bias,
    out_weight,
    out_bias,
    first_gain,
    first_shift,
    up_weight,
    up_bias,
    down_weight,
    down_bias,
    second_gain,
    second_shift,
    output_grad,
):
    rows, width = tokens.shape
    seq = segment_ids.shape[1]
    heads = qkv_weight.shape[2] // HEAD_DIM
    hidden = up_weight.shape[1]
    shard = qkv_weight.shape[0]
    assert seq == 2 * rows and rows % BLOCK == 0
    d = HEAD_DIM
    z, y, x, c = (lax.axis_index(name) for name in ("z", "y", "x", "c"))
    regular = g.regular(shard)
    meta = jnp.stack([c, (z * 2 + y) if regular else c * 0]).astype(jnp.int32)

    segments = lax.dynamic_index_in_dim(segment_ids, x, 0, keepdims=False)
    blocks = seq // BLOCK
    by_block = segments.reshape(blocks, BLOCK)
    lows = jnp.sum((segments[None, :] < by_block[:, :1]).astype(jnp.int32), axis=1) // BLOCK
    highs = (jnp.sum((segments[None, :] <= by_block[:, -1:]).astype(jnp.int32), axis=1) + BLOCK - 1) // BLOCK
    seg_col = segments.reshape(seq, 1)
    seg_row = segments.reshape(blocks, 1, BLOCK)

    small = jnp.concatenate([up_bias, qv_bias.reshape(-1)]).reshape(1, -1)
    small = jnp.concatenate([small, g.swap(small, "c")], axis=0)
    small = jnp.concatenate([small, g.swap(small, "x")], axis=0).astype(F32)
    hidden_bias = small[:, :hidden].reshape(1, 4 * hidden)
    pair_bias = small[:, hidden:].reshape(2, 2, 2, heads, d)[:, 0]
    vectors = jnp.stack(
        [out_bias, first_gain, first_shift, down_bias, second_gain, second_shift, out_bias, out_bias]
    ).astype(F32)

    other_tokens = g.swap(tokens, "c")
    head_pieces = []
    for j in range(heads):
        at = slice(j * d, (j + 1) * d)
        chunk = jnp.concatenate(
            [qkv_weight[:, 0, at], qkv_weight[:, 1, at], qkv_weight[:, 2, at], out_weight[:, at]], axis=1
        )
        head_pieces.append(gather(g, chunk, True, "x"))
    up_pieces = across_cores(g, gather(g, up_weight, True, "x"))
    down_pieces = across_cores(g, gather(g, down_weight, True, "x"))

    saved = []
    for j in range(heads):
        pieces = head_pieces[j]
        count = len(pieces.arrays)
        bias = jnp.concatenate([pair_bias[0, :, j], pair_bias[1, :, j]], axis=1)
        ins = [meta, lows, highs, *pieces.arrays, tokens, other_tokens, bias, seg_col, seg_row]
        outs = [shape_of((seq, PAIR), BF16)] * 3 + [shape_of((rows, PAIR), BF16)] * 2
        outs += [shape_of((blocks, 8, BLOCK), F32), shape_of((width, 3 * PAIR), BF16), shape_of((width, PAIR), BF16)]
        saved.append(
            call(
                partial(attention_forward, pieces.entries, count),
                outs,
                ins,
                in_specs=[SMEM] * 3 + [ANY] * count + [VMEM] * 5,
                scratch=[
                    pltpu.VMEM((2, width, 4 * d), BF16),
                    pltpu.VMEM((2, blocks, BLOCK, BLOCK), F32),
                    pltpu.VMEM((2, seq, PAIR), BF16),
                    pltpu.SemaphoreType.DMA((len(pieces.entries),)),
                ],
                flops=2 * seq * width * 3 * PAIR + 8 * seq * seq * PAIR,
                name="attention_forward",
            )
        )
    contexts = [s[3] for s in saved] + [g.swap(s[4], "c") for s in saved]
    out_weights = [s[7] for s in saved] + [g.swap(s[7], "c") for s in saved]

    steps = (rows // BLOCK,)

    def by_rows(lanes):
        return pl.BlockSpec((BLOCK, lanes), lambda i: (i, 0))

    def fixed(array):
        return pl.BlockSpec(array.shape, lambda i: (0,) * len(array.shape))

    normed_one, inverse_one, first_low = call(
        project_and_norm,
        [shape_of((rows, width), F32), shape_of((rows, 1), F32), shape_of((rows, width), BF16)],
        [tokens, vectors, *contexts, *out_weights],
        in_specs=[by_rows(width), fixed(vectors)] + [by_rows(PAIR)] * 6 + [fixed(out_weights[0])] * 6,
        out_specs=[by_rows(width), by_rows(1), by_rows(width)],
        scratch=[pltpu.VMEM((width, width), BF16), pltpu.VMEM((BLOCK, width), BF16)],
        grid=steps,
        flops=2 * rows * width * width,
        name="project_and_norm",
    )
    ffn = 2 * rows * width * 4 * hidden
    weight_scratch = pltpu.VMEM((4, width, hidden), BF16)

    count = len(up_pieces.arrays)
    activated, slope = call(
        partial(hidden_forward, up_pieces.entries, count),
        [shape_of((rows, 4 * hidden), BF16)] * 2,
        [meta, *up_pieces.arrays, first_low, hidden_bias],
        in_specs=[SMEM] + [ANY] * count + [by_rows(width), fixed(hidden_bias)],
        out_specs=[by_rows(4 * hidden)] * 2,
        scratch=[weight_scratch, pltpu.SemaphoreType.DMA((len(up_pieces.entries),))],
        grid=steps,
        flops=ffn,
        name="hidden_forward",
    )
    sums_shape = shape_of((8, width), F32)
    bias_shape = shape_of((8, 4 * hidden), F32)
    output, dr2, df, du, sums_two, hidden_sums = call(
        partial(finish_forward, down_pieces.entries, len(down_pieces.arrays)),
        [
            shape_of((rows, width), BF16),
            shape_of((rows, width), F32),
            shape_of((rows, width), BF16),
            shape_of((rows, 4 * hidden), BF16),
            sums_shape,
            bias_shape,
        ],
        [meta, *down_pieces.arrays, activated, slope, normed_one, output_grad, vectors],
        in_specs=[SMEM]
        + [ANY] * len(down_pieces.arrays)
        + [by_rows(4 * hidden)] * 2
        + [by_rows(width)] * 2
        + [fixed(vectors)],
        out_specs=[by_rows(width)] * 3 + [by_rows(4 * hidden), fixed(sums_shape), fixed(bias_shape)],
        scratch=[weight_scratch, pltpu.SemaphoreType.DMA((len(down_pieces.entries),))],
        grid=steps,
        flops=2 * ffn,
        name="finish_forward",
    )

    def weight_grad(left, right, order):
        outs = [shape_of((2, width, hidden), BF16)]
        whole_left = pl.BlockSpec((rows, width), lambda i: (0, 0))
        by_place = pl.BlockSpec((1, width, hidden), lambda i: (i, 0, 0))
        (for_partner,) = call(
            grad_for_partner,
            outs,
            [left, right],
            in_specs=[whole_left, pl.BlockSpec((rows, hidden), lambda i: (0, 2 * i + 1))],
            out_specs=[by_place],
            scratch=[pltpu.VMEM((width, rows), BF16)],
            grid=(2,),
            flops=ffn // 2,
            name="grad_for_partner",
        )
        received = g.swap(for_partner, "c")
        leaving = scatter_layout(g, shard, hidden, order)
        keep, send = call(
            partial(grad_for_chip, order),
            [leaving] * 2,
            [meta, left, right, received],
            in_specs=[SMEM, whole_left, pl.BlockSpec((rows, hidden), lambda i: (0, 2 * i)), by_place],
            out_specs=[fixed(leaving)] * 2,
            scratch=[pltpu.VMEM((width, rows), BF16)],
            grid=(2,),
            flops=ffn // 2,
            name="grad_for_chip",
        )
        return scatter_sum(g, keep, send, shard, order)

    down_order, up_order = ("x", "y") if regular else ("x", "x")
    down_share = weight_grad(df, activated, down_order)
    up_share = weight_grad(first_low, du, up_order)

    dr1, da, sums_one = call(
        partial(first_norm_back, up_pieces.entries, count),
        [shape_of((rows, width), F32), shape_of((rows, width), BF16), sums_shape],
        [meta, *up_pieces.arrays, du, dr2, normed_one, inverse_one, vectors],
        in_specs=[SMEM] + [ANY] * count + [by_rows(4 * hidden), by_rows(width), by_rows(width), by_rows(1), fixed(vectors)],
        out_specs=[by_rows(width)] * 2 + [fixed(sums_shape)],
        scratch=[weight_scratch, pltpu.SemaphoreType.DMA((len(up_pieces.entries),))],
        grid=steps,
        flops=ffn,
        name="first_norm_back",
    )
    other_da = g.swap(da, "c")

    head_shares, bias_sums = [], []
    ig_own = ig_other = None
    for j in range(heads):
        q, k, v, ctx_own, ctx_other, lse, w, wo = saved[j]
        last = j == heads - 1
        leaving = scatter_layout(g, shard, 4 * d, "x")
        ins = [meta, lows, highs, tokens, other_tokens, da, other_da, q, k, v, ctx_own, ctx_other, lse, w, wo, seg_col, seg_row]
        body = partial(first_pair, attention_backward) if ig_own is None else attention_backward
        if ig_own is not None:
            ins += [ig_own, ig_other]
        keep, send, ig_own, ig_other, sums = call(
            body,
            [
                leaving,
                leaving,
                shape_of((rows, width), F32),
                shape_of((rows, width), BF16 if last else F32),
                shape_of((8, 3 * PAIR), F32),
            ],
            ins,
            in_specs=[SMEM] * 3 + [VMEM] * (len(ins) - 3),
            scratch=[
                pltpu.VMEM((2, seq, PAIR), BF16),
                pltpu.VMEM((2, seq, PAIR), BF16),
                pltpu.VMEM((PAIR, seq), F32),
                pltpu.VMEM((PAIR, seq), BF16),
                pltpu.VMEM((seq, 3 * PAIR), BF16),
                pltpu.VMEM((blocks, 8, BLOCK), F32),
                pltpu.VMEM((width, seq), BF16),
                pltpu.VMEM((width, seq), BF16),
                pltpu.VMEM((seq, PAIR), BF16),
            ],
            flops=2 * seq * width * 9 * PAIR + 20 * seq * seq * PAIR,
            name="attention_backward",
        )
        head_shares.append(scatter_sum(g, keep, send, shard, "x"))
        bias_sums.append(sums[0].reshape(3, 2, d))
    input_grad = dr1 + ig_own + g.swap(ig_other, "c").astype(F32)

    me = x * 2 + c
    places = jnp.arange(4, dtype=jnp.int32) ^ me
    hidden_abs = hidden_sums[0].reshape(4, hidden)[places]
    pair_sums = jnp.stack(bias_sums)
    kinds = jnp.stack([pair_sums[:, 0], pair_sums[:, 2]])
    kinds = kinds.transpose(2, 0, 1, 3).reshape(2, 2 * heads * d)
    owned = jnp.zeros((4, 2 * heads * d), F32)
    owned = lax.dynamic_update_slice(owned, kinds[0:1], (me, 0))
    owned = lax.dynamic_update_slice(owned, kinds[1:2], (me ^ 2, 0))
    six = jnp.stack([sums_one[0], sums_one[1], sums_one[2], sums_two[0], sums_two[1], sums_two[2]])
    summed = lax.psum(jnp.concatenate([six.reshape(-1), hidden_abs.reshape(-1), owned.reshape(-1)]), ("z", "y", "x", "c"))
    vectors_grad = summed[: 6 * width].reshape(6, width)
    hidden_all = summed[6 * width : 6 * width + 4 * hidden].reshape(4, hidden)
    owned_all = summed[6 * width + 4 * hidden :].reshape(4, 2, heads * d)
    up_bias_share = lax.dynamic_index_in_dim(hidden_all, me, 0, keepdims=False)
    qv_share = lax.dynamic_index_in_dim(owned_all, me, 0, keepdims=False)

    qkv_share = jnp.stack(
        [jnp.concatenate([h[:, n * d : (n + 1) * d] for h in head_shares], axis=1) for n in range(3)], axis=1
    )
    out_share = jnp.concatenate([h[:, 3 * d :] for h in head_shares], axis=1)
    return (output, input_grad, qkv_share, qv_share, out_share, up_share, up_bias_share, down_share, vectors_grad)


def first_pair(body, *refs):
    body(*refs[:17], None, None, *refs[17:])


def solution(mesh):
    g = Grid(mesh)
    dp, tensor = ("z", "y"), ("x", "c")
    rows = P(dp + tensor, None)
    in_specs = (
        rows,
        P(dp, None),
        P(dp, None, tensor),
        P(None, tensor),
        P(dp, tensor),
        P(),
        P(),
        P(),
        P(dp, tensor),
        P(tensor),
        P(dp, tensor),
        P(),
        P(),
        P(),
        rows,
    )
    out_specs = (
        rows,
        rows,
        P(dp, None, tensor),
        P(None, tensor),
        P(dp, tensor),
        P(dp, tensor),
        P(tensor),
        P(dp, tensor),
        P(),
    )
    return jax.shard_map(partial(local, g), mesh=g.mesh, in_specs=in_specs, out_specs=out_specs, check_vma=False)
```

time: 1480 us -> 572 us (0.39)
  waiting for transfers between devices: 586 us -> 87.6 us
  matrix products: 424 us -> 0 us
  Pallas kernels: 0 us -> 292 us
  other arithmetic: 146 us -> 23 us
  blocking collectives: 136 us -> 42 us
  local copies, waits for them, and re-layouts: 122 us -> 35.9 us
  starting transfers between devices: 10.9 us -> 82 us
  loops' own time: 28 us -> 0 us
    reduce_scatter x8 -> x0, waiting for transfers between devices: 437 us -> none  [the longest x1 97.6 us: local(): lax.psum_scatter(times_transposed(context, out_full), 'tensor', scatter_d...]
    dot_general x68 -> x0, matrix products: 424 us -> none  [the longest x16 71.9 us: masked_scores(): jnp.einsum('qhd,khd->hqk', query_rows, key_seq, preferred_element_type=jn...]
    pallas_call x0 -> x14, Pallas kernels: none -> 292 us  [call(): pl.pallas_call(body, grid=grid, out_shape=outs, in_specs=in_specs or [who...]
    all_gather x6 -> x0, waiting for transfers between devices: 147 us -> none  [the longest x1 46.3 us: local(): fed_rows = lax.all_gather(fed_low, 'tensor', axis=0, tiled=True)]
    ppermute x0 -> x81, waiting for transfers between devices: none -> 87.6 us  [swap(): return lax.ppermute(array, axis, [(i, i ^ r) for i in range(size)])]
    ppermute x0 -> x81, starting transfers between devices: none -> 82 us  [swap(): return lax.ppermute(array, axis, [(i, i ^ r) for i in range(size)])]
    reduce_sum x17 -> x1, other arithmetic: 75.1 us -> 0.23 us  [local(): jnp.sum((segments[None, :] <= by_block[:, -1:]).astype(jnp.int32), axis=1)]
    all_gather x2 -> x0, blocking collectives: 72 us -> none  [the longest x1 38.8 us: local(): lax.all_gather(qkv_weight, 'dp', axis=0, tiled=True)]
  transfers between devices with their start and end apart: 14 -> 81, of which waited for: 11 -> 30; matrix products, arithmetic and copies ran while one was open for 6% -> 9% of each run, Pallas kernels for 0% -> 45%
where the time goes in v1:
time: 572 us; the launch traced here: 565 us
  Pallas kernels  292 us (51%)
  waiting for transfers between devices  87.6 us (15%)
  starting transfers between devices  82 us (14%)
  blocking collectives  42 us (7%)
  local copies, waits for them, and re-layouts  35.9 us (6%)
  other arithmetic  23 us (4%)
    pallas_call x14, Pallas kernels, call(): pl.pallas_call(body, grid=grid, out_shape=outs, in_specs=in_specs or [who...  292 us
    ppermute x81, waiting for transfers between devices, swap(): return lax.ppermute(array, axis, [(i, i ^ r) for i in range(size)])  87.6 us
    ppermute x81, starting transfers between devices, swap(): return lax.ppermute(array, axis, [(i, i ^ r) for i in range(size)])  82 us
    psum x1, blocking collectives, local(): lax.psum(jnp.concatenate([six.reshape(-1), hidden_abs.reshape(-1), owned....  42 us
  transfers between devices with their start and end apart: 81, of which 30 were waited for; matrix products, arithmetic and copies ran while one was open for 9% of the time, Pallas kernels for 45%

profile of v1, /device:TPU:0, one launch (start us, length us, event | category | flops | bytes accessed | tf_op | source)
XLA Modules:
  0.0 564.9 jit_solution(13433963100164864340)
XLA Ops:
  23.9 3.9 collective-permute-start.23
  47.3 8.6 %collective-permute-done.1 = bf16[96,768]{1,0:T(8,128)(2,1)S(1)} collective-permute-done((bf16[96,768]{1,0:T(8,128)(2,1)S(1)}, bf16[96,768]{1,0:T(8,128)(2,1)S(1)}, u32[]{:S(2)}, u32[]{:S(2)}) %collective-permute-start.1) | collective-permute-done | bytes 147488 | tf_op jit(solution)/shard_map/ppermute | solution.py:66
  66.2 3.6 collective-permute-done.43.refs_1_
  77.1 6.8 %collective-permute-done.36.refs_1_ = bf16[2,4,48,256]{3,2,1,0:T(8,128)(2,1)S(1)} collective-permute-done((bf16[2,4,48,256]{3,2,1,0:T(8,128)(2,1)S(1)}, bf16[2,4,48,256]{3,2,1,0:T(8,128)(2,1)S(1)}, u32[]{:S(2)}, u32[]{:S(2)}) %collective-permute-start.36) | collective-permute-done | bytes 196640 | tf_op jit(solution)/shard_map/ppermute | solution.py:66
  95.0 29.3 %attention_forward.5 = (bf16[2048,128]{1,0:T(8,128)(2,1)}, bf16[2048,128]{1,0:T(8,128)(2,1)}, bf16[2048,128]{1,0:T(8,128)(2,1)}, bf16[1024,128]{1,0:T(8,128)(2,1...) custom-call(s32[2]{0:T(128)} %pad_add_fusion.meta.refs_0_, ...), custom_call_target="tpu_custom_call" | custom-call | flops 5502926848 | bytes 6898760 | tf_op jit(solution)/shard_map/attention_forward/pallas_call | solution.py:32
  125.7 29.1 %attention_forward.4 = (bf16[2048,128]{1,0:T(8,128)(2,1)}, bf16[2048,128]{1,0:T(8,128)(2,1)}, bf16[2048,128]{1,0:T(8,128)(2,1)}, bf16[1024,128]{1,0:T(8,128)(2,1...) custom-call(s32[2]{0:T(128)} %pad_add_fusion.meta.refs_0_, ...), custom_call_target="tpu_custom_call" | custom-call | flops 5502926848 | bytes 6898760 | tf_op jit(solution)/shard_map/attention_forward/pallas_call | solution.py:32
  156.0 29.1 %attention_forward.3 = (bf16[2048,128]{1,0:T(8,128)(2,1)}, bf16[2048,128]{1,0:T(8,128)(2,1)}, bf16[2048,128]{1,0:T(8,128)(2,1)}, bf16[1024,128]{1,0:T(8,128)(2,1...) custom-call(s32[2]{0:T(128)} %pad_add_fusion.meta.refs_0_, ...), custom_call_target="tpu_custom_call" | custom-call | flops 5502926848 | bytes 6898760 | tf_op jit(solution)/shard_map/attention_forward/pallas_call | solution.py:32
  189.9 6.9 %project_and_norm.1 = (f32[1024,768]{1,0:T(8,128)}, f32[1024,1]{1,0:T(8,128)}, bf16[1024,768]{1,0:T(8,128)(2,1)}) custom-call(bf16[1024,768]{1,0:T(8,128)(2,1)} %own.3, f32[8,768]{1,0:T(8,128)} %convert_element_type.245.vectors.refs_12_, bf16[1024,128]{1,0:T(8,128)(2,1)} %get-tuple-element.66.refs_0_.refs_10_, ...), custom_call_target="tpu_custom_call" | custom-call | flops 1207959552 | bytes 9072640 | tf_op jit(solution)/shard_map/project_and_norm/pallas_call | solution.py:32
  196.7 14.5 %hidden_forward.1 = (bf16[1024,3072]{1,0:T(8,128)(2,1)}, bf16[1024,3072]{1,0:T(8,128)(2,1)}) custom-call(s32[2]{0:T(128)} %pad_add_fusion.meta.refs_0_, bf16[2,4,48,768]{3,2,1,0:T(8,128)(2,1)} %copy-done.5, bf16[2,4,48,768]{3,2,1,0:T(8,128)(2,1)} %copy-done.31, bf16[2,4,48,768]{3,2,1,0:T(8,128)(2,1)} %copy-done.6, ...), custom_call_target="tpu_custom_call" | custom-call | flops 4831838208 | bytes 18886664 | tf_op jit(solution)/shard_map/hidden_forward/pallas_call | solution.py:32
  212.2 25.8 %finish_forward.1 = (bf16[1024,768]{1,0:T(8,128)(2,1)}, f32[1024,768]{1,0:T(8,128)}, bf16[1024,768]{1,0:T(8,128)(2,1)}, bf16[1024,3072]{1,0:T(8,128)(2,1)}, f32[8,768]{1,0:T(8,128)}, /*index=5*/f32[8,3072]{1,0:T(8,128)}) custom-call(s32[2]{0:T(128)} %pad_add_fusion.meta.refs_0_, bf16[2,4,48,768]{3,2,1,0:T(8,128)(2,1)} %copy-done.8, ...), custom_call_target="tpu_custom_call" | custom-call | flops 9663676416 | bytes 34750472 | tf_op jit(solution)/shard_map/finish_forward/pallas_call | solution.py:32
  238.0 14.4 %first_norm_back.1 = (f32[1024,768]{1,0:T(8,128)}, bf16[1024,768]{1,0:T(8,128)(2,1)}, f32[8,768]{1,0:T(8,128)}) custom-call(s32[2]{0:T(128)} %pad_add_fusion.meta.refs_0_, bf16[2,4,48,768]{3,2,1,0:T(8,128)(2,1)} %copy-done.5, bf16[2,4,48,768]{3,2,1,0:T(8,128)(2,1)} %copy-done.31, bf16[2,4,48,768]{3,2,1,0:T(8,128)(2,1)} %copy-done.6, ...), custom_call_target="tpu_custom_call" | custom-call | flops 4831838208 | bytes 22073352 | tf_op jit(solution)/shard_map/first_norm_back/pallas_call | solution.py:32
  252.6 6.2 %grad_for_partner.3 = bf16[2,768,768]{2,1,0:T(8,128)(2,1)} custom-call(bf16[1024,768]{1,0:T(8,128)(2,1)} %get-tuple-element.120.left, bf16[1024,3072]{1,0:T(8,128)(2,1)} %get-tuple-element.76.refs_8_.right), custom_call_target="tpu_custom_call" | custom-call | flops 2415919104 | bytes 10223616 | tf_op jit(solution)/shard_map/grad_for_partner/pallas_call | solution.py:32
  259.2 6.2 %grad_for_partner.2 = bf16[2,768,768]{2,1,0:T(8,128)(2,1)} custom-call(bf16[1024,768]{1,0:T(8,128)(2,1)} %get-tuple-element.75.refs_8_.left, bf16[1024,3072]{1,0:T(8,128)(2,1)} %get-tuple-element.80.refs_8_.right), custom_call_target="tpu_custom_call" | custom-call | flops 2415919104 | bytes 10223616 | tf_op jit(solution)/shard_map/grad_for_partner/pallas_call | solution.py:32
  267.7 36.8 %attention_backward.3 = (bf16[2,4,96,256]{3,2,1,0:T(8,128)(2,1)}, bf16[2,4,96,256]{3,2,1,0:T(8,128)(2,1)}, f32[1024,768]{1,0:T(8,128)}, f32[1024,768]{1,0:T(8,128)}, f32[8,384]{1,0:T(8,128)}) custom-call(s32[2]{0:T(128)} %pad_add_fusion.meta.refs_0_, s32[8]{0:T(128)} %get-tuple-element.249.lows.refs_1_, s32[8]{0:T(128)} %get-tuple-element.248.highs.refs_2_, ...), custom_call_target="tpu_custom_call" | custom-call | flops 14361296896 | bytes 16347208 | tf_op jit(solution)/shard_map/attention_backward/pallas_call | solution.py:32
  304.6 39.3 %attention_backward.4 = (bf16[2,4,96,256]{3,2,1,0:T(8,128)(2,1)}, bf16[2,4,96,256]{3,2,1,0:T(8,128)(2,1)}, f32[1024,768]{1,0:T(8,128)}, f32[1024,768]{1,0:T(8,128)}, f32[8,384]{1,0:T(8,128)}) custom-call(s32[2]{0:T(128)} %pad_add_fusion.meta.refs_0_, s32[8]{0:T(128)} %get-tuple-element.249.lows.refs_1_, s32[8]{0:T(128)} %get-tuple-element.248.highs.refs_2_, ...), custom_call_target="tpu_custom_call" | custom-call | flops 14361296896 | bytes 22638664 | tf_op jit(solution)/shard_map/attention_backward/pallas_call | solution.py:32
  346.8 38.4 %attention_backward.5 = (bf16[2,4,96,256]{3,2,1,0:T(8,128)(2,1)}, bf16[2,4,96,256]{3,2,1,0:T(8,128)(2,1)}, f32[1024,768]{1,0:T(8,128)}, bf16[1024,768]{1,0:T(8,128)(2,1)}, f32[8,384]{1,0:T(8,128)}) custom-call(s32[2]{0:T(128)} %pad_add_fusion.meta.refs_0_, s32[8]{0:T(128)} %get-tuple-element.249.lows.refs_1_, s32[8]{0:T(128)} %get-tuple-element.248.highs.refs_2_, ...), custom_call_target="tpu_custom_call" | custom-call | flops 14361296896 | bytes 21065800 | tf_op jit(solution)/shard_map/attention_backward/pallas_call | solution.py:32
  398.9 42.0 %psum.7 = f32[9216]{0:T(1024)} all-reduce(f32[9216]{0:T(1024)} %pad_maximum_fusion.25), channel_id=1, replica_groups=mesh['z'=4,'y'=2,'x'=2,'c'=2] {'z','y','x','c'}, use_global_device_ids=true, to_apply=%region_2.3 | all-reduce | flops 9216 | bytes 73728 | tf_op jit(solution)/shard_map/psum | solution.py:714
  479.9 3.9 collective-permute-done.68
  485.2 6.6 %grad_for_chip.3 = (bf16[2,4,96,768]{3,2,1,0:T(8,128)(2,1)}, bf16[2,4,96,768]{3,2,1,0:T(8,128)(2,1)}) custom-call(s32[2]{0:T(128)} %pad_add_fusion.meta.refs_0_, bf16[1024,768]{1,0:T(8,128)(2,1)} %get-tuple-element.120.left, bf16[1024,3072]{1,0:T(8,128)(2,1)} %get-tuple-element.76.refs_8_.right, bf16[2,768,768]{2,1,0:T(8,128)(2,1)} %copy-done.2), custom_call_target="tpu_custom_call" | custom-call | flops 2415919104 | bytes 12582920 | tf_op jit(solution)/shard_map/grad_for_chip/pallas_call | solution.py:32
  492.6 9.8 %grad_for_chip.2 = (bf16[2,4,96,768]{3,2,1,0:T(8,128)(2,1)}, bf16[2,4,96,768]{3,2,1,0:T(8,128)(2,1)}) custom-call(s32[2]{0:T(128)} %pad_add_fusion.meta.refs_0_, bf16[1024,768]{1,0:T(8,128)(2,1)} %get-tuple-element.75.refs_8_.left, bf16[1024,3072]{1,0:T(8,128)(2,1)} %get-tuple-element.80.refs_8_.right, bf16[2,768,768]{2,1,0:T(8,128)(2,1)} %collective-permute-done.69.received), custom_call_target="tpu_custom_call" | custom-call | flops 2415919104 | bytes 12582920 | tf_op jit(solution)/shard_map/grad_for_chip/pallas_call | solution.py:32
  504.9 11.7 %collective-permute-done.76 = bf16[2,4,96,768]{3,2,1,0:T(8,128)(2,1)} collective-permute-done((bf16[2,4,96,768]{3,2,1,0:T(8,128)(2,1)}, bf16[2,4,96,768]{3,2,1,0:T(8,128)(2,1)}, u32[]{:S(2)}, u32[]{:S(2)}) %collective-permute-start.76) | collective-permute-done | bytes 1179680 | tf_op jit(solution)/shard_map/ppermute | solution.py:66
  520.0 11.5 %collective-permute-done.70 = bf16[2,4,96,768]{3,2,1,0:T(8,128)(2,1)S(1)} collective-permute-done((bf16[2,4,96,768]{3,2,1,0:T(8,128)(2,1)}, bf16[2,4,96,768]{3,2,1,0:T(8,128)(2,1)S(1)}, u32[]{:S(2)}, u32[]{:S(2)}) %collective-permute-start.70) | collective-permute-done | bytes 1179680 | tf_op jit(solution)/shard_map/ppermute | solution.py:66
  532.9 3.6 convert_add_fusion
  555.5 8.4 %collective-permute-done.73 = bf16[96,768]{1,0:T(8,128)(2,1)S(1)} collective-permute-done((bf16[96,768]{1,0:T(8,128)(2,1)S(1)}, bf16[96,768]{1,0:T(8,128)(2,1)S(1)}, u32[]{:S(2)}, u32[]{:S(2)}) %collective-permute-start.73) | collective-permute-done | bytes 147488 | tf_op jit(solution)/shard_map/ppermute | solution.py:66
  (387 shorter events, 166.7 us)
Async XLA Ops:
  34.5 21.4 %collective-permute-start.1 = (bf16[96,768]{1,0:T(8,128)(2,1)S(1)}, bf16[96,768]{1,0:T(8,128)(2,1)S(1)}, u32[]{:S(2)}, u32[]{:S(2)}) collective-permute-start(bf16[96,768]{1,0:T(8,128)(2,1)S(1)} %copy-done.19), channel_id=1, source_target_pairs={{0,16},{8,24},{16,0},{24,8},{1,17},{9,25},{17,1},{25,9},{2,18},{10... | collective-permute-start | bytes 442376 | tf_op jit(solution)/shard_map/ppermute | solution.py:66
  44.1 48.2 %collective-permute-start.29 = (bf16[1024,768]{1,0:T(8,128)(2,1)S(1)}, bf16[1024,768]{1,0:T(8,128)(2,1)S(1)}, u32[]{:S(2)}, u32[]{:S(2)}) collective-permute-start(bf16[1024,768]{1,0:T(8,128)(2,1)S(1)} %copy-done.29), channel_id=1, source_target_pairs={{0,1},{1,0},{2,3},{3,2},{4,5},{5,4},{6,7},{7,6},{8,9},{9,8},{10,11... | collective-permute-start | bytes 4718600 | tf_op jit(solution)/shard_map/ppermute | solution.py:66
  86.1 38.3 %collective-permute-start.15 = (bf16[2,4,48,768]{3,2,1,0:T(8,128)(2,1)S(1)}, bf16[2,4,48,768]{3,2,1,0:T(8,128)(2,1)S(1)}, u32[]{:S(2)}, u32[]{:S(2)}) collective-permute-start(bf16[2,4,48,768]{3,2,1,0:T(8,128)(2,1)S(1)} %pad_maximum_fusion.2.refs_0_), channel_id=1, source_target_pairs={{0,4},{4,0},{1,5},{5,1},{2,6},{6,2},{3,7},{7,3},{8,12},{12,8},{9,1... | collective-permute-start | bytes 1769480 | tf_op jit(solution)/shard_map/ppermute | solution.py:66
  87.3 38.3 %collective-permute-start.17 = (bf16[2,4,48,768]{3,2,1,0:T(8,128)(2,1)S(1)}, bf16[2,4,48,768]{3,2,1,0:T(8,128)(2,1)}, u32[]{:S(2)}, u32[]{:S(2)}) collective-permute-start(bf16[2,4,48,768]{3,2,1,0:T(8,128)(2,1)S(1)} %pad_maximum_fusion.3.refs_2_), channel_id=1, source_target_pairs={{0,2},{2,0},{1,3},{3,1},{4,6},{6,4},{5,7},{7,5},{8,10},{10,8},{9,1... | collective-permute-start | bytes 1769480 | tf_op jit(solution)/shard_map/ppermute | solution.py:66
  91.8 63.0 %collective-permute-start.18 = (bf16[2,4,48,768]{3,2,1,0:T(8,128)(2,1)S(1)}, bf16[2,4,48,768]{3,2,1,0:T(8,128)(2,1)}, u32[]{:S(2)}, u32[]{:S(2)}) collective-permute-start(bf16[2,4,48,768]{3,2,1,0:T(8,128)(2,1)S(1)} %pad_maximum_fusion.2.refs_0_), channel_id=1, source_target_pairs={{0,1},{1,0},{2,3},{3,2},{4,5},{5,4},{6,7},{7,6},{8,9},{9,8},{10,11... | collective-permute-start | bytes 1769480 | tf_op jit(solution)/shard_map/ppermute | solution.py:66
  92.3 63.0 %collective-permute-start.20 = (bf16[2,4,48,768]{3,2,1,0:T(8,128)(2,1)S(1)}, bf16[2,4,48,768]{3,2,1,0:T(8,128)(2,1)}, u32[]{:S(2)}, u32[]{:S(2)}) collective-permute-start(bf16[2,4,48,768]{3,2,1,0:T(8,128)(2,1)S(1)} %pad_maximum_fusion.3.refs_2_), channel_id=1, source_target_pairs={{0,1},{1,0},{2,3},{3,2},{4,5},{5,4},{6,7},{7,6},{8,9},{9,8},{10,11... | collective-permute-start | bytes 1769480 | tf_op jit(solution)/shard_map/ppermute | solution.py:66
  93.5 61.9 %collective-permute-start.6 = (bf16[2,4,48,768]{3,2,1,0:T(8,128)(2,1)S(1)}, bf16[2,4,48,768]{3,2,1,0:T(8,128)(2,1)}, u32[]{:S(2)}, u32[]{:S(2)}) collective-permute-start(bf16[2,4,48,768]{3,2,1,0:T(8,128)(2,1)S(1)} %pad_maximum_fusion.1.refs_2_), channel_id=1, source_target_pairs={{0,2},{2,0},{1,3},{3,1},{4,6},{6,4},{5,7},{7,5},{8,10},{10,8},{9,1... | collective-permute-start | bytes 1769480 | tf_op jit(solution)/shard_map/ppermute | solution.py:66
  124.4 60.8 %collective-permute-start.4 = (bf16[2,4,48,768]{3,2,1,0:T(8,128)(2,1)S(1)}, bf16[2,4,48,768]{3,2,1,0:T(8,128)(2,1)}, u32[]{:S(2)}, u32[]{:S(2)}) collective-permute-start(bf16[2,4,48,768]{3,2,1,0:T(8,128)(2,1)S(1)} %pad_maximum_fusion.refs_0_), channel_id=1, source_target_pairs={{0,4},{4,0},{1,5},{5,1},{2,6},{6,2},{3,7},{7,3},{8,12},{12,8},{9,1... | collective-permute-start | bytes 1769480 | tf_op jit(solution)/shard_map/ppermute | solution.py:66
  125.6 59.7 %collective-permute-start.19 = (bf16[2,4,48,768]{3,2,1,0:T(8,128)(2,1)S(1)}, bf16[2,4,48,768]{3,2,1,0:T(8,128)(2,1)}, u32[]{:S(2)}, u32[]{:S(2)}) collective-permute-start(bf16[2,4,48,768]{3,2,1,0:T(8,128)(2,1)S(1)} %collective-permute-done.15.refs_1_), channel_id=1, source_target_pairs={{0,1},{1,0},{2,3},{3,2},{4,5},{5,4},{6,7},{7,6},{8,9},{9,8},{10,11... | collective-permute-start | bytes 1769480 | tf_op jit(solution)/shard_map/ppermute | solution.py:66
  154.8 41.9 %collective-permute-start.21 = (bf16[2,4,48,768]{3,2,1,0:T(8,128)(2,1)}, bf16[2,4,48,768]{3,2,1,0:T(8,128)(2,1)}, u32[]{:S(2)}, u32[]{:S(2)}) collective-permute-start(bf16[2,4,48,768]{3,2,1,0:T(8,128)(2,1)} %collective-permute-done.17.refs_3_), channel_id=1, source_target_pairs={{0,1},{1,0},{2,3},{3,2},{4,5},{5,4},{6,7},{7,6},{8,9},{9,8},{10,11... | collective-permute-start | bytes 1769480 | tf_op jit(solution)/shard_map/ppermute | solution.py:66
  155.3 30.4 %collective-permute-start.51 = (bf16[768,128]{1,0:T(8,128)(2,1)S(1)}, bf16[768,128]{1,0:T(8,128)(2,1)S(1)}, u32[]{:S(2)}, u32[]{:S(2)}) collective-permute-start(bf16[768,128]{1,0:T(8,128)(2,1)S(1)} %copy-done.38), channel_id=1, source_target_pairs={{0,1},{1,0},{2,3},{3,2},{4,5},{5,4},{6,7},{7,6},{8,9},{9,8},{10,11... | collective-permute-start | bytes 589832 | tf_op jit(solution)/shard_map/ppermute | solution.py:66
  155.5 30.3 %collective-permute-start.50 = (bf16[768,128]{1,0:T(8,128)(2,1)}, bf16[768,128]{1,0:T(8,128)(2,1)S(1)}, u32[]{:S(2)}, u32[]{:S(2)}) collective-permute-start(bf16[768,128]{1,0:T(8,128)(2,1)} %get-tuple-element.73.refs_7_.wo), channel_id=1, source_target_pairs={{0,1},{1,0},{2,3},{3,2},{4,5},{5,4},{6,7},{7,6},{8,9},{9,8},{10,11... | collective-permute-start | bytes 589832 | tf_op jit(solution)/shard_map/ppermute | solution.py:66
  188.1 23.1 %collective-permute-start.9 = (bf16[2,4,48,768]{3,2,1,0:T(8,128)(2,1)S(1)}, bf16[2,4,48,768]{3,2,1,0:T(8,128)(2,1)S(1)}, u32[]{:S(2)}, u32[]{:S(2)}) collective-permute-start(bf16[2,4,48,768]{3,2,1,0:T(8,128)(2,1)S(1)} %pad_maximum_fusion.1.refs_2_), channel_id=1, source_target_pairs={{0,1},{1,0},{2,3},{3,2},{4,5},{5,4},{6,7},{7,6},{8,9},{9,8},{10,11... | collective-permute-start | bytes 1769480 | tf_op jit(solution)/shard_map/ppermute | solution.py:66
  188.3 23.0 %collective-permute-start.7 = (bf16[2,4,48,768]{3,2,1,0:T(8,128)(2,1)S(1)}, bf16[2,4,48,768]{3,2,1,0:T(8,128)(2,1)S(1)}, u32[]{:S(2)}, u32[]{:S(2)}) collective-permute-start(bf16[2,4,48,768]{3,2,1,0:T(8,128)(2,1)S(1)} %pad_maximum_fusion.refs_0_), channel_id=1, source_target_pairs={{0,1},{1,0},{2,3},{3,2},{4,5},{5,4},{6,7},{7,6},{8,9},{9,8},{10,11... | collective-permute-start | bytes 1769480 | tf_op jit(solution)/shard_map/ppermute | solution.py:66
  188.7 22.6 %collective-permute-start.10 = (bf16[2,4,48,768]{3,2,1,0:T(8,128)(2,1)}, bf16[2,4,48,768]{3,2,1,0:T(8,128)(2,1)}, u32[]{:S(2)}, u32[]{:S(2)}) collective-permute-start(bf16[2,4,48,768]{3,2,1,0:T(8,128)(2,1)} %collective-permute-done.6.refs_3_), channel_id=1, source_target_pairs={{0,1},{1,0},{2,3},{3,2},{4,5},{5,4},{6,7},{7,6},{8,9},{9,8},{10,11... | collective-permute-start | bytes 1769480 | tf_op jit(solution)/shard_map/ppermute | solution.py:66
  188.8 22.4 %collective-permute-start.8 = (bf16[2,4,48,768]{3,2,1,0:T(8,128)(2,1)}, bf16[2,4,48,768]{3,2,1,0:T(8,128)(2,1)}, u32[]{:S(2)}, u32[]{:S(2)}) collective-permute-start(bf16[2,4,48,768]{3,2,1,0:T(8,128)(2,1)} %collective-permute-done.4.refs_1_), channel_id=1, source_target_pairs={{0,1},{1,0},{2,3},{3,2},{4,5},{5,4},{6,7},{7,6},{8,9},{9,8},{10,11... | collective-permute-start | bytes 1769480 | tf_op jit(solution)/shard_map/ppermute | solution.py:66
  258.8 224.9 %collective-permute-start.75 = (bf16[2,768,768]{2,1,0:T(8,128)(2,1)}, bf16[2,768,768]{2,1,0:T(8,128)(2,1)S(1)}, u32[]{:S(2)}, u32[]{:S(2)}) collective-permute-start(bf16[2,768,768]{2,1,0:T(8,128)(2,1)} %grad_for_partner.3), channel_id=1, source_target_pairs={{0,1},{1,0},{2,3},{3,2},{4,5},{5,4},{6,7},{7,6},{8,9},{9,8},{10,11... | collective-permute-start | bytes 7077896 | tf_op jit(solution)/shard_map/ppermute | solution.py:66
  265.4 227.1 %collective-permute-start.69 = (bf16[2,768,768]{2,1,0:T(8,128)(2,1)}, bf16[2,768,768]{2,1,0:T(8,128)(2,1)}, u32[]{:S(2)}, u32[]{:S(2)}) collective-permute-start(bf16[2,768,768]{2,1,0:T(8,128)(2,1)} %grad_for_partner.2), channel_id=1, source_target_pairs={{0,1},{1,0},{2,3},{3,2},{4,5},{5,4},{6,7},{7,6},{8,9},{9,8},{10,11... | collective-permute-start | bytes 7077896 | tf_op jit(solution)/shard_map/ppermute | solution.py:66
  304.6 146.6 %collective-permute-start.54 = (bf16[2,4,96,256]{3,2,1,0:T(8,128)(2,1)}, bf16[2,4,96,256]{3,2,1,0:T(8,128)(2,1)}, u32[]{:S(2)}, u32[]{:S(2)}) collective-permute-start(bf16[2,4,96,256]{3,2,1,0:T(8,128)(2,1)} %get-tuple-element.107), channel_id=1, source_target_pairs={{0,2},{2,0},{1,3},{3,1},{4,6},{6,4},{5,7},{7,5},{8,10},{10,8},{9,1... | collective-permute-start | bytes 1179656 | tf_op jit(solution)/shard_map/ppermute | solution.py:66
  343.8 108.5 %collective-permute-start.59 = (bf16[2,4,96,256]{3,2,1,0:T(8,128)(2,1)}, bf16[2,4,96,256]{3,2,1,0:T(8,128)(2,1)}, u32[]{:S(2)}, u32[]{:S(2)}) collective-permute-start(bf16[2,4,96,256]{3,2,1,0:T(8,128)(2,1)} %get-tuple-element.109), channel_id=1, source_target_pairs={{0,2},{2,0},{1,3},{3,1},{4,6},{6,4},{5,7},{7,5},{8,10},{10,8},{9,1... | collective-permute-start | bytes 1179656 | tf_op jit(solution)/shard_map/ppermute | solution.py:66
  479.8 53.1 %collective-permute-start.53 = (bf16[1024,768]{1,0:T(8,128)(2,1)}, bf16[1024,768]{1,0:T(8,128)(2,1)}, u32[]{:S(2)}, u32[]{:S(2)}) collective-permute-start(bf16[1024,768]{1,0:T(8,128)(2,1)} %get-tuple-element.105), channel_id=1, source_target_pairs={{0,1},{1,0},{2,3},{3,2},{4,5},{5,4},{6,7},{7,6},{8,9},{9,8},{10,11... | collective-permute-start | bytes 4718600 | tf_op jit(solution)/shard_map/ppermute | solution.py:66
  491.7 24.8 %collective-permute-start.76 = (bf16[2,4,96,768]{3,2,1,0:T(8,128)(2,1)}, bf16[2,4,96,768]{3,2,1,0:T(8,128)(2,1)}, u32[]{:S(2)}, u32[]{:S(2)}) collective-permute-start(bf16[2,4,96,768]{3,2,1,0:T(8,128)(2,1)} %get-tuple-element.122), channel_id=1, source_target_pairs={{0,2},{2,0},{1,3},{3,1},{4,6},{6,4},{5,7},{7,5},{8,10},{10,8},{9,1... | collective-permute-start | bytes 3538952 | tf_op jit(solution)/shard_map/ppermute | solution.py:66
  502.4 29.1 %collective-permute-start.70 = (bf16[2,4,96,768]{3,2,1,0:T(8,128)(2,1)}, bf16[2,4,96,768]{3,2,1,0:T(8,128)(2,1)S(1)}, u32[]{:S(2)}, u32[]{:S(2)}) collective-permute-start(bf16[2,4,96,768]{3,2,1,0:T(8,128)(2,1)} %get-tuple-element.119), channel_id=1, source_target_pairs={{0,4},{4,0},{1,5},{5,1},{2,6},{6,2},{3,7},{7,3},{8,12},{12,8},{9,1... | collective-permute-start | bytes 3538952 | tf_op jit(solution)/shard_map/ppermute | solution.py:66
  517.9 21.3 %collective-permute-start.77 = (bf16[4,96,768]{2,1,0:T(8,128)(2,1)S(1)}, bf16[4,96,768]{2,1,0:T(8,128)(2,1)S(1)}, u32[]{:S(2)}, u32[]{:S(2)}) collective-permute-start(bf16[4,96,768]{2,1,0:T(8,128)(2,1)S(1)} %fusion.1), channel_id=1, source_target_pairs={{0,4},{4,0},{1,5},{5,1},{2,6},{6,2},{3,7},{7,3},{8,12},{12,8},{9,1... | collective-permute-start | bytes 1769480 | tf_op jit(solution)/shard_map/ppermute | solution.py:66
  (104 other events, 1719.6 us)

commit v2 on v0

v2 whole, which is shorter than its diff:
```python
from functools import partial

import jax
import jax.numpy as jnp
from jax import lax
from jax.experimental import pallas as pl
from jax.experimental.pallas import tpu as pltpu
from jax.sharding import Mesh
from jax.sharding import PartitionSpec as P

HEAD_DIM = 64
PAIR = 2 * HEAD_DIM
EPSILON = 1e-12
MASKED = -1e30
BLOCK = 256
F32 = jnp.float32
BF16 = jnp.bfloat16
MIB = 1 << 20


def dot_nn(left, right):
    return jnp.dot(left, right, preferred_element_type=F32)


def dot_nt(left, right):
    return lax.dot_general(left, right, (((1,), (1,)), ((), ())), preferred_element_type=F32)


def call(body, outs, ins, in_specs=None, out_specs=None, scratch=(), grid=(), flops=0, name=None, vmem=60, alias=None):
    moved = sum(a.size * a.dtype.itemsize for a in ins) + sum(o.size * o.dtype.itemsize for o in outs)
    return pl.pallas_call(
        body,
        grid=grid,
        out_shape=outs,
        in_specs=in_specs or [VMEM] * len(ins),
        out_specs=out_specs or [VMEM] * len(outs),
        scratch_shapes=list(scratch),
        compiler_params=pltpu.CompilerParams(vmem_limit_bytes=vmem * MIB),
        cost_estimate=pl.CostEstimate(flops=int(flops), bytes_accessed=int(moved), transcendentals=0),
        input_output_aliases=alias or {},
        name=name,
    )(*ins)


ANY = pl.BlockSpec(memory_space=pl.ANY)
SMEM = pl.BlockSpec(memory_space=pltpu.SMEM)
VMEM = pl.BlockSpec(memory_space=pltpu.VMEM)


def shape_of(shape, dtype):
    return jax.ShapeDtypeStruct(shape, dtype)


def after(values, done):
    return lax.optimization_barrier((values, done))[0]


class Grid:
    def __init__(self, mesh):
        n_dp, n_tensor = mesh.devices.shape
        assert n_tensor == 4 and n_dp % 2 == 0
        self.nz = n_dp // 2
        self.n_dp = n_dp
        self.mesh = Mesh(mesh.devices.reshape(self.nz, 2, 2, 2), ("z", "y", "x", "c"))

    def swap(self, array, axis, r=1):
        size = self.nz if axis == "z" else 2
        return lax.ppermute(array, axis, [(i, i ^ r) for i in range(size)])

    def regular(self, rows):
        return rows % 32 == 0 and self.nz & (self.nz - 1) == 0

    def total_dp(self, array):
        if self.nz & (self.nz - 1):
            return lax.psum(array, ("z", "y"))
        array = array + self.swap(array, "y")
        r = 1
        while r < self.nz:
            array = array + self.swap(array, "z", r)
            r *= 2
        return array


class Gather:
    def __init__(self, g, shard):
        self.g, self.shard, self.rows = g, shard, shard.shape[0]
        self.regular = g.regular(self.rows)

    def line(self):
        g, half = self.g, self.rows // 2
        if not self.regular:
            full = lax.all_gather(self.shard, ("z", "y"), axis=0, tiled=True)[None, None]
            self.arrays = [full, g.swap(full, "x")]
            self.entries = [(n, 0, 0, n, 0, 0, full.shape[2]) for n in range(2)]
            return self.arrays
        near = [self.shard] + [g.swap(self.shard, "z", r) for r in range(1, g.nz)]
        self.lines = [jnp.stack([part[:half] for part in near]), jnp.stack([part[half:] for part in near])]
        return self.lines

    def wait(self, step, done):
        if self.regular:
            setattr(self, step, after(getattr(self, step), done))

    def first(self, done=()):
        if not self.regular:
            return self.arrays
        arrived = after([self.g.swap(line, axis) for line, axis in zip(self.lines, "xy")], done)
        self.twos = [jnp.stack([line, other]) for line, other in zip(self.lines, arrived)]
        return arrived

    def second(self):
        if not self.regular:
            return self.arrays
        half = self.rows // 2
        self.arrays, self.entries = [], []
        for number, axis in enumerate("xy"):
            two = self.twos[number]
            four = self.g.swap(two, "yx"[number])
            for index, array in ((0, two), (1, four)):
                for i in range(2):
                    rx, ry = (i, index) if axis == "x" else (index, i)
                    for k in range(self.g.nz):
                        self.entries.append((len(self.arrays), i, k, rx, k * 2 + ry, number * half, half))
                self.arrays.append(array)
        return self.arrays


def load_pieces(entries, refs, index, target, sems, lanes):
    slots = 1 + max(entry[4] for entry in entries)
    copies = []
    for number, (a, i, k, place, slot, first, size) in enumerate(entries):
        row = pl.multiple_of((slot ^ index) * (target.shape[1] // slots) + first, 16)
        copies.append(
            pltpu.make_async_copy(refs[a].at[i, k, :, lanes], target.at[place, pl.ds(row, size)], sems.at[number])
        )
    for copy in copies:
        copy.start()
    for copy in copies:
        copy.wait()


def gather_everywhere(g, shard):
    if g.regular(shard.shape[0]):
        full = lax.all_gather(shard, ("z", "y", "x", "c"), axis=0)
        return full.reshape(g.n_dp, 4, *shard.shape)
    full = lax.all_gather(shard, ("z", "y"), axis=0, tiled=True)
    return lax.all_gather(full, ("x", "c"), axis=0)[None]


def everywhere_copies(source, me, target, sems, lanes):
    blocks, places, rows = source.shape[:3]
    return [
        pltpu.make_async_copy(
            source.at[block, t, :, lanes],
            target.at[t ^ me, pl.ds(block * rows, rows)],
            sems.at[block * places + t],
        )
        for block in range(blocks)
        for t in range(places)
    ]


class Scatter:
    def __init__(self, g, rows, arrays):
        self.g, self.rows = g, rows
        self.regular = g.regular(rows)
        self.arrays = arrays

    @staticmethod
    def shapes(g, rows, lanes):
        if not g.regular(rows):
            return [shape_of((2, rows * g.n_dp, lanes), BF16)]
        return [shape_of((2, g.nz, rows // 2, lanes), BF16)] * 4

    def first(self, done=()):
        g = self.g
        if not self.regular:
            (whole,) = self.arrays
            both = whole[0].astype(F32) + g.swap(whole[1], "x").astype(F32)
            self.sum = lax.psum_scatter(both, ("z", "y"), scatter_dimension=0, tiled=True)
            return [self.sum]
        keep_x, send_x, keep_y, send_y = self.arrays
        self.got = after([g.swap(send_x, "x"), g.swap(send_y, "y")], done)
        shape = shape_of(keep_x.shape[1:], BF16)
        self.away = call(
            sum_away, [shape] * 2, [keep_x, self.got[0], keep_y, self.got[1]], name="sum_away", vmem=SUM_VMEM
        )
        return self.away

    def wait(self, step, done):
        if self.regular:
            setattr(self, step, after(getattr(self, step), done))

    def second(self, done=()):
        if not self.regular:
            return [self.sum]
        g = self.g
        seconds = after([g.swap(self.away[0], "y"), g.swap(self.away[1], "x")], done)
        half, lanes = self.away[0].shape[1:]
        self.near, *self.far = call(
            sum_line,
            [shape_of((2, half, lanes), F32)] + [shape_of((2, half, lanes), BF16)] * (g.nz - 1),
            [self.arrays[0], self.got[0], seconds[0], self.arrays[2], self.got[1], seconds[1]],
            name="sum_line",
            vmem=SUM_VMEM,
        )
        return [self.near, *self.far]

    def third(self, done=()):
        if not self.regular:
            return self.sum
        total = self.near
        for arrived in after([self.g.swap(far, "z", r + 1) for r, far in enumerate(self.far)], done):
            total = total + arrived.astype(F32)
        return total.reshape(self.rows, total.shape[-1])


SUM_VMEM = 12
VM_HEADS = 40
VM_ROWS = 48
VM_GRAD = 24
VM_BACK = 50
VM_PROJ = 36


def sum_away(keep_x, got_x, keep_y, got_y, out_x, out_y):
    for keep, got, out in ((keep_x, got_x, out_x), (keep_y, got_y, out_y)):
        out[...] = (keep[1].astype(F32) + got[1].astype(F32)).astype(BF16)


def sum_line(keep_x, got_x, last_x, keep_y, got_y, last_y, near, *far):
    for n, (keep, got, last) in enumerate(((keep_x, got_x, last_x), (keep_y, got_y, last_y))):
        for r in range(1 + len(far)):
            total = keep[0, r].astype(F32) + got[0, r].astype(F32) + last[r].astype(F32)
            if r:
                far[r - 1][n] = total.astype(BF16)
            else:
                near[n] = total


def store_blocks(value, outs, place, index, lanes=slice(None)):
    value = value.astype(BF16)
    if len(outs) == 1:
        outs[0][place, :, lanes] = value
        return
    by_x, by_y = outs[place], outs[2:]
    half = by_x.shape[2]
    blocks = value.shape[0] // (2 * half)
    for block in range(blocks):
        slot = block ^ index
        by_x[lax.rem(slot, 2), lax.div(slot, 2), :, lanes] = value[2 * block * half : (2 * block + 1) * half]
    for odd in range(2):

        @pl.when(lax.rem(index, 2) == odd)
        def _():
            for block in range(blocks):
                rows = value[(2 * block + 1) * half : (2 * block + 2) * half]
                by_y[(block + odd) % 2][place, lax.div(block ^ index, 2), :, lanes] = rows


SUMMED = HEAD_DIM + 16


def heads_forward(entries, count, meta, lows, highs, *refs):
    pieces = refs[:count]
    own, other, bias, seg_col, seg_row = refs[count : count + 5]
    q, k, v, w_out, wo_out, ctx_own, ctx_other, lse = refs[count + 5 : count + 13]
    weights, v_t, q_masked, powers, sems = refs[count + 13 :]
    rows = own.shape[0]
    core = meta[0]
    load_pieces(entries, pieces, meta[1], weights, sems, slice(None))
    d = HEAD_DIM
    width = q.shape[1]
    pairs = width // PAIR
    for j in range(pairs):
        for kind in range(4):
            at = slice((4 * j + kind) * d, (4 * j + kind + 1) * d)
            pair = jnp.concatenate([weights[0][:, at], weights[1][:, at]], axis=1)
            lanes = slice(j * PAIR, (j + 1) * PAIR)
            if kind == 3:
                wo_out[:, lanes] = pair
            else:
                w_out[:, kind * width + j * PAIR : kind * width + (j + 1) * PAIR] = pair
    ones = jnp.ones((SUMMED - d, BLOCK), BF16)
    for source, base in ((own, core * rows), (other, (1 - core) * rows)):

        def project(n, carry):
            at = pl.ds(pl.multiple_of(base + n * BLOCK, BLOCK), BLOCK)
            block = source[pl.ds(pl.multiple_of(n * BLOCK, BLOCK), BLOCK), :]
            all_three = dot_nn(block, w_out[...])
            query = (all_three[:, :width] + bias[0:1, :]).astype(BF16)
            q[at, :] = (query.astype(F32) * d**-0.5).astype(BF16)
            k[at, :] = all_three[:, width : 2 * width].astype(BF16)
            values = (all_three[:, 2 * width :] + bias[1:2, :]).astype(BF16)
            v[at, :] = values
            for p in range(pairs):
                columns = values[:, p * PAIR : (p + 1) * PAIR].T
                for h in range(2):
                    v_t[2 * p + h, :d, at] = columns[h * d : (h + 1) * d]
                    v_t[2 * p + h, d:, at] = ones
            return carry

        lax.fori_loop(0, rows // BLOCK, project, 0)
    left = lax.broadcasted_iota(jnp.int32, (BLOCK, PAIR), 1) < d
    half = rows // BLOCK

    def query_block(i, carry):
        at = pl.ds(pl.multiple_of(i * BLOCK, BLOCK), BLOCK)
        seg_q = seg_row[i]
        for p in range(pairs):
            query = q[at, p * PAIR : (p + 1) * PAIR].astype(F32)
            q_masked[2 * p] = jnp.where(left, query, 0.0).astype(BF16)
            q_masked[2 * p + 1] = jnp.where(left, 0.0, query).astype(BF16)

        def key_block(b, carry):
            tops, sums = carry
            rows = pl.ds(pl.multiple_of(b * BLOCK, BLOCK), BLOCK)
            same = seg_col[rows, :] == seg_q
            new_tops, new_sums = [], []
            for h in range(2 * pairs):
                s = dot_nt(k[rows, (h // 2) * PAIR : (h // 2 + 1) * PAIR], q_masked[h])
                s = jnp.where(same, s, MASKED)
                top = jnp.maximum(tops[h], jnp.max(s, axis=0, keepdims=True))
                powers[h] = jnp.exp(s - top).astype(BF16)
                new_tops.append(top)
            for h in range(2 * pairs):
                scale = jnp.exp(tops[h] - new_tops[h])
                new_sums.append(sums[h] * scale + dot_nn(v_t[h, :, rows], powers[h]))
            return tuple(new_tops), tuple(new_sums)

        first_top = jnp.full((1, BLOCK), MASKED, F32)
        first_sum = jnp.zeros((SUMMED, BLOCK), F32)
        tops, sums = lax.fori_loop(
            lows[i], highs[i], key_block, ((first_top,) * (2 * pairs), (first_sum,) * (2 * pairs))
        )
        for p in range(pairs):
            parts = []
            for h in (2 * p, 2 * p + 1):
                total = sums[h][d : d + 1, :]
                lse[i, h : h + 1, :] = tops[h] + jnp.log(total)
                parts.append(sums[h][:d, :] / total)
            ctx = jnp.concatenate(parts, axis=0).T.astype(BF16)
            lanes = slice(p * PAIR, (p + 1) * PAIR)
            own_half = lax.div(i, half) == core
            within = pl.ds(pl.multiple_of(lax.rem(i, half) * BLOCK, BLOCK), BLOCK)

            @pl.when(own_half)
            def _():
                ctx_own[within, lanes] = ctx

            @pl.when(jnp.logical_not(own_half))
            def _():
                ctx_other[within, lanes] = ctx

        return carry

    lax.fori_loop(0, 2 * half, query_block, 0)


def attention_backward(
    meta, lows, highs, da_own, da_other, q, k, v, ctx_own, ctx_other, lse, wo, seg_col, seg_row,
    dqkv, sums, q_masked, d_masked, dq_t, k_t, delta, dk_sum, dv_sum, powers, slopes,
):
    rows = da_own.shape[0]
    seq = 2 * rows
    core = meta[0]
    d = HEAD_DIM
    width = q.shape[1]
    pairs = width // PAIR
    left = lax.broadcasted_iota(jnp.int32, (BLOCK, PAIR), 1) < d
    for source, values, base in ((da_own, ctx_own, core * rows), (da_other, ctx_other, (1 - core) * rows)):
        for r in range(0, rows, BLOCK):
            at = pl.ds(pl.multiple_of(base + r, BLOCK), BLOCK)
            block = (base + r) // BLOCK
            grads = dot_nn(source[r : r + BLOCK, :], wo[...]).astype(BF16).astype(F32)
            for p in range(pairs):
                lanes = slice(p * PAIR, (p + 1) * PAIR)
                grad = grads[:, lanes]
                d_masked[2 * p, at, :] = jnp.where(left, grad, 0.0).astype(BF16)
                d_masked[2 * p + 1, at, :] = jnp.where(left, 0.0, grad).astype(BF16)
                prod = (grad * values[r : r + BLOCK, lanes].astype(F32)).T
                delta[block, 2 * p : 2 * p + 1, :] = jnp.sum(prod[:d], axis=0, keepdims=True)
                delta[block, 2 * p + 1 : 2 * p + 2, :] = jnp.sum(prod[d:], axis=0, keepdims=True)
    for r in range(0, seq, BLOCK):
        for p in range(pairs):
            lanes = slice(p * PAIR, (p + 1) * PAIR)
            query = q[r : r + BLOCK, lanes].astype(F32)
            q_masked[2 * p, r : r + BLOCK, :] = jnp.where(left, query, 0.0).astype(BF16)
            q_masked[2 * p + 1, r : r + BLOCK, :] = jnp.where(left, 0.0, query).astype(BF16)
            k_t[p, :, r : r + BLOCK] = k[r : r + BLOCK, lanes].T
    dq_t[...] = jnp.zeros_like(dq_t)

    def key_block(b, carry):
        at = pl.ds(pl.multiple_of(b * BLOCK, BLOCK), BLOCK)
        seg_k = seg_col[at, :]
        dk_sum[...] = jnp.zeros_like(dk_sum)
        dv_sum[...] = jnp.zeros_like(dv_sum)

        def query_block(i, carry):
            rows_q = pl.ds(pl.multiple_of(i * BLOCK, BLOCK), BLOCK)
            same = seg_k == seg_row[i]
            for h in range(2 * pairs):
                lanes = slice((h // 2) * PAIR, (h // 2 + 1) * PAIR)
                s = jnp.where(same, dot_nt(k[at, lanes], q_masked[h, rows_q, :]), MASKED)
                p = jnp.exp(s - lse[i, h : h + 1, :])
                dp = dot_nt(v[at, lanes], d_masked[h, rows_q, :])
                powers[h] = p.astype(BF16)
                slopes[h] = (p * (dp - delta[i, h : h + 1, :])).astype(BF16)
            for h in range(2 * pairs):
                p, lanes = h // 2, slice((h % 2) * d, (h % 2 + 1) * d)
                dv_sum[p] += dot_nn(powers[h], d_masked[h, rows_q, :])
                dk_sum[p] += dot_nn(slopes[h], q_masked[h, rows_q, :])
                dq_t[p, lanes, rows_q] += dot_nn(k_t[p, lanes, at], slopes[h])
            return carry

        lax.fori_loop(lows[b], highs[b], query_block, 0)
        for p in range(pairs):
            dqkv[at, width + p * PAIR : width + (p + 1) * PAIR] = dk_sum[p].astype(BF16)
            dqkv[at, 2 * width + p * PAIR : 2 * width + (p + 1) * PAIR] = dv_sum[p].astype(BF16)
        return carry

    lax.fori_loop(0, seq // BLOCK, key_block, 0)
    total = jnp.zeros((1, 3 * width), F32)
    for r in range(0, seq, BLOCK):
        for p in range(pairs):
            dqkv[r : r + BLOCK, p * PAIR : (p + 1) * PAIR] = (dq_t[p, :, r : r + BLOCK].T * d**-0.5).astype(BF16)
        total = total + column_sum(dqkv[r : r + BLOCK, :].astype(F32))
    sums[0:1, :] = total


def transpose_tokens(meta, own, other, out):
    rows = own.shape[0]
    for base, source in ((meta[0] * rows, own), ((1 - meta[0]) * rows, other)):
        for r in range(0, rows, BLOCK):
            out[:, pl.ds(pl.multiple_of(base + r, BLOCK), BLOCK)] = source[r : r + BLOCK, :].T


def projection_grad(meta, token_t, da_own, da_other, ctx_own, ctx_other, dqkv, *refs):
    outs, da_t = refs[:-1], refs[-1]
    d = HEAD_DIM
    width = ctx_own.shape[1]
    da_t[...] = da_own[...].T
    part = dot_nn(da_t[...], ctx_own[...])
    da_t[...] = da_other[...].T
    part = part + dot_nn(da_t[...], ctx_other[...])
    full = dot_nn(token_t[...], dqkv[...])
    for place in range(2):
        lanes = []
        for j in range(width // PAIR):
            at = j * PAIR + place * d
            lanes += [full[:, n * width + at : n * width + at + d] for n in range(3)] + [part[:, at : at + d]]
        store_blocks(jnp.concatenate(lanes, axis=1), outs, place, meta[1])


def input_grad_part(groups, other, meta, *refs):
    out = refs[2 * groups]
    rows = out.shape[0]
    base = (1 - meta[0] if other else meta[0]) * rows
    for r in range(0, rows, BLOCK):
        at = pl.ds(pl.multiple_of(base + r, BLOCK), BLOCK)
        total = dot_nt(refs[0][at, :], refs[groups][...])
        for n in range(1, groups):
            total = total + dot_nt(refs[n][at, :], refs[groups + n][...])
        out[r : r + BLOCK, :] = total.astype(out.dtype)


def normalize(values):
    center = jnp.mean(values, axis=-1, keepdims=True)
    offset = values - center
    inverse = lax.rsqrt(jnp.mean(offset * offset, axis=-1, keepdims=True) + EPSILON)
    return offset * inverse, inverse


def normalize_back(incoming, normed, inverse, gain):
    weighted = incoming * gain
    centered = weighted - jnp.mean(weighted, axis=-1, keepdims=True)
    centered = centered - normed * jnp.mean(weighted * normed, axis=-1, keepdims=True)
    return centered * inverse


def column_sum(values):
    return jnp.sum(values, axis=0, keepdims=True)


def accumulate(target, row, value, lanes=slice(None)):
    @pl.when(pl.program_id(0) == 0)
    def _():
        target[row : row + 1, lanes] = value

    @pl.when(pl.program_id(0) != 0)
    def _():
        target[row : row + 1, lanes] += value


def rows_step(
    meta, everywhere, tokens, vectors, ctx_own, ctx_other, wo_own, wo_other, bias, out_grad,
    output, dr1_out, da_out, act_out, du_out, df_t, low_t, sums, bias_sums,
    w_out, w_up, w_down, slope, sems_up, sems_down,
):
    hidden = w_up.shape[2]
    half = ctx_own.shape[1]
    copies_up = everywhere_copies(everywhere, meta[2], w_up, sems_up, slice(0, hidden))
    copies_down = everywhere_copies(everywhere, meta[2], w_down, sems_down, slice(hidden, 2 * hidden))
    start = pl.program_id(0) == 0

    @pl.when(start)
    def _():
        for copy in copies_up + copies_down:
            copy.start()
        w_out[:, :half] = wo_own[...]
        w_out[:, half:] = wo_other[...]

    out_bias, gain_one, shift_one, down_bias, gain_two, shift_two = (vectors[n : n + 1, :] for n in range(6))
    mixed = dot_nt(jnp.concatenate([ctx_own[...], ctx_other[...]], axis=1), w_out[...])
    normed_one, inverse_one = normalize(tokens[...].astype(F32) + mixed + out_bias)
    first = normed_one * gain_one + shift_one
    low = first.astype(BF16)
    low_t[...] = low.T

    @pl.when(start)
    def _():
        for copy in copies_up:
            copy.wait()

    for t in range(4):
        for n in range(0, hidden, BLOCK):
            at = slice(t * hidden + n, t * hidden + n + BLOCK)
            u = dot_nn(low, w_up[t, :, n : n + BLOCK]) + bias[:, at]
            share = 0.5 + 0.5 * lax.erf(u * 0.5**0.5)
            act_out[:, at] = (u * share).astype(BF16)
            slope[:, at] = share + u * (jnp.exp(-0.5 * u * u) * 0.3989422804014327)

    @pl.when(start)
    def _():
        for copy in copies_down:
            copy.wait()

    fed = first + down_bias
    for t in range(4):
        fed = fed + dot_nt(act_out[:, t * hidden : (t + 1) * hidden], w_down[t])
    normed, inverse = normalize(fed)
    output[...] = (normed * gain_two + shift_two).astype(BF16)
    incoming = out_grad[...].astype(F32)
    dr2 = normalize_back(incoming, normed, inverse, gain_two)
    df = dr2.astype(BF16)
    df_t[...] = df.T
    accumulate(sums, 3, column_sum(df.astype(F32)))
    accumulate(sums, 4, column_sum(incoming * normed))
    accumulate(sums, 5, column_sum(incoming))
    for t in range(4):
        for n in range(0, hidden, BLOCK):
            at = slice(t * hidden + n, t * hidden + n + BLOCK)
            du = (dot_nn(df, w_down[t, :, n : n + BLOCK]) * slope[:, at]).astype(BF16)
            du_out[:, at] = du
            accumulate(bias_sums, 0, column_sum(du.astype(F32)), at)
    incoming = dr2
    for t in range(4):
        incoming = incoming + dot_nt(du_out[:, t * hidden : (t + 1) * hidden], w_up[t])
    dr1 = normalize_back(incoming, normed_one, inverse_one, gain_one)
    dr1_out[...] = dr1
    da = dr1.astype(BF16)
    da_out[...] = da
    accumulate(sums, 0, column_sum(da.astype(F32)))
    accumulate(sums, 1, column_sum(incoming * normed_one))
    accumulate(sums, 2, column_sum(incoming))


def grad_for_partner(left_t, *refs):
    count = len(refs) // 2
    for n in range(count):
        refs[count + n][...] = dot_nn(left_t[...], refs[n][...]).astype(BF16)


def grad_for_chip(meta, left_t, right_one, right_two, received_one, received_two, *outs):
    for place, right, received in ((0, right_one, received_one), (1, right_two, received_two)):
        store_blocks(dot_nn(left_t[...], right[...]) + received[...].astype(F32), outs, place, meta[1])


def local(
    g,
    tokens,
    segment_ids,
    qkv_weight,
    qv_bias,
    out_weight,
    out_bias,
    first_gain,
    first_shift,
    up_weight,
    up_bias,
    down_weight,
    down_bias,
    second_gain,
    second_shift,
    output_grad,
):
    rows, width = tokens.shape
    seq = segment_ids.shape[1]
    heads = qkv_weight.shape[2] // HEAD_DIM
    hidden = up_weight.shape[1]
    shard = qkv_weight.shape[0]
    assert seq == 2 * rows and rows % BLOCK == 0
    d = HEAD_DIM
    local_width = heads * d
    z, y, x, c = (lax.axis_index(name) for name in ("z", "y", "x", "c"))
    regular = g.regular(shard)
    meta = jnp.stack([c, (z * 2 + y) if regular else c * 0, x * 2 + c]).astype(jnp.int32)

    segments = lax.dynamic_index_in_dim(segment_ids, x, 0, keepdims=False)
    blocks = seq // BLOCK
    by_block = segments.reshape(blocks, BLOCK)
    lows = jnp.sum((segments[None, :] < by_block[:, :1]).astype(jnp.int32), axis=1) // BLOCK
    highs = (jnp.sum((segments[None, :] <= by_block[:, -1:]).astype(jnp.int32), axis=1) + BLOCK - 1) // BLOCK
    seg_col = segments.reshape(seq, 1)
    seg_row = segments.reshape(blocks, 1, BLOCK)

    small = jnp.concatenate([up_bias, qv_bias.reshape(-1)]).reshape(1, -1)
    small = jnp.concatenate([small, g.swap(small, "c")], axis=0)
    small = jnp.concatenate([small, g.swap(small, "x")], axis=0).astype(F32)
    hidden_bias = small[:, :hidden].reshape(1, 4 * hidden)
    pair_bias = small[:, hidden:].reshape(2, 2, 2, heads, d)[:, 0].transpose(1, 2, 0, 3)
    pair_bias = pair_bias.reshape(2, heads * PAIR)
    vectors = jnp.stack(
        [out_bias, first_gain, first_shift, down_bias, second_gain, second_shift, out_bias, out_bias]
    ).astype(F32)

    parts = []
    for j in range(heads):
        at = slice(j * d, (j + 1) * d)
        parts += [qkv_weight[:, n, at] for n in range(3)] + [out_weight[:, at]]
    head_weights = Gather(g, jnp.concatenate(parts, axis=1))
    both = gather_everywhere(g, jnp.concatenate([up_weight, down_weight], axis=1))
    other_tokens = g.swap(tokens, "c")
    head_weights.line()
    (token_t,) = call(
        transpose_tokens,
        [shape_of((width, seq), BF16)],
        [meta, tokens, other_tokens],
        in_specs=[SMEM, VMEM, VMEM],
        name="transpose_tokens",
        vmem=16,
    )
    head_weights.first(token_t)
    head_weights.second()

    lanes = heads * PAIR
    blocks = seq // BLOCK
    count = len(head_weights.arrays)
    q, k, v, w, wo, ctx_own, ctx_send, lse = call(
        partial(heads_forward, head_weights.entries, count),
        [shape_of((seq, lanes), BF16)] * 3
        + [shape_of((width, 3 * lanes), BF16), shape_of((width, lanes), BF16)]
        + [shape_of((rows, lanes), BF16)] * 2
        + [shape_of((blocks, 8, BLOCK), F32)],
        [meta, lows, highs, *head_weights.arrays, tokens, other_tokens, pair_bias, seg_col, seg_row],
        in_specs=[SMEM] * 3 + [ANY] * count + [VMEM] * 5,
        scratch=[
            pltpu.VMEM((2, width, 2 * lanes), BF16),
            pltpu.VMEM((2 * heads, SUMMED, seq), BF16),
            pltpu.VMEM((2 * heads, BLOCK, PAIR), BF16),
            pltpu.VMEM((2 * heads, BLOCK, BLOCK), BF16),
            pltpu.SemaphoreType.DMA((len(head_weights.entries),)),
        ],
        flops=2 * seq * width * 3 * lanes + 4 * seq * seq * lanes,
        name="heads_forward",
        vmem=VM_HEADS,
    )
    ctx_other = g.swap(ctx_send, "c")
    other_wo = g.swap(wo, "c")

    def by_rows(lanes):
        return pl.BlockSpec((BLOCK, lanes), lambda i: (i, 0))

    def by_columns(array_rows):
        return pl.BlockSpec((array_rows, BLOCK), lambda i: (0, i))

    def fixed(array):
        return pl.BlockSpec(array.shape, lambda i: (0,) * len(array.shape))

    ffn = 2 * rows * width * 4 * hidden
    sums_shape = shape_of((8, width), F32)
    bias_shape = shape_of((8, 4 * hidden), F32)
    weight_sems = pltpu.SemaphoreType.DMA((both.shape[0] * both.shape[1],))
    output, dr1, da, act, du, df_t, low_t, sums_rows, hidden_sums = call(
        rows_step,
        [
            shape_of((rows, width), BF16),
            shape_of((rows, width), F32),
            shape_of((rows, width), BF16),
            shape_of((rows, 4 * hidden), BF16),
            shape_of((rows, 4 * hidden), BF16),
            shape_of((width, rows), BF16),
            shape_of((width, rows), BF16),
            sums_shape,
            bias_shape,
        ],
        [meta, both, tokens, vectors, ctx_own, ctx_other, wo, other_wo, hidden_bias, output_grad],
        in_specs=[SMEM, ANY, by_rows(width), fixed(vectors), by_rows(lanes), by_rows(lanes), fixed(wo), fixed(wo)]
        + [fixed(hidden_bias), by_rows(width)],
        out_specs=[by_rows(width)] * 3
        + [by_rows(4 * hidden)] * 2
        + [by_columns(width)] * 2
        + [fixed(sums_shape), fixed(bias_shape)],
        scratch=[
            pltpu.VMEM((width, width), BF16),
            pltpu.VMEM((4, width, hidden), BF16),
            pltpu.VMEM((4, width, hidden), BF16),
            pltpu.VMEM((BLOCK, 4 * hidden), F32),
            weight_sems,
            weight_sems,
        ],
        grid=(rows // BLOCK,),
        flops=4 * ffn + 2 * rows * width * width,
        name="rows_step",
        vmem=VM_ROWS,
    )
    other_da = g.swap(da, "c")
    tiles = hidden // BLOCK
    left_spec = pl.BlockSpec((width, rows), lambda i: (0, 0))

    def partner_grad(left_t, right):
        return call(
            grad_for_partner,
            [shape_of((width, hidden), BF16)] * 2,
            [left_t, right, right],
            in_specs=[left_spec] + [pl.BlockSpec((rows, BLOCK), lambda i, t=t: (0, t * tiles + i)) for t in (1, 3)],
            out_specs=[by_columns(width)] * 2,
            grid=(tiles,),
            flops=ffn // 2,
            name="grad_for_partner",
            vmem=VM_GRAD,
        )

    def chip_grad(left_t, right, received):
        leaving = Scatter.shapes(g, shard, hidden)
        arrays = call(
            grad_for_chip,
            leaving,
            [meta, left_t, right, right, *received],
            in_specs=[SMEM, left_spec]
            + [pl.BlockSpec((rows, BLOCK), lambda i, t=t: (0, t * tiles + i)) for t in (0, 2)]
            + [by_columns(width)] * 2,
            out_specs=[
                pl.BlockSpec((*a.shape[:-1], BLOCK), lambda i, n=len(a.shape) - 1: (0,) * n + (i,)) for a in leaving
            ],
            grid=(tiles,),
            flops=ffn // 2,
            name="grad_for_chip",
            vmem=VM_GRAD,
        )
        return Scatter(g, shard, arrays)

    down_other = partner_grad(df_t, act)
    down_received = [g.swap(a, "c") for a in down_other]
    up_other = partner_grad(after(low_t, down_other), du)
    up_received = [g.swap(a, "c") for a in up_other]
    down_grad = chip_grad(after(df_t, up_other), act, down_received)
    up_grad = chip_grad(after(low_t, down_grad.arrays), du, up_received)
    down_away = down_grad.first(up_grad.arrays)

    dqkv, head_sums = call(
        attention_backward,
        [shape_of((seq, 3 * lanes), BF16), shape_of((8, 3 * lanes), F32)],
        [meta, lows, highs, after(da, down_away), other_da, q, k, v, ctx_own, ctx_send, lse, wo, seg_col, seg_row],
        in_specs=[SMEM] * 3 + [VMEM] * 11,
        scratch=[
            pltpu.VMEM((2 * heads, seq, PAIR), BF16),
            pltpu.VMEM((2 * heads, seq, PAIR), BF16),
            pltpu.VMEM((heads, PAIR, seq), F32),
            pltpu.VMEM((heads, PAIR, seq), BF16),
            pltpu.VMEM((blocks, 8, BLOCK), F32),
            pltpu.VMEM((heads, BLOCK, PAIR), F32),
            pltpu.VMEM((heads, BLOCK, PAIR), F32),
            pltpu.VMEM((2 * heads, BLOCK, BLOCK), BF16),
            pltpu.VMEM((2 * heads, BLOCK, BLOCK), BF16),
        ],
        flops=2 * seq * width * lanes + 10 * seq * seq * lanes,
        name="attention_backward",
        vmem=VM_BACK,
    )
    up_away = up_grad.first(dqkv)
    down_second = down_grad.second(dqkv)
    arrays = call(
        projection_grad,
        Scatter.shapes(g, shard, 2 * lanes),
        [meta, token_t, da, other_da, ctx_own, ctx_send, after(dqkv, (up_away, down_second))],
        in_specs=[SMEM] + [VMEM] * 6,
        scratch=[pltpu.VMEM((width, rows), BF16)],
        flops=2 * seq * width * 4 * lanes,
        name="projection_grad",
        vmem=VM_PROJ,
    )
    head_grad = Scatter(g, shard, arrays)

    six = sums_rows[:6]
    six = (six + g.swap(six, "c")).reshape(-1)
    hidden_sums = hidden_sums[0].reshape(2, 2, hidden)
    hidden_sums = hidden_sums[:, 0] + g.swap(hidden_sums[:, 1], "c")
    kinds = head_sums[0].reshape(3, heads, 2, d).transpose(2, 0, 1, 3).reshape(2, 3, local_width)
    keep, send = (jnp.concatenate([six, hidden_sums[r], kinds[r, 0], kinds[r, 2]]) for r in range(2))

    def input_part(first, dtype, dqkv):
        return call(
            partial(input_grad_part, 1, first),
            [shape_of((rows, width), dtype)],
            [meta, dqkv, w],
            in_specs=[SMEM] + [VMEM] * 2,
            flops=seq * width * 3 * lanes,
            name="input_grad_part",
            vmem=VM_PROJ,
        )[0]

    up_second = up_grad.second(arrays)
    down_share = down_grad.third(arrays)
    ig_other = input_part(1, BF16, after(dqkv, (up_second, down_share)))
    head_away = head_grad.first(ig_other)
    summed = keep + after(g.swap(send, "x"), ig_other)
    ig_own = input_part(0, F32, after(dqkv, head_away))
    head_grad.second(ig_own)
    up_share = up_grad.third(ig_own)
    shares = head_grad.third().reshape(shard, heads, 4, d)
    summed = g.total_dp(summed)
    vectors_grad = summed[: 6 * width].reshape(6, width)
    up_bias_share = summed[6 * width : 6 * width + hidden]
    qv_share = summed[6 * width + hidden :].reshape(2, local_width)
    input_grad = dr1 + ig_own + g.swap(ig_other, "c").astype(F32)
    qkv_share = shares[:, :, :3].transpose(0, 2, 1, 3).reshape(shard, 3, local_width)
    out_share = shares[:, :, 3].reshape(shard, local_width)
    return (output, input_grad, qkv_share, qv_share, out_share, up_share, up_bias_share, down_share, vectors_grad)


def solution(mesh):
    g = Grid(mesh)
    dp, tensor = ("z", "y"), ("x", "c")
    rows = P(dp + tensor, None)
    in_specs = (
        rows,
        P(dp, None),
        P(dp, None, tensor),
        P(None, tensor),
        P(dp, tensor),
        P(),
        P(),
        P(),
        P(dp, tensor),
        P(tensor),
        P(dp, tensor),
        P(),
        P(),
        P(),
        rows,
    )
    out_specs = (
        rows,
        rows,
        P(dp, None, tensor),
        P(None, tensor),
        P(dp, tensor),
        P(dp, tensor),
        P(tensor),
        P(dp, tensor),
        P(),
    )
    return jax.shard_map(partial(local, g), mesh=g.mesh, in_specs=in_specs, out_specs=out_specs, check_vma=False)
```

time: 1480 us -> 371 us (0.25)
  waiting for transfers between devices: 586 us -> 71.2 us
  matrix products: 424 us -> 0 us
  Pallas kernels: 0 us -> 194 us
  blocking collectives: 136 us -> 0 us
  other arithmetic: 146 us -> 11.2 us
  local copies, waits for them, and re-layouts: 122 us -> 35.9 us
  starting transfers between devices: 10.9 us -> 39.6 us
  loops' own time: 28 us -> 0 us
    reduce_scatter x8 -> x0, waiting for transfers between devices: 437 us -> none  [the longest x1 97.6 us: local(): lax.psum_scatter(times_transposed(context, out_full), 'tensor', scatter_d...]
    dot_general x68 -> x0, matrix products: 424 us -> none  [the longest x16 71.9 us: masked_scores(): jnp.einsum('qhd,khd->hqk', query_rows, key_seq, preferred_element_type=jn...]
    pallas_call x0 -> x17, Pallas kernels: none -> 194 us  [call(): pl.pallas_call(body, grid=grid, out_shape=outs, in_specs=in_specs or [VME...]
    all_gather x6 -> x1, waiting for transfers between devices: 147 us -> 0.01 us  [gather_everywhere(): full = lax.all_gather(shard, ('z', 'y', 'x', 'c'), axis=0)]
    reduce_sum x17 -> x1, other arithmetic: 75.1 us -> 0.24 us  [local(): jnp.sum((segments[None, :] <= by_block[:, -1:]).astype(jnp.int32), axis=1)]
    all_gather x2 -> x0, blocking collectives: 72 us -> none  [the longest x1 38.8 us: local(): lax.all_gather(qkv_weight, 'dp', axis=0, tiled=True)]
    ppermute x0 -> x45, waiting for transfers between devices: none -> 71.2 us  [swap(): return lax.ppermute(array, axis, [(i, i ^ r) for i in range(size)])]
    psum x2 -> x0, blocking collectives: 63.5 us -> none  [the longest x1 41 us: local(): lax.psum(jnp.stack([out_bias_g, gain_one_g, shift_one_g, down_bias_g, gai...]
  transfers between devices with their start and end apart: 14 -> 46, of which waited for: 11 -> 14; matrix products, arithmetic and copies ran while one was open for 6% -> 6% of each run, Pallas kernels for 0% -> 37%
where the time goes in v2:
time: 371 us; the launch traced here: 367 us
  Pallas kernels  194 us (52%)
  waiting for transfers between devices  71.2 us (19%)
  starting transfers between devices  39.6 us (11%)
  local copies, waits for them, and re-layouts  35.9 us (10%)
  between operations  15.1 us (4%)
  other arithmetic  11.2 us (3%)
    pallas_call x17, Pallas kernels, call(): pl.pallas_call(body, grid=grid, out_shape=outs, in_specs=in_specs or [VME...  194 us
    ppermute x45, waiting for transfers between devices, swap(): return lax.ppermute(array, axis, [(i, i ^ r) for i in range(size)])  71.2 us
    ppermute x45, starting transfers between devices, swap(): return lax.ppermute(array, axis, [(i, i ^ r) for i in range(size)])  39.5 us
    unnamed x96, local copies, waits for them, and re-layouts  21 us
  transfers between devices with their start and end apart: 46, of which 14 were waited for; matrix products, arithmetic and copies ran while one was open for 6% of the time, Pallas kernels for 37%

profile of v2, /device:TPU:0, one launch (start us, length us, event | category | flops | bytes accessed | tf_op | source)
XLA Modules:
  0.0 367.2 jit_solution(2330723851061018349)
XLA Ops:
  11.1 5.1 %collective-permute-start.2 = (bf16[96,768]{1,0:T(8,128)(2,1)S(1)}, bf16[96,768]{1,0:T(8,128)(2,1)}, u32[]{:S(2)}, u32[]{:S(2)}) collective-permute-start(bf16[96,768]{1,0:T(8,128)(2,1)S(1)} %concatenate.23), channel_id=1, source_target_pairs={{0,24},{8,16},{16,8},{24,0},{1,25},{9,17},{17,9},{25,1},{2,26},{10... | collective-permute-start | bytes 442376 | tf_op jit(solution)/shard_map/ppermute | solution.py:68
  22.1 10.7 %collective-permute-done.1 = bf16[96,768]{1,0:T(8,128)(2,1)} collective-permute-done((bf16[96,768]{1,0:T(8,128)(2,1)S(1)}, bf16[96,768]{1,0:T(8,128)(2,1)}, u32[]{:S(2)}, u32[]{:S(2)}) %collective-permute-start.1) | collective-permute-done | bytes 147488 | tf_op jit(solution)/shard_map/ppermute | solution.py:68
  49.4 14.4 %collective-permute-done.9 = bf16[2,1152]{1,0:T(2,128)(2,1)S(1)} collective-permute-done((bf16[2,1152]{1,0:T(2,128)(2,1)S(1)}, bf16[2,1152]{1,0:T(2,128)(2,1)S(1)}, u32[]{:S(2)}, u32[]{:S(2)}) %collective-permute-start.9) | collective-permute-done | bytes 4640 | tf_op jit(solution)/shard_map/ppermute | solution.py:68
  65.2 44.8 %heads_forward.1 = (bf16[2048,384]{1,0:T(8,128)(2,1)S(1)}, bf16[2048,384]{1,0:T(8,128)(2,1)S(1)}, bf16[2048,384]{1,0:T(8,128)(2,1)S(1)}, bf16[768,1152]{1,0:T(8,...) custom-call(s32[3]{0:T(128)S(1)} %pad_add_fusion.meta, ...), custom_call_target="tpu_custom_call" | custom-call | flops 10066329600 | bytes 14240844 | tf_op jit(solution)/shard_map/heads_forward/pallas_call | solution.py:31
  115.0 2.6 collective-permute-done.11.wo_other
  118.8 55.4 %rows_step.1 = (bf16[1024,768]{1,0:T(8,128)(2,1)}, f32[1024,768]{1,0:T(8,128)}, bf16[1024,768]{1,0:T(8,128)(2,1)}, bf16[1024,3072]{1,0:T(8,128)(2,1)}, bf16[1024...) custom-call(s32[3]{0:T(128)S(1)} %pad_add_fusion.meta, ...), custom_call_target="tpu_custom_call" | custom-call | flops 20535312384 | bytes 37515276 | tf_op jit(solution)/shard_map/rows_step/pallas_call | solution.py:31
  174.2 2.9 copy-done
  177.1 4.6 %grad_for_partner.2 = (bf16[768,768]{1,0:T(8,128)(2,1)}, bf16[768,768]{1,0:T(8,128)(2,1)}) custom-call(bf16[768,1024]{1,0:T(8,128)(2,1)S(1)} %get-tuple-element.110.left_t, bf16[1024,3072]{1,0:T(8,128)(2,1)S(1)} %copy-done, bf16[1024,3072]{1,0:T(8,128)(2,1)S(1)} %copy-done), custom_call_target="tpu_custom_call" | custom-call | flops 2415919104 | bytes 16515072 | tf_op jit(solution)/shard_map/grad_for_partner/pallas_call | solution.py:31
  182.3 4.4 %grad_for_partner.3 = (bf16[768,768]{1,0:T(8,128)(2,1)}, bf16[768,768]{1,0:T(8,128)(2,1)}) custom-call(bf16[768,1024]{1,0:T(8,128)(2,1)S(1)} %copy-done.6, bf16[1024,3072]{1,0:T(8,128)(2,1)S(1)} %bitcast.79, bf16[1024,3072]{1,0:T(8,128)(2,1)S(1)} %bitcast.79), custom_call_target="tpu_custom_call" | custom-call | flops 2415919104 | bytes 16515072 | tf_op jit(solution)/shard_map/grad_for_partner/pallas_call | solution.py:31
  187.8 3.0 copy-done.1
  190.9 7.6 %grad_for_chip.2 = (bf16[2,4,48,768]{3,2,1,0:T(8,128)(2,1)S(1)}, bf16[2,4,48,768]{3,2,1,0:T(8,128)(2,1)S(1)}, bf16[2,4,48,768]{3,2,1,0:T(8,128)(2,1)S(1)}, bf16[2,4,48,768]{3,2,1,0:T(8,128)(2,1)S(1)}) custom-call(s32[3]{0:T(128)S(1)} %pad_add_fusion.meta, bf16[768,1024]{1,0:T(8,128)(2,1)S(1)} %get-tuple-element.110.left_t, bf16[1024,3072]{1,0:T(8,128)(2,1)S(1)} %copy-done.1, ...), custom_call_target="tpu_custom_call" | custom-call | flops 2415919104 | bytes 18874380 | tf_op jit(solution)/shard_map/grad_for_chip/pallas_call | solution.py:31
  200.7 7.6 %grad_for_chip.3 = (bf16[2,4,48,768]{3,2,1,0:T(8,128)(2,1)S(1)}, bf16[2,4,48,768]{3,2,1,0:T(8,128)(2,1)S(1)}, bf16[2,4,48,768]{3,2,1,0:T(8,128)(2,1)S(1)}, bf16[2,4,48,768]{3,2,1,0:T(8,128)(2,1)S(1)}) custom-call(s32[3]{0:T(128)S(1)} %pad_add_fusion.meta, bf16[768,1024]{1,0:T(8,128)(2,1)S(1)} %copy-done.6, bf16[1024,3072]{1,0:T(8,128)(2,1)S(1)} %bitcast.81, ...), custom_call_target="tpu_custom_call" | custom-call | flops 2415919104 | bytes 18874380 | tf_op jit(solution)/shard_map/grad_for_chip/pallas_call | solution.py:31
  210.5 4.3 %collective-permute-done.14.got_x = bf16[2,4,48,768]{3,2,1,0:T(8,128)(2,1)S(1)} collective-permute-done((bf16[2,4,48,768]{3,2,1,0:T(8,128)(2,1)S(1)}, bf16[2,4,48,768]{3,2,1,0:T(8,128)(2,1)S(1)}, u32[]{:S(2)}, u32[]{:S(2)}) %collective-permute-start.14) | collective-permute-done | bytes 589856 | tf_op jit(solution)/shard_map/ppermute | solution.py:68
  217.2 48.7 %attention_backward.1 = (bf16[2048,1152]{1,0:T(8,128)(2,1)}, f32[8,1152]{1,0:T(8,128)S(1)}) custom-call(s32[3]{0:T(128)S(1)} %pad_add_fusion.meta, s32[8]{0:T(128)S(1)} %get-tuple-element.243.lows, s32[8]{0:T(128)S(1)} %get-tuple-element.242.highs, bf16[1024,768]{1,0:T(8,128)(2,1)} %get-tuple-element.124.da_own, ...), custom_call_target="tpu_custom_call" | custom-call | flops 17314086912 | bytes 14864460 | tf_op jit(solution)/shard_map/attention_backward/pallas_call | solution.py:31
  274.0 9.6 %projection_grad.1 = (bf16[2,4,48,768]{3,2,1,0:T(8,128)(2,1)S(1)}, bf16[2,4,48,768]{3,2,1,0:T(8,128)(2,1)}, bf16[2,4,48,768]{3,2,1,0:T(8,128)(2,1)S(1)}, bf16[2,4,48,768]{3,2,1,0:T(8,128)(2,1)S(1)}) custom-call(s32[3]{0:T(128)S(1)} %pad_add_fusion.meta, bf16[768,2048]{1,0:T(8,128)(2,1)S(1)} %copy-done.8, bf16[1024,768]{1,0:T(8,128)(2,1)} %get-tuple-element.124.da_own, ...), custom_call_target="tpu_custom_call" | custom-call | flops 4831838208 | bytes 14942220 | tf_op jit(solution)/shard_map/projection_grad/pallas_call | solution.py:31
  287.4 3.9 %input_grad_part.2 = bf16[1024,768]{1,0:T(8,128)(2,1)} custom-call(s32[3]{0:T(128)S(1)} %pad_add_fusion.meta, bf16[2048,1152]{1,0:T(8,128)(2,1)S(1)} %copy-done.2, bf16[768,1152]{1,0:T(8,128)(2,1)S(1)} %copy-done.4), custom_call_target="tpu_custom_call" | custom-call | flops 1811939328 | bytes 8060940 | tf_op jit(solution)/shard_map/input_grad_part/pallas_call | solution.py:31
  291.7 8.1 %collective-permute-done.23.got_x = bf16[2,4,48,768]{3,2,1,0:T(8,128)(2,1)S(1)} collective-permute-done((bf16[2,4,48,768]{3,2,1,0:T(8,128)(2,1)}, bf16[2,4,48,768]{3,2,1,0:T(8,128)(2,1)S(1)}, u32[]{:S(2)}, u32[]{:S(2)}) %collective-permute-start.23) | collective-permute-done | bytes 589856 | tf_op jit(solution)/shard_map/ppermute | solution.py:68
  305.5 6.8 %collective-permute-done.38 = f32[5760]{0:T(1024)S(1)} collective-permute-done((f32[5760]{0:T(1024)S(1)}, f32[5760]{0:T(1024)S(1)}, u32[]{:S(2)}, u32[]{:S(2)}) %collective-permute-start.38) | collective-permute-done | bytes 23072 | tf_op jit(solution)/shard_map/ppermute | solution.py:68
  313.7 2.5 collective-permute-done.39
  316.2 4.1 %collective-permute-done.40 = f32[5760]{0:T(1024)S(1)} collective-permute-done((f32[5760]{0:T(1024)S(1)}, f32[5760]{0:T(1024)S(1)}, u32[]{:S(2)}, u32[]{:S(2)}) %collective-permute-start.40) | collective-permute-done | bytes 23072 | tf_op jit(solution)/shard_map/ppermute | solution.py:68
  320.9 4.8 %collective-permute-done.41 = f32[5760]{0:T(1024)S(1)} collective-permute-done((f32[5760]{0:T(1024)S(1)}, f32[5760]{0:T(1024)S(1)}, u32[]{:S(2)}, u32[]{:S(2)}) %collective-permute-start.41) | collective-permute-done | bytes 23072 | tf_op jit(solution)/shard_map/ppermute | solution.py:68
  333.8 2.8 input_grad_part.3
  344.1 4.2 %collective-permute-done.34 = bf16[2,48,768]{2,1,0:T(8,128)(2,1)S(1)} collective-permute-done((bf16[2,48,768]{2,1,0:T(8,128)(2,1)S(1)}, bf16[2,48,768]{2,1,0:T(8,128)(2,1)S(1)}, u32[]{:S(2)}, u32[]{:S(2)}) %collective-permute-start.34) | collective-permute-done | bytes 147488 | tf_op jit(solution)/shard_map/ppermute | solution.py:68
  355.6 4.5 %convert_add_fusion = f32[1024,768]{1,0:T(8,128)} fusion(bf16[1024,768]{1,0:T(8,128)(2,1)} %collective-permute-done.30, f32[1024,768]{1,0:T(8,128)} %get-tuple-element.99, f32[1024,768]{1,0:T(8,128)S(1)} %input_grad_part.3), kind=kLoop, calls=%fused_computation | loop fusion | flops 2359296 | bytes 11010048 | tf_op jit(solution)/shard_map/add | solution.py:826
  (254 shorter events, 84.8 us)
Async XLA Ops:
  7.2 110.4 %all-gather.3.cloned.1.call-start = ((), (), s32[]{:S(2)}) async-start(), calls=%async_computation | async-start | bytes 9732096 | tf_op jit(solution)/shard_map/all_gather | solution.py:144
  16.2 16.5 %collective-permute-start.1 = (bf16[96,768]{1,0:T(8,128)(2,1)S(1)}, bf16[96,768]{1,0:T(8,128)(2,1)}, u32[]{:S(2)}, u32[]{:S(2)}) collective-permute-start(bf16[96,768]{1,0:T(8,128)(2,1)S(1)} %concatenate.23), channel_id=1, source_target_pairs={{0,16},{8,24},{16,0},{24,8},{1,17},{9,25},{17,1},{25,9},{2,18},{10... | collective-permute-start | bytes 442376 | tf_op jit(solution)/shard_map/ppermute | solution.py:68
  16.3 17.5 %collective-permute-start = (bf16[96,768]{1,0:T(8,128)(2,1)S(1)}, bf16[96,768]{1,0:T(8,128)(2,1)S(1)}, u32[]{:S(2)}, u32[]{:S(2)}) collective-permute-start(bf16[96,768]{1,0:T(8,128)(2,1)S(1)} %concatenate.23), channel_id=1, source_target_pairs={{0,8},{8,0},{16,24},{24,16},{1,9},{9,1},{17,25},{25,17},{2,10},{10... | collective-permute-start | bytes 442376 | tf_op jit(solution)/shard_map/ppermute | solution.py:68
  17.0 30.9 %collective-permute-start.8 = (bf16[1,1152]{1,0:T(2,128)(2,1)S(1)}, bf16[1,1152]{1,0:T(2,128)(2,1)S(1)}, u32[]{:S(2)}, u32[]{:S(2)}) collective-permute-start(bf16[1,1152]{1,0:T(2,128)(2,1)S(1)} %reshape.78), channel_id=1, source_target_pairs={{0,1},{1,0},{2,3},{3,2},{4,5},{5,4},{6,7},{7,6},{8,9},{9,8},{10,11... | collective-permute-start | bytes 6920 | tf_op jit(solution)/shard_map/ppermute | solution.py:68
  17.1 21.2 %collective-permute-start.5 = (bf16[1024,768]{1,0:T(8,128)(2,1)S(1)}, bf16[1024,768]{1,0:T(8,128)(2,1)S(1)}, u32[]{:S(2)}, u32[]{:S(2)}) collective-permute-start(bf16[1024,768]{1,0:T(8,128)(2,1)S(1)} %copy-done.21), channel_id=1, source_target_pairs={{0,1},{1,0},{2,3},{3,2},{4,5},{5,4},{6,7},{7,6},{8,9},{9,8},{10,11... | collective-permute-start | bytes 4718600 | tf_op jit(solution)/shard_map/ppermute | solution.py:68
  44.6 19.4 %collective-permute-start.7 = (bf16[2,4,48,768]{3,2,1,0:T(8,128)(2,1)}, bf16[2,4,48,768]{3,2,1,0:T(8,128)(2,1)}, u32[]{:S(2)}, u32[]{:S(2)}) collective-permute-start(bf16[2,4,48,768]{3,2,1,0:T(8,128)(2,1)} %pad_maximum_fusion.1.refs_2_), channel_id=1, source_target_pairs={{0,2},{2,0},{1,3},{3,1},{4,6},{6,4},{5,7},{7,5},{8,10},{10,8},{9,1... | collective-permute-start | bytes 1769480 | tf_op jit(solution)/shard_map/ppermute | solution.py:68
  47.9 16.0 %collective-permute-start.6 = (bf16[2,4,48,768]{3,2,1,0:T(8,128)(2,1)}, bf16[2,4,48,768]{3,2,1,0:T(8,128)(2,1)}, u32[]{:S(2)}, u32[]{:S(2)}) collective-permute-start(bf16[2,4,48,768]{3,2,1,0:T(8,128)(2,1)} %pad_maximum_fusion.refs_0_), channel_id=1, source_target_pairs={{0,4},{4,0},{1,5},{5,1},{2,6},{6,2},{3,7},{7,3},{8,12},{12,8},{9,1... | collective-permute-start | bytes 1769480 | tf_op jit(solution)/shard_map/ppermute | solution.py:68
  47.9 15.8 %collective-permute-start.9 = (bf16[2,1152]{1,0:T(2,128)(2,1)S(1)}, bf16[2,1152]{1,0:T(2,128)(2,1)S(1)}, u32[]{:S(2)}, u32[]{:S(2)}) collective-permute-start(bf16[2,1152]{1,0:T(2,128)(2,1)S(1)} %pad_maximum_fusion.7), channel_id=1, source_target_pairs={{0,2},{2,0},{1,3},{3,1},{4,6},{6,4},{5,7},{7,5},{8,10},{10,8},{9,1... | collective-permute-start | bytes 13832 | tf_op jit(solution)/shard_map/ppermute | solution.py:68
  182.2 35.0 %collective-permute-start.18 = (bf16[1024,768]{1,0:T(8,128)(2,1)}, bf16[1024,768]{1,0:T(8,128)(2,1)}, u32[]{:S(2)}, u32[]{:S(2)}) collective-permute-start(bf16[1024,768]{1,0:T(8,128)(2,1)} %get-tuple-element.124.da_own), channel_id=1, source_target_pairs={{0,1},{1,0},{2,3},{3,2},{4,5},{5,4},{6,7},{7,6},{8,9},{9,8},{10,11... | collective-permute-start | bytes 4718600 | tf_op jit(solution)/shard_map/ppermute | solution.py:68
  198.5 16.3 %collective-permute-start.14 = (bf16[2,4,48,768]{3,2,1,0:T(8,128)(2,1)S(1)}, bf16[2,4,48,768]{3,2,1,0:T(8,128)(2,1)S(1)}, u32[]{:S(2)}, u32[]{:S(2)}) collective-permute-start(bf16[2,4,48,768]{3,2,1,0:T(8,128)(2,1)S(1)} %get-tuple-element.112), channel_id=1, source_target_pairs={{0,2},{2,0},{1,3},{3,1},{4,6},{6,4},{5,7},{7,5},{8,10},{10,8},{9,1... | collective-permute-start | bytes 1769480 | tf_op jit(solution)/shard_map/ppermute | solution.py:68
  200.6 16.2 %collective-permute-start.15 = (bf16[2,4,48,768]{3,2,1,0:T(8,128)(2,1)S(1)}, bf16[2,4,48,768]{3,2,1,0:T(8,128)(2,1)S(1)}, u32[]{:S(2)}, u32[]{:S(2)}) collective-permute-start(bf16[2,4,48,768]{3,2,1,0:T(8,128)(2,1)S(1)} %get-tuple-element.113), channel_id=1, source_target_pairs={{0,4},{4,0},{1,5},{5,1},{2,6},{6,2},{3,7},{7,3},{8,12},{12,8},{9,1... | collective-permute-start | bytes 1769480 | tf_op jit(solution)/shard_map/ppermute | solution.py:68
  208.3 57.6 %collective-permute-start.19 = (bf16[2,4,48,768]{3,2,1,0:T(8,128)(2,1)S(1)}, bf16[2,4,48,768]{3,2,1,0:T(8,128)(2,1)S(1)}, u32[]{:S(2)}, u32[]{:S(2)}) collective-permute-start(bf16[2,4,48,768]{3,2,1,0:T(8,128)(2,1)S(1)} %get-tuple-element.117), channel_id=1, source_target_pairs={{0,2},{2,0},{1,3},{3,1},{4,6},{6,4},{5,7},{7,5},{8,10},{10,8},{9,1... | collective-permute-start | bytes 1769480 | tf_op jit(solution)/shard_map/ppermute | solution.py:68
  208.6 57.3 %collective-permute-start.20 = (bf16[2,4,48,768]{3,2,1,0:T(8,128)(2,1)S(1)}, bf16[2,4,48,768]{3,2,1,0:T(8,128)(2,1)S(1)}, u32[]{:S(2)}, u32[]{:S(2)}) collective-permute-start(bf16[2,4,48,768]{3,2,1,0:T(8,128)(2,1)S(1)} %get-tuple-element.119), channel_id=1, source_target_pairs={{0,4},{4,0},{1,5},{5,1},{2,6},{6,2},{3,7},{7,3},{8,12},{12,8},{9,1... | collective-permute-start | bytes 1769480 | tf_op jit(solution)/shard_map/ppermute | solution.py:68
  216.9 51.3 %collective-permute-start.21 = (bf16[4,48,768]{2,1,0:T(8,128)(2,1)S(1)}, bf16[4,48,768]{2,1,0:T(8,128)(2,1)S(1)}, u32[]{:S(2)}, u32[]{:S(2)}) collective-permute-start(bf16[4,48,768]{2,1,0:T(8,128)(2,1)S(1)} %get-tuple-element.122), channel_id=1, source_target_pairs={{0,4},{4,0},{1,5},{5,1},{2,6},{6,2},{3,7},{7,3},{8,12},{12,8},{9,1... | collective-permute-start | bytes 884744 | tf_op jit(solution)/shard_map/ppermute | solution.py:68
  217.0 51.2 %collective-permute-start.22 = (bf16[4,48,768]{2,1,0:T(8,128)(2,1)S(1)}, bf16[4,48,768]{2,1,0:T(8,128)(2,1)S(1)}, u32[]{:S(2)}, u32[]{:S(2)}) collective-permute-start(bf16[4,48,768]{2,1,0:T(8,128)(2,1)S(1)} %get-tuple-element.123), channel_id=1, source_target_pairs={{0,2},{2,0},{1,3},{3,1},{4,6},{6,4},{5,7},{7,5},{8,10},{10,8},{9,1... | collective-permute-start | bytes 884744 | tf_op jit(solution)/shard_map/ppermute | solution.py:68
  266.1 17.6 %collective-permute-start.25 = (bf16[4,48,768]{2,1,0:T(8,128)(2,1)S(1)}, bf16[4,48,768]{2,1,0:T(8,128)(2,1)S(1)}, u32[]{:S(2)}, u32[]{:S(2)}) collective-permute-start(bf16[4,48,768]{2,1,0:T(8,128)(2,1)S(1)} %get-tuple-element.132), channel_id=1, source_target_pairs={{0,4},{4,0},{1,5},{5,1},{2,6},{6,2},{3,7},{7,3},{8,12},{12,8},{9,1... | collective-permute-start | bytes 884744 | tf_op jit(solution)/shard_map/ppermute | solution.py:68
  268.4 18.1 %collective-permute-start.27 = (bf16[2,48,768]{2,1,0:T(8,128)(2,1)S(1)}, bf16[2,48,768]{2,1,0:T(8,128)(2,1)S(1)}, u32[]{:S(2)}, u32[]{:S(2)}) collective-permute-start(bf16[2,48,768]{2,1,0:T(8,128)(2,1)S(1)} %get-tuple-element.137), channel_id=1, source_target_pairs={{0,8},{8,0},{16,24},{24,16},{1,9},{9,1},{17,25},{25,17},{2,10},{10... | collective-permute-start | bytes 442376 | tf_op jit(solution)/shard_map/ppermute | solution.py:68
  268.5 18.1 %collective-permute-start.28 = (bf16[2,48,768]{2,1,0:T(8,128)(2,1)S(1)}, bf16[2,48,768]{2,1,0:T(8,128)(2,1)S(1)}, u32[]{:S(2)}, u32[]{:S(2)}) collective-permute-start(bf16[2,48,768]{2,1,0:T(8,128)(2,1)S(1)} %get-tuple-element.138), channel_id=1, source_target_pairs={{0,16},{8,24},{16,0},{24,8},{1,17},{9,25},{17,1},{25,9},{2,18},{10... | collective-permute-start | bytes 442376 | tf_op jit(solution)/shard_map/ppermute | solution.py:68
  270.7 15.9 %collective-permute-start.29 = (bf16[2,48,768]{2,1,0:T(8,128)(2,1)S(1)}, bf16[2,48,768]{2,1,0:T(8,128)(2,1)S(1)}, u32[]{:S(2)}, u32[]{:S(2)}) collective-permute-start(bf16[2,48,768]{2,1,0:T(8,128)(2,1)S(1)} %get-tuple-element.139), channel_id=1, source_target_pairs={{0,24},{8,16},{16,8},{24,0},{1,25},{9,17},{17,9},{25,1},{2,26},{10... | collective-permute-start | bytes 442376 | tf_op jit(solution)/shard_map/ppermute | solution.py:68
  283.7 16.1 %collective-permute-start.23 = (bf16[2,4,48,768]{3,2,1,0:T(8,128)(2,1)}, bf16[2,4,48,768]{3,2,1,0:T(8,128)(2,1)S(1)}, u32[]{:S(2)}, u32[]{:S(2)}) collective-permute-start(bf16[2,4,48,768]{3,2,1,0:T(8,128)(2,1)} %get-tuple-element.142), channel_id=1, source_target_pairs={{0,2},{2,0},{1,3},{3,1},{4,6},{6,4},{5,7},{7,5},{8,10},{10,8},{9,1... | collective-permute-start | bytes 1769480 | tf_op jit(solution)/shard_map/ppermute | solution.py:68
  291.3 64.3 %collective-permute-start.30 = (bf16[1024,768]{1,0:T(8,128)(2,1)}, bf16[1024,768]{1,0:T(8,128)(2,1)}, u32[]{:S(2)}, u32[]{:S(2)}) collective-permute-start(bf16[1024,768]{1,0:T(8,128)(2,1)} %input_grad_part.2), channel_id=1, source_target_pairs={{0,1},{1,0},{2,3},{3,2},{4,5},{5,4},{6,7},{7,6},{8,9},{9,8},{10,11... | collective-permute-start | bytes 4718600 | tf_op jit(solution)/shard_map/ppermute | solution.py:68
  291.7 36.1 %collective-permute-start.42 = (bf16[2,48,768]{2,1,0:T(8,128)(2,1)S(1)}, bf16[2,48,768]{2,1,0:T(8,128)(2,1)}, u32[]{:S(2)}, u32[]{:S(2)}) collective-permute-start(bf16[2,48,768]{2,1,0:T(8,128)(2,1)S(1)} %get-tuple-element.148), channel_id=1, source_target_pairs={{0,8},{8,0},{16,24},{24,16},{1,9},{9,1},{17,25},{25,17},{2,10},{10... | collective-permute-start | bytes 442376 | tf_op jit(solution)/shard_map/ppermute | solution.py:68
  302.9 33.7 %collective-permute-start.31 = (bf16[4,48,768]{2,1,0:T(8,128)(2,1)}, bf16[4,48,768]{2,1,0:T(8,128)(2,1)S(1)}, u32[]{:S(2)}, u32[]{:S(2)}) collective-permute-start(bf16[4,48,768]{2,1,0:T(8,128)(2,1)} %get-tuple-element.158), channel_id=1, source_target_pairs={{0,4},{4,0},{1,5},{5,1},{2,6},{6,2},{3,7},{7,3},{8,12},{12,8},{9,1... | collective-permute-start | bytes 884744 | tf_op jit(solution)/shard_map/ppermute | solution.py:68
  303.3 33.3 %collective-permute-start.32 = (bf16[4,48,768]{2,1,0:T(8,128)(2,1)}, bf16[4,48,768]{2,1,0:T(8,128)(2,1)}, u32[]{:S(2)}, u32[]{:S(2)}) collective-permute-start(bf16[4,48,768]{2,1,0:T(8,128)(2,1)} %get-tuple-element.159), channel_id=1, source_target_pairs={{0,2},{2,0},{1,3},{3,1},{4,6},{6,4},{5,7},{7,5},{8,10},{10,8},{9,1... | collective-permute-start | bytes 884744 | tf_op jit(solution)/shard_map/ppermute | solution.py:68
  (68 other events, 875.0 us)
Sparse Core Ops, SparseCore 0:
  11.5 93.2 all-gather.2

commit v3 on v2

v3 whole, which is shorter than its diff:
```python
from functools import partial

import jax
import jax.numpy as jnp
from jax import lax
from jax.experimental import pallas as pl
from jax.experimental.pallas import tpu as pltpu
from jax.sharding import Mesh
from jax.sharding import PartitionSpec as P

HEAD_DIM = 64
PAIR = 2 * HEAD_DIM
EPSILON = 1e-12
MASKED = -1e30
BLOCK = 256
ROW_BLOCK = 256
F32 = jnp.float32
BF16 = jnp.bfloat16
MIB = 1 << 20
COST = 1


def dot_nn(left, right):
    return jnp.dot(left, right, preferred_element_type=F32)


def dot_nt(left, right):
    return lax.dot_general(left, right, (((1,), (1,)), ((), ())), preferred_element_type=F32)


def call(body, outs, ins, in_specs=None, out_specs=None, scratch=(), grid=(), flops=0, name=None, vmem=60, alias=None):
    moved = sum(a.size * a.dtype.itemsize for a in ins) + sum(o.size * o.dtype.itemsize for o in outs)
    return pl.pallas_call(
        body,
        grid=grid,
        out_shape=outs,
        in_specs=in_specs or [VMEM] * len(ins),
        out_specs=out_specs or [VMEM] * len(outs),
        scratch_shapes=list(scratch),
        compiler_params=pltpu.CompilerParams(vmem_limit_bytes=vmem * MIB),
        cost_estimate=pl.CostEstimate(flops=int(flops) // COST, bytes_accessed=int(moved) // COST, transcendentals=0),
        input_output_aliases=alias or {},
        name=name,
    )(*ins)


ANY = pl.BlockSpec(memory_space=pl.ANY)
SMEM = pl.BlockSpec(memory_space=pltpu.SMEM)
VMEM = pl.BlockSpec(memory_space=pltpu.VMEM)


def shape_of(shape, dtype):
    return jax.ShapeDtypeStruct(shape, dtype)


def after(values, done):
    return lax.optimization_barrier((values, done))[0]


class Grid:
    def __init__(self, mesh):
        n_dp, n_tensor = mesh.devices.shape
        assert n_tensor == 4 and n_dp % 2 == 0
        self.nz = n_dp // 2
        self.n_dp = n_dp
        self.mesh = Mesh(mesh.devices.reshape(self.nz, 2, 2, 2), ("z", "y", "x", "c"))

    def swap(self, array, axis, r=1):
        size = self.nz if axis == "z" else 2
        return lax.ppermute(array, axis, [(i, i ^ r) for i in range(size)])

    def regular(self, rows):
        return rows % 32 == 0 and self.nz & (self.nz - 1) == 0

    def total_dp(self, array):
        if self.nz & (self.nz - 1):
            return lax.psum(array, ("z", "y"))
        array = array + self.swap(array, "y")
        r = 1
        while r < self.nz:
            array = array + self.swap(array, "z", r)
            r *= 2
        return array


class Gather:
    def __init__(self, g, shard):
        self.g, self.shard, self.rows = g, shard, shard.shape[0]
        self.regular = g.regular(self.rows)

    def line(self):
        g, half = self.g, self.rows // 2
        if not self.regular:
            full = lax.all_gather(self.shard, ("z", "y"), axis=0, tiled=True)[None, None]
            self.arrays = [full, g.swap(full, "x")]
            self.entries = [(n, 0, 0, n, 0, 0, full.shape[2]) for n in range(2)]
            return self.arrays
        near = [self.shard] + [g.swap(self.shard, "z", r) for r in range(1, g.nz)]
        self.lines = [jnp.stack([part[:half] for part in near]), jnp.stack([part[half:] for part in near])]
        return self.lines

    def wait(self, step, done):
        if self.regular:
            setattr(self, step, after(getattr(self, step), done))

    def first(self, done=()):
        if not self.regular:
            return self.arrays
        arrived = after([self.g.swap(line, axis) for line, axis in zip(self.lines, "xy")], done)
        self.twos = [jnp.stack([line, other]) for line, other in zip(self.lines, arrived)]
        return arrived

    def second(self):
        if not self.regular:
            return self.arrays
        half = self.rows // 2
        self.arrays, self.entries = [], []
        for number, axis in enumerate("xy"):
            two = self.twos[number]
            four = self.g.swap(two, "yx"[number])
            for index, array in ((0, two), (1, four)):
                for i in range(2):
                    rx, ry = (i, index) if axis == "x" else (index, i)
                    for k in range(self.g.nz):
                        self.entries.append((len(self.arrays), i, k, rx, k * 2 + ry, number * half, half))
                self.arrays.append(array)
        return self.arrays


def load_pieces(entries, refs, index, target, sems, lanes):
    slots = 1 + max(entry[4] for entry in entries)
    copies = []
    for number, (a, i, k, place, slot, first, size) in enumerate(entries):
        row = pl.multiple_of((slot ^ index) * (target.shape[1] // slots) + first, 16)
        copies.append(
            pltpu.make_async_copy(refs[a].at[i, k, :, lanes], target.at[place, pl.ds(row, size)], sems.at[number])
        )
    for copy in copies:
        copy.start()
    for copy in copies:
        copy.wait()


def gather_everywhere(g, shard):
    if g.regular(shard.shape[0]):
        full = lax.all_gather(shard, ("z", "y", "x", "c"), axis=0)
        return full.reshape(g.n_dp, 4, *shard.shape)
    full = lax.all_gather(shard, ("z", "y"), axis=0, tiled=True)
    return lax.all_gather(full, ("x", "c"), axis=0)[None]


def everywhere_copies(source, me, target, sems, lanes):
    blocks, places, rows = source.shape[:3]
    return [
        pltpu.make_async_copy(
            source.at[block, t, :, lanes],
            target.at[t ^ me, pl.ds(block * rows, rows)],
            sems.at[block * places + t],
        )
        for block in range(blocks)
        for t in range(places)
    ]


SPARE = 16


class Scatter:
    def __init__(self, g, rows, arrays, vector=None):
        self.g, self.rows = g, rows
        self.regular = g.regular(rows)
        self.arrays = arrays
        self.vector = vector

    @staticmethod
    def shapes(g, rows, lanes, spare=0, weights=None):
        lead = () if weights is None else (weights,)
        if not g.regular(rows):
            return [shape_of((*lead, 2, rows * g.n_dp, lanes), BF16)]
        size = 2 * g.nz * rows // 2
        block = shape_of((*lead, size, lanes), BF16)
        return [block, shape_of((*lead, size + spare, lanes), BF16), block, block]

    def first(self, done=()):
        g = self.g
        if not self.regular:
            (whole,) = self.arrays
            both = whole[..., 0, :, :].astype(F32) + g.swap(whole[..., 1, :, :], "x").astype(F32)
            self.sum = lax.psum_scatter(both, ("z", "y"), scatter_dimension=both.ndim - 2, tiled=True)
            if self.vector is not None:
                self.vector = lax.psum(self.vector[0] + g.swap(self.vector[1], "x"), ("z", "y"))
            return [self.sum]
        keep_x, send_x, keep_y, send_y = self.arrays
        self.got = after([g.swap(send_x, "x"), g.swap(send_y, "y")], done)
        lead, half, lanes = keep_x.shape[:-2], keep_x.shape[-2] // 2, keep_x.shape[-1]
        outs, ins = [shape_of((*lead, half, lanes), BF16)] * 2, [keep_x, self.got[0], keep_y, self.got[1]]
        if self.vector is not None:
            outs = [shape_of((half + SPARE, lanes), BF16), outs[1], shape_of((SPARE // 2, lanes), F32)]
            ins.append(self.vector[0])
        self.away = call(sum_away, outs, ins, name="sum_away", vmem=SUM_VMEM)
        return self.away

    def second(self, done=()):
        if not self.regular:
            return [self.sum]
        g = self.g
        seconds = after([g.swap(self.away[0], "y"), g.swap(self.away[1], "x")], done)
        lead, lanes = self.away[1].shape[:-2], self.away[1].shape[-1]
        outs = [shape_of((*lead, self.rows, lanes), F32)]
        ins = [self.arrays[0], self.got[0], seconds[0], self.arrays[2], self.got[1], seconds[1]]
        far_rows = self.rows
        if self.vector is not None:
            outs.append(shape_of((SPARE // 2, lanes), F32))
            ins.append(self.away[2])
            far_rows += SPARE
        outs += [shape_of((*lead, far_rows, lanes), BF16)] * (g.nz - 1)
        self.line = call(partial(sum_line, g.nz), outs, ins, name="sum_line", vmem=SUM_VMEM)
        return self.line

    def third(self, done=()):
        if not self.regular:
            return [self.sum] if self.vector is None else [self.sum, self.vector]
        count = 1 if self.vector is None else 2
        arrived = [self.g.swap(far, "z", r + 1) for r, far in enumerate(self.line[count:])]
        return [*self.line[:count], *after(arrived, done)]


SUM_VMEM = 12
VM_HEADS = 60
VM_ROWS = 60
VM_GRAD = 40
VM_BACK = 36
VM_PROJ = 36


def split_in_two(value):
    high = value.astype(BF16)
    return jnp.concatenate([high, (value - high.astype(F32)).astype(BF16)], axis=0)


def join_two(ref):
    spare = ref[ref.shape[0] - SPARE :, :].astype(F32)
    return spare[: SPARE // 2] + spare[SPARE // 2 :]


def sum_away(keep_x, got_x, keep_y, got_y, *refs):
    half = keep_x.shape[-2] // 2
    if len(refs) == 4:
        vector, out_x, out_y, vector_out = refs
        total = vector[...] + join_two(got_x)
        vector_out[...] = total
        out_x[half:, :] = split_in_two(total)
    else:
        out_x, out_y = refs
    for keep, got, out in ((keep_x, got_x, out_x), (keep_y, got_y, out_y)):
        away = keep[..., half:, :].astype(F32) + got[..., half : 2 * half, :].astype(F32)
        out[..., :half, :] = away.astype(BF16)


def sum_line(nz, keep_x, got_x, last_x, keep_y, got_y, last_y, *refs):
    size = keep_x.shape[-2] // (2 * nz)
    if len(refs) > nz:
        vector, near, vector_out, *far = refs
        total = vector[...] + join_two(last_x)
        vector_out[...] = total
        parts = split_in_two(total)
        for out in far:
            out[2 * size :, :] = parts
    else:
        near, *far = refs
    for n, (keep, got, last) in enumerate(((keep_x, got_x, last_x), (keep_y, got_y, last_y))):
        for r in range(nz):
            at = slice(r * size, (r + 1) * size)
            total = keep[..., at, :].astype(F32) + got[..., at, :].astype(F32) + last[..., at, :].astype(F32)
            out = far[r - 1] if r else near
            out[..., n * size : (n + 1) * size, :] = total.astype(out.dtype)


def store_blocks(value, outs, stage, place, index, nz):
    value = value.astype(BF16)
    if len(outs) == 1:
        outs[0][place] = value
        return
    by_x = outs[place]
    half = stage.shape[1] // (2 * nz)
    for block in range(value.shape[0] // (2 * half)):
        slot = block ^ index
        ry, rz = lax.rem(slot, 2), lax.div(slot, 2)
        row = pl.multiple_of((ry * nz + rz) * half, 16)
        by_x[pl.ds(row, half), :] = value[2 * block * half : (2 * block + 1) * half]
        row = pl.multiple_of((place * nz + rz) * half, 16)
        stage[ry, pl.ds(row, half), :] = value[(2 * block + 1) * half : (2 * block + 2) * half]
    if place == 1:
        outs[2][...] = stage[0]
        outs[3][...] = stage[1]


SUMMED = HEAD_DIM + 16


def heads_forward(entries, count, meta, lows, highs, *refs):
    pieces = refs[:count]
    own, other, bias, seg_row = refs[count : count + 4]
    q, k, v, w_out, ctx_own, ctx_other, lse = refs[count + 4 : count + 11]
    weights, v_t, q_masked, powers, seg_col, sems = refs[count + 11 :]
    rows = own.shape[0]
    core = meta[0]
    load_pieces(entries, pieces, meta[1], weights, sems, slice(None))
    d = HEAD_DIM
    width = q.shape[1]
    pairs = width // PAIR
    for j in range(pairs):
        for kind in range(3):
            at = slice((3 * j + kind) * d, (3 * j + kind + 1) * d)
            pair = jnp.concatenate([weights[0][:, at], weights[1][:, at]], axis=1)
            w_out[:, kind * width + j * PAIR : kind * width + (j + 1) * PAIR] = pair
    ones = jnp.ones((SUMMED - d, BLOCK), BF16)
    for source, base in ((own, core * rows), (other, (1 - core) * rows)):

        def project(n, carry):
            at = pl.ds(pl.multiple_of(base + n * BLOCK, BLOCK), BLOCK)
            block = source[pl.ds(pl.multiple_of(n * BLOCK, BLOCK), BLOCK), :]
            all_three = dot_nn(block, w_out[...])
            query = (all_three[:, :width] + bias[0:1, :]).astype(BF16)
            q[at, :] = (query.astype(F32) * d**-0.5).astype(BF16)
            k[at, :] = all_three[:, width : 2 * width].astype(BF16)
            values = (all_three[:, 2 * width :] + bias[1:2, :]).astype(BF16)
            v[at, :] = values
            for p in range(pairs):
                columns = values[:, p * PAIR : (p + 1) * PAIR].T
                for h in range(2):
                    v_t[2 * p + h, :d, at] = columns[h * d : (h + 1) * d]
                    v_t[2 * p + h, d:, at] = ones
            return carry

        lax.fori_loop(0, rows // BLOCK, project, 0)
    left = lax.broadcasted_iota(jnp.int32, (BLOCK, PAIR), 1) < d
    half = rows // BLOCK
    for b in range(2 * half):
        seg_col[b * BLOCK : (b + 1) * BLOCK, :] = column_of(seg_row[b])

    def query_block(i, carry):
        at = pl.ds(pl.multiple_of(i * BLOCK, BLOCK), BLOCK)
        seg_q = seg_row[i]
        for p in range(pairs):
            query = q[at, p * PAIR : (p + 1) * PAIR].astype(F32)
            q_masked[2 * p] = jnp.where(left, query, 0.0).astype(BF16)
            q_masked[2 * p + 1] = jnp.where(left, 0.0, query).astype(BF16)

        def key_block(b, carry):
            tops, sums = carry
            rows = pl.ds(pl.multiple_of(b * BLOCK, BLOCK), BLOCK)
            same = seg_col[rows, :] == seg_q
            new_tops, new_sums = [], []
            for h in range(2 * pairs):
                s = dot_nt(k[rows, (h // 2) * PAIR : (h // 2 + 1) * PAIR], q_masked[h])
                s = jnp.where(same, s, MASKED)
                top = jnp.maximum(tops[h], jnp.max(s, axis=0, keepdims=True))
                powers[h] = jnp.exp(s - top).astype(BF16)
                new_tops.append(top)
            for h in range(2 * pairs):
                scale = jnp.exp(tops[h] - new_tops[h])
                new_sums.append(sums[h] * scale + dot_nn(v_t[h, :, rows], powers[h]))
            return tuple(new_tops), tuple(new_sums)

        first_top = jnp.full((1, BLOCK), MASKED, F32)
        first_sum = jnp.zeros((SUMMED, BLOCK), F32)
        tops, sums = lax.fori_loop(
            lows[i], highs[i], key_block, ((first_top,) * (2 * pairs), (first_sum,) * (2 * pairs))
        )
        for p in range(pairs):
            parts = []
            for h in (2 * p, 2 * p + 1):
                total = sums[h][d : d + 1, :]
                lse[i, h : h + 1, :] = tops[h] + jnp.log(total)
                parts.append(sums[h][:d, :] / total)
            ctx = jnp.concatenate(parts, axis=0).T.astype(BF16)
            lanes = slice(p * PAIR, (p + 1) * PAIR)
            own_half = lax.div(i, half) == core
            within = pl.ds(pl.multiple_of(lax.rem(i, half) * BLOCK, BLOCK), BLOCK)

            @pl.when(own_half)
            def _():
                ctx_own[within, lanes] = ctx

            @pl.when(jnp.logical_not(own_half))
            def _():
                ctx_other[within, lanes] = ctx

        return carry

    lax.fori_loop(0, 2 * half, query_block, 0)


def heads_back_start(meta, da_own, da_other, ctx_own, ctx_other, wo, dctx, delta, out_grad, left_t):
    rows = da_own.shape[0]
    core = meta[0]
    d = HEAD_DIM
    pairs = ctx_own.shape[1] // PAIR
    for source, values, base in ((da_own, ctx_own, core * rows), (da_other, ctx_other, (1 - core) * rows)):

        def context_grad(n, carry):
            here = pl.ds(pl.multiple_of(n * BLOCK, BLOCK), BLOCK)
            at = pl.ds(pl.multiple_of(base + n * BLOCK, BLOCK), BLOCK)
            block = base // BLOCK + n
            left_t[:, here] = source[here, :].T
            grads = dot_nn(source[here, :], wo[...]).astype(BF16)
            dctx[at, :] = grads
            for p in range(pairs):
                lanes = slice(p * PAIR, (p + 1) * PAIR)
                prod = (grads[:, lanes].astype(F32) * values[here, lanes].astype(F32)).T
                delta[block, 2 * p : 2 * p + 1, :] = jnp.sum(prod[:d], axis=0, keepdims=True)
                delta[block, 2 * p + 1 : 2 * p + 2, :] = jnp.sum(prod[d:], axis=0, keepdims=True)
            return carry

        lax.fori_loop(0, rows // BLOCK, context_grad, 0)
        part = dot_nn(left_t[...], values[...])
        if source is da_own:
            out_grad[...] = part
        else:
            out_grad[...] += part


def attention_backward(first, last, given, meta, lows, highs, q, k, v, dctx, lse, delta, seg_row, *refs):
    dq_in, (dq_t, dkv, dk_sum, dv_sum, powers, slopes) = refs[:given], refs[given:]
    d = HEAD_DIM
    width = q.shape[1]
    pairs = width // PAIR
    left = lax.broadcasted_iota(jnp.int32, (BLOCK, PAIR), 1) < d
    dq_t[...] = dq_in[0][...] if given else jnp.zeros_like(dq_t)

    def key_block(b, carry):
        at = pl.ds(pl.multiple_of(b * BLOCK, BLOCK), BLOCK)
        seg_k = column_of(seg_row[b])
        dk_sum[...] = jnp.zeros_like(dk_sum)
        dv_sum[...] = jnp.zeros_like(dv_sum)
        keys, values, keys_t = [], [], []
        for p in range(pairs):
            lanes = slice(p * PAIR, (p + 1) * PAIR)
            key, value = k[at, lanes].astype(F32), v[at, lanes].astype(F32)
            keys += [jnp.where(left, key, 0.0).astype(BF16), jnp.where(left, 0.0, key).astype(BF16)]
            values += [jnp.where(left, value, 0.0).astype(BF16), jnp.where(left, 0.0, value).astype(BF16)]
            keys_t.append(k[at, lanes].T)

        def query_block(i, carry):
            rows_q = pl.ds(pl.multiple_of(i * BLOCK, BLOCK), BLOCK)
            same = seg_k == seg_row[i]
            for h in range(2 * pairs):
                lanes = slice((h // 2) * PAIR, (h // 2 + 1) * PAIR)
                s = jnp.where(same, dot_nt(keys[h], q[rows_q, lanes]), MASKED)
                p = jnp.exp(s - lse[i, h : h + 1, :])
                dp = dot_nt(values[h], dctx[rows_q, lanes])
                powers[h] = p.astype(BF16)
                slopes[h] = (p * (dp - delta[i, h : h + 1, :])).astype(BF16)
            for h in range(2 * pairs):
                p, half = h // 2, slice((h % 2) * d, (h % 2 + 1) * d)
                lanes = slice(p * PAIR, (p + 1) * PAIR)
                dv_sum[h] += dot_nn(powers[h], dctx[rows_q, lanes])
                dk_sum[h] += dot_nn(slopes[h], q[rows_q, lanes])
                dq_t[p, half, rows_q] += dot_nn(keys_t[p][half, :], slopes[h])
            return carry

        lax.fori_loop(lows[b], highs[b], query_block, 0)
        for p in range(pairs):
            for n, total in ((1, dk_sum), (2, dv_sum)):
                value = jnp.where(left, total[2 * p], total[2 * p + 1])
                here = pl.ds(pl.multiple_of((b - first) * BLOCK, BLOCK), BLOCK)
                dkv[here, (n - 1) * width + p * PAIR : (n - 1) * width + (p + 1) * PAIR] = value.astype(BF16)
        return carry

    lax.fori_loop(first, last, key_block, 0)


def column_of(row):
    return jnp.broadcast_to(row.astype(F32), (128, BLOCK)).T[:, 0:1].astype(jnp.int32)


def transpose_tokens(meta, own, other, out):
    rows = own.shape[0]
    for base, source in ((meta[0] * rows, own), ((1 - meta[0]) * rows, other)):
        for r in range(0, rows, BLOCK):
            out[:, pl.ds(pl.multiple_of(base + r, BLOCK), BLOCK)] = source[r : r + BLOCK, :].T


def projection_grad(nz, meta, token_t, out_grad, dq_t, dkv_one, dkv_two, vector, *refs):
    outs, dqkv, stage = refs[:-2], refs[-2], refs[-1]
    d = HEAD_DIM
    seq = token_t.shape[1]
    width = out_grad.shape[1]

    def join(n, total):
        at = pl.ds(pl.multiple_of(n * BLOCK, BLOCK), BLOCK)
        for p in range(width // PAIR):
            dqkv[at, p * PAIR : (p + 1) * PAIR] = (dq_t[p, :, at].T * d**-0.5).astype(BF16)
        return total + column_sum(dqkv[at, :width].astype(F32))

    dqkv[: seq // 2, width:] = dkv_one[...]
    dqkv[seq // 2 :, width:] = dkv_two[...]
    q_sum = lax.fori_loop(0, seq // BLOCK, join, jnp.zeros((1, width), F32))
    v_sum = column_sum(dkv_one[:, width:].astype(F32)) + column_sum(dkv_two[:, width:].astype(F32))
    full = dot_nn(token_t[...], dqkv[...])
    vectors = []
    for place in range(2):
        lanes, biases = [], []
        for j in range(width // PAIR):
            at = j * PAIR + place * d
            lanes += [full[:, n * width + at : n * width + at + d] for n in range(3)] + [out_grad[:, at : at + d]]
        store_blocks(jnp.concatenate(lanes, axis=1), outs[:-1], stage, place, meta[1], nz)
        for total in (q_sum, v_sum):
            biases += [total[:, j * PAIR + place * d : j * PAIR + (place + 1) * d] for j in range(width // PAIR)]
        biases.append(jnp.zeros((1, vector.shape[2] - len(biases) * d), F32))
        vectors.append(jnp.concatenate([vector[place], jnp.concatenate(biases, axis=1)], axis=0))
    outs[-1][0] = vectors[0]
    outs[-1][1] = vectors[1]
    if len(outs) > 2:
        outs[1][outs[0].shape[0] :, :] = split_in_two(vectors[1])


def input_grad_other(meta, dqkv, w, out):
    rows = out.shape[0]
    base = (1 - meta[0]) * rows
    for r in range(0, rows, BLOCK):
        at = pl.ds(pl.multiple_of(base + r, BLOCK), BLOCK)
        out[r : r + BLOCK, :] = dot_nt(dqkv[at, :], w[...]).astype(BF16)


def input_grad_own(meta, dqkv, w, dr1, arrived, out):
    rows = out.shape[0]
    base = meta[0] * rows
    for r in range(0, rows, BLOCK):
        at = pl.ds(pl.multiple_of(base + r, BLOCK), BLOCK)
        here = slice(r, r + BLOCK)
        out[here, :] = dot_nt(dqkv[at, :], w[...]) + dr1[here, :] + arrived[here, :].astype(F32)


def finish_heads(count, near, vector, *refs):
    arrived, (qkv_out, out_out, vector_out) = refs[:count], refs[count:]
    total, sums = near[...], vector[...]
    rows = total.shape[0]
    for part in arrived:
        total = total + part[:rows, :].astype(F32)
        sums = sums + join_two(part)
    d = HEAD_DIM
    heads = total.shape[1] // (4 * d)
    for kind in range(4):
        value = jnp.concatenate([total[:, (4 * j + kind) * d : (4 * j + kind + 1) * d] for j in range(heads)], axis=1)
        if kind == 3:
            out_out[...] = value
        else:
            qkv_out[kind] = value
    vector_out[...] = sums


def normalize(values):
    center = jnp.mean(values, axis=-1, keepdims=True)
    offset = values - center
    inverse = lax.rsqrt(jnp.mean(offset * offset, axis=-1, keepdims=True) + EPSILON)
    return offset * inverse, inverse


def normalize_back(incoming, normed, inverse, gain):
    weighted = incoming * gain
    centered = weighted - jnp.mean(weighted, axis=-1, keepdims=True)
    centered = centered - normed * jnp.mean(weighted * normed, axis=-1, keepdims=True)
    return centered * inverse


def column_sum(values):
    return jnp.sum(values, axis=0, keepdims=True)


def rows_step(
    meta, everywhere, tokens, vectors, ctx_own, ctx_other, bias, out_grad,
    output, dr1_out, da_out, act_out, du_out, df_t, low_t, sums, bias_sums, wo_own,
    w_out, w_all, slope, sems,
):
    hidden = tokens.shape[1]
    half = ctx_own.shape[1]
    copies = everywhere_copies(everywhere, meta[2], w_all, sems, slice(None))
    w_up = w_all.at[:, :, :hidden]
    w_down = w_all.at[:, :, hidden : 2 * hidden]
    start = pl.program_id(0) == 0

    @pl.when(start)
    def _():
        for copy in copies:
            copy.start()
        for copy in copies:
            copy.wait()
        d = HEAD_DIM
        for core in range(2):
            for j in range(half // PAIR):
                first = 2 * hidden + j * d
                pair = [w_all[2 * place + core, :, first : first + d] for place in range(2)]
                at = core * half + j * PAIR
                w_out[:, at : at + PAIR] = jnp.concatenate(pair, axis=1)
        wo_own[...] = w_out[:, :half]
        sums[...] = jnp.zeros_like(sums)
        bias_sums[...] = jnp.zeros_like(bias_sums)

    out_bias, gain_one, shift_one, down_bias, gain_two, shift_two = (vectors[n : n + 1, :] for n in range(6))
    mixed = dot_nt(jnp.concatenate([ctx_own[...], ctx_other[...]], axis=1), w_out[...])
    normed_one, inverse_one = normalize(tokens[...].astype(F32) + mixed + out_bias)
    first = normed_one * gain_one + shift_one
    low = first.astype(BF16)
    low_t[...] = low.T

    for t in range(4):
        for n in range(0, hidden, BLOCK):
            at = slice(t * hidden + n, t * hidden + n + BLOCK)
            u = dot_nn(low, w_up[t, :, n : n + BLOCK]) + bias[:, at]
            share = 0.5 + 0.5 * lax.erf(u * 0.5**0.5)
            act_out[:, at] = (u * share).astype(BF16)
            slope[:, at] = share + u * (jnp.exp(-0.5 * u * u) * 0.3989422804014327)

    fed = first + down_bias
    for t in range(4):
        fed = fed + dot_nt(act_out[:, t * hidden : (t + 1) * hidden], w_down[t])
    normed, inverse = normalize(fed)
    output[...] = (normed * gain_two + shift_two).astype(BF16)
    incoming = out_grad[...].astype(F32)
    dr2 = normalize_back(incoming, normed, inverse, gain_two)
    df = dr2.astype(BF16)
    df_t[...] = df.T
    sums[3:4, :] += column_sum(df.astype(F32))
    sums[4:5, :] += column_sum(incoming * normed)
    sums[5:6, :] += column_sum(incoming)
    for t in range(4):
        for n in range(0, hidden, BLOCK):
            at = slice(t * hidden + n, t * hidden + n + BLOCK)
            du = (dot_nn(df, w_down[t, :, n : n + BLOCK]) * slope[:, at]).astype(BF16)
            du_out[:, at] = du
            bias_sums[0:1, at] += column_sum(du.astype(F32))
    incoming = dr2
    for t in range(4):
        incoming = incoming + dot_nt(du_out[:, t * hidden : (t + 1) * hidden], w_up[t])
    dr1 = normalize_back(incoming, normed_one, inverse_one, gain_one)
    dr1_out[...] = dr1
    da = dr1.astype(BF16)
    da_out[...] = da
    sums[0:1, :] += column_sum(da.astype(F32))
    sums[1:2, :] += column_sum(incoming * normed_one)
    sums[2:3, :] += column_sum(incoming)


def grad_for_partner(df_t, low_t, act_one, act_two, du_one, du_two, out_one, out_two):
    for out, act, du in ((out_one, act_one, du_one), (out_two, act_two, du_two)):
        out[0] = dot_nn(df_t[...], act[...]).astype(BF16)
        out[1] = dot_nn(low_t[...], du[...]).astype(BF16)


def grad_for_chip(nz, meta, df_t, low_t, act_one, act_two, du_one, du_two, received_one, received_two, *refs):
    outs, stage = refs[:-1], refs[-1]
    for n, left_t, rights in ((0, df_t, (act_one, act_two)), (1, low_t, (du_one, du_two))):
        for place, received in ((0, received_one), (1, received_two)):
            value = dot_nn(left_t[...], rights[place][...]) + received[n].astype(F32)
            store_blocks(value, [out.at[n] for out in outs], stage.at[n], place, meta[1], nz)


def local(
    g,
    tokens,
    segment_ids,
    qkv_weight,
    qv_bias,
    out_weight,
    out_bias,
    first_gain,
    first_shift,
    up_weight,
    up_bias,
    down_weight,
    down_bias,
    second_gain,
    second_shift,
    output_grad,
):
    rows, width = tokens.shape
    seq = segment_ids.shape[1]
    heads = qkv_weight.shape[2] // HEAD_DIM
    hidden = up_weight.shape[1]
    shard = qkv_weight.shape[0]
    assert seq == 2 * rows and rows % BLOCK == 0 and hidden == width
    d = HEAD_DIM
    local_width = heads * d
    z, y, x, c = (lax.axis_index(name) for name in ("z", "y", "x", "c"))
    regular = g.regular(shard)
    meta = jnp.stack([c, (z * 2 + y) if regular else c * 0, x * 2 + c]).astype(jnp.int32)

    segments = lax.dynamic_index_in_dim(segment_ids, x, 0, keepdims=False)
    blocks = seq // BLOCK
    by_block = segments.reshape(blocks, BLOCK)
    lows = jnp.sum((segments[None, :] < by_block[:, :1]).astype(jnp.int32), axis=1) // BLOCK
    highs = (jnp.sum((segments[None, :] <= by_block[:, -1:]).astype(jnp.int32), axis=1) + BLOCK - 1) // BLOCK
    seg_row = segments.reshape(blocks, 1, BLOCK)

    small = jnp.concatenate([up_bias, qv_bias.reshape(-1)]).reshape(1, -1)
    small = jnp.concatenate([small, g.swap(small, "x")], axis=0)
    small = jnp.stack([small, g.swap(small, "c")], axis=1).reshape(4, -1).astype(F32)
    hidden_bias = small[:, :hidden].reshape(1, 4 * hidden)
    pair_bias = small[:, hidden:].reshape(2, 2, 2, heads, d)[:, 0].transpose(1, 2, 0, 3)
    pair_bias = pair_bias.reshape(2, heads * PAIR)
    vectors = jnp.stack(
        [out_bias, first_gain, first_shift, down_bias, second_gain, second_shift, out_bias, out_bias]
    ).astype(F32)

    parts = []
    for j in range(heads):
        at = slice(j * d, (j + 1) * d)
        parts += [qkv_weight[:, n, at] for n in range(3)]
    parts.append(jnp.zeros((shard, -3 * local_width % 128), BF16))
    head_weights = Gather(g, jnp.concatenate(parts, axis=1))
    rest = jnp.zeros((shard, -local_width % 128), BF16)
    rest = jnp.concatenate([up_weight, after(down_weight, head_weights.shard), out_weight, rest], axis=1)
    both = gather_everywhere(g, rest)
    other_tokens = g.swap(tokens, "c")
    head_weights.line()
    head_weights.wait("lines", small)
    (token_t,) = call(
        transpose_tokens,
        [shape_of((width, seq), BF16)],
        [meta, tokens, other_tokens],
        in_specs=[SMEM, VMEM, VMEM],
        name="transpose_tokens",
        vmem=16,
    )
    head_weights.first(token_t)
    head_weights.second()

    lanes = heads * PAIR
    blocks = seq // BLOCK
    count = len(head_weights.arrays)
    q, k, v, w, ctx_own, ctx_send, lse = call(
        partial(heads_forward, head_weights.entries, count),
        [shape_of((seq, lanes), BF16)] * 3
        + [shape_of((width, 3 * lanes), BF16)]
        + [shape_of((rows, lanes), BF16)] * 2
        + [shape_of((blocks, 8, BLOCK), F32)],
        [meta, lows, highs, *head_weights.arrays, tokens, other_tokens, pair_bias, seg_row],
        in_specs=[SMEM] * 3 + [ANY] * count + [VMEM] * 4,
        scratch=[
            pltpu.VMEM((2, width, head_weights.shard.shape[1]), BF16),
            pltpu.VMEM((2 * heads, SUMMED, seq), BF16),
            pltpu.VMEM((2 * heads, BLOCK, PAIR), BF16),
            pltpu.VMEM((2 * heads, BLOCK, BLOCK), BF16),
            pltpu.VMEM((seq, 1), jnp.int32),
            pltpu.SemaphoreType.DMA((len(head_weights.entries),)),
        ],
        flops=2 * seq * width * 3 * lanes + 4 * seq * seq * lanes,
        name="heads_forward",
        vmem=VM_HEADS,
    )
    ctx_other = g.swap(ctx_send, "c")

    def by_rows(lanes):
        return pl.BlockSpec((ROW_BLOCK, lanes), lambda i: (i, 0))

    def by_columns(array_rows):
        return pl.BlockSpec((array_rows, ROW_BLOCK), lambda i: (0, i))

    def fixed(array):
        return pl.BlockSpec(array.shape, lambda i: (0,) * len(array.shape))

    ffn = 2 * rows * width * 4 * hidden
    sums_shape = shape_of((8, width), F32)
    bias_shape = shape_of((8, 4 * hidden), F32)
    weight_sems = pltpu.SemaphoreType.DMA((both.shape[0] * both.shape[1],))
    output, dr1, da, act, du, df_t, low_t, sums_rows, hidden_sums, wo = call(
        rows_step,
        [
            shape_of((rows, width), BF16),
            shape_of((rows, width), F32),
            shape_of((rows, width), BF16),
            shape_of((rows, 4 * hidden), BF16),
            shape_of((rows, 4 * hidden), BF16),
            shape_of((width, rows), BF16),
            shape_of((width, rows), BF16),
            sums_shape,
            bias_shape,
            shape_of((width, lanes), BF16),
        ],
        [meta, both, tokens, vectors, ctx_own, ctx_other, hidden_bias, output_grad],
        in_specs=[SMEM, ANY, by_rows(width), fixed(vectors), by_rows(lanes), by_rows(lanes)]
        + [fixed(hidden_bias), by_rows(width)],
        out_specs=[by_rows(width)] * 3
        + [by_rows(4 * hidden)] * 2
        + [by_columns(width)] * 2
        + [fixed(sums_shape), fixed(bias_shape), pl.BlockSpec((width, lanes), lambda i: (0, 0))],
        scratch=[
            pltpu.VMEM((width, width), BF16),
            pltpu.VMEM((4, width, both.shape[3]), BF16),
            pltpu.VMEM((ROW_BLOCK, 4 * hidden), F32),
            weight_sems,
        ],
        grid=(rows // ROW_BLOCK,),
        flops=4 * ffn + 2 * rows * width * width,
        name="rows_step",
        vmem=VM_ROWS,
    )
    other_da = g.swap(da, "c")
    tiles = hidden // BLOCK
    left_spec = pl.BlockSpec((width, rows), lambda i: (0, 0))

    def right_specs(places):
        return [pl.BlockSpec((rows, BLOCK), lambda i, t=t: (0, t * tiles + i)) for t in places] * 2

    partner_spec = pl.BlockSpec((2, width, BLOCK), lambda i: (0, 0, i))
    for_partner = call(
        grad_for_partner,
        [shape_of((2, width, hidden), BF16)] * 2,
        [df_t, low_t, act, act, du, du],
        in_specs=[left_spec] * 2 + right_specs((1, 3)),
        out_specs=[partner_spec] * 2,
        grid=(tiles,),
        flops=ffn,
        name="grad_for_partner",
        vmem=VM_GRAD,
    )
    dctx, delta, out_grad = call(
        heads_back_start,
        [shape_of((seq, lanes), BF16), shape_of((blocks, 8, BLOCK), F32), shape_of((width, lanes), F32)],
        [meta, da, other_da, ctx_own, ctx_send, wo],
        in_specs=[SMEM] + [VMEM] * 5,
        scratch=[pltpu.VMEM((width, rows), BF16)],
        flops=4 * seq * width * lanes,
        name="heads_back_start",
        vmem=VM_PROJ,
    )
    received = [g.swap(a, "c") for a in after(for_partner, other_da)]
    leaving = Scatter.shapes(g, shard, hidden, weights=2)
    ffn_grad = Scatter(
        g,
        shard,
        call(
            partial(grad_for_chip, g.nz),
            leaving,
            [meta, after(df_t, dctx), low_t, act, act, du, du, *received],
            in_specs=[SMEM] + [left_spec] * 2 + right_specs((0, 2)) + [partner_spec] * 2,
            out_specs=[
                pl.BlockSpec((*a.shape[:-1], BLOCK), lambda i, n=len(a.shape) - 1: (0,) * n + (i,)) for a in leaving
            ],
            scratch=[pltpu.VMEM((2, 2, leaving[0].shape[-2], BLOCK), BF16)],
            grid=(tiles,),
            flops=ffn,
            name="grad_for_chip",
            vmem=VM_GRAD,
        ),
    )

    def attend_back(first, last, dctx, *dq):
        return call(
            partial(attention_backward, first, last, len(dq)),
            [shape_of((heads, PAIR, seq), F32), shape_of(((last - first) * BLOCK, 2 * lanes), BF16)],
            [meta, lows, highs, q, k, v, dctx, lse, delta, seg_row, *dq],
            in_specs=[SMEM] * 3 + [VMEM] * (7 + len(dq)),
            scratch=[pltpu.VMEM((2 * heads, BLOCK, PAIR), F32)] * 2 + [pltpu.VMEM((2 * heads, BLOCK, BLOCK), BF16)] * 2,
            flops=5 * seq * seq * lanes,
            name="attention_backward",
            vmem=VM_BACK,
        )

    dq_t, dkv_one = attend_back(0, blocks // 2, after(dctx, ffn_grad.arrays))
    ffn_away = ffn_grad.first(dkv_one)
    dq_t, dkv_two = attend_back(blocks // 2, blocks, after(dctx, ffn_away), dq_t)
    ffn_second = ffn_grad.second(dkv_two)

    six = sums_rows[:6]
    six = six + g.swap(six, "c")
    hidden_sums = hidden_sums[0].reshape(2, 2, hidden)
    hidden_sums = hidden_sums[:, 0] + g.swap(hidden_sums[:, 1], "c")
    vector = jnp.concatenate([jnp.stack([six, six]), hidden_sums[:, None]], axis=1)
    *arrays, vector, dqkv = call(
        partial(projection_grad, g.nz),
        Scatter.shapes(g, shard, 2 * lanes, SPARE) + [shape_of((2, 8, width), F32), shape_of((seq, 3 * lanes), BF16)],
        [meta, token_t, out_grad, after(dq_t, ffn_second), dkv_one, dkv_two, vector],
        in_specs=[SMEM] + [VMEM] * 6,
        scratch=[pltpu.VMEM((2, width // 2, 2 * lanes), BF16)],
        flops=2 * seq * width * 3 * lanes,
        name="projection_grad",
        vmem=VM_PROJ,
    )
    head_grad = Scatter(g, shard, arrays, (vector[0], vector[1]))
    ffn_parts = ffn_grad.third(arrays)
    ffn_share = ffn_parts[0] + sum(part.astype(F32) for part in ffn_parts[1:])
    head_away = head_grad.first(ffn_share)
    (ig_other,) = call(
        input_grad_other,
        [shape_of((rows, width), BF16)],
        [meta, after(dqkv, head_away), w],
        in_specs=[SMEM] + [VMEM] * 2,
        flops=seq * width * 3 * lanes,
        name="input_grad_other",
        vmem=VM_PROJ,
    )
    ig_arrived = g.swap(ig_other, "c")
    (input_grad,) = call(
        input_grad_own,
        [shape_of((rows, width), F32)],
        [meta, dqkv, w, dr1, ig_arrived],
        in_specs=[SMEM] + [VMEM] * 4,
        flops=seq * width * 3 * lanes,
        name="input_grad_own",
        vmem=VM_PROJ,
    )
    head_grad.second(input_grad)
    down_share, up_share = ffn_share[0], ffn_share[1]
    parts = head_grad.third()
    if regular:
        qkv_share, out_share, summed = call(
            partial(finish_heads, len(parts) - 2),
            [shape_of((3, shard, local_width), F32), shape_of((shard, local_width), F32), shape_of((8, width), F32)],
            parts,
            name="finish_heads",
            vmem=SUM_VMEM,
        )
    else:
        shares, summed = parts
        shares = shares.reshape(shard, heads, 4, d).transpose(2, 0, 1, 3).reshape(4, shard, local_width)
        qkv_share, out_share = shares[:3], shares[3]
    qkv_share = qkv_share.transpose(1, 0, 2)
    vectors_grad, up_bias_share = summed[:6], summed[6]
    qv_share = summed[7, : 2 * local_width].reshape(2, local_width)
    return (output, input_grad, qkv_share, qv_share, out_share, up_share, up_bias_share, down_share, vectors_grad)


def solution(mesh):
    g = Grid(mesh)
    dp, tensor = ("z", "y"), ("x", "c")
    rows = P(dp + tensor, None)
    in_specs = (
        rows,
        P(dp, None),
        P(dp, None, tensor),
        P(None, tensor),
        P(dp, tensor),
        P(),
        P(),
        P(),
        P(dp, tensor),
        P(tensor),
        P(dp, tensor),
        P(),
        P(),
        P(),
        rows,
    )
    out_specs = (
        rows,
        rows,
        P(dp, None, tensor),
        P(None, tensor),
        P(dp, tensor),
        P(dp, tensor),
        P(tensor),
        P(dp, tensor),
        P(),
    )
    return jax.shard_map(partial(local, g), mesh=g.mesh, in_specs=in_specs, out_specs=out_specs, check_vma=False)
```

time: 371 us -> 325 us (0.88)
  Pallas kernels: 194 us -> 165 us
  starting transfers between devices: 39.6 us -> 33.1 us
  other arithmetic: 11.2 us -> 6.23 us
    pallas_call x17 -> x16, Pallas kernels: 194 us -> 165 us  [call(): pl.pallas_call(body, grid=grid, out_shape=outs, in_specs=in_specs or [VME...]
    add x9 -> x1, other arithmetic: 7.15 us -> 0.16 us  [local(): ffn_share = ffn_parts[0] + sum((part.astype(F32) for part in ffn_parts[1:]))]
    ppermute x45 -> x31, starting transfers between devices: 39.5 us -> 33.1 us  [swap(): return lax.ppermute(array, axis, [(i, i ^ r) for i in range(size)])]
    unnamed x96 -> x99, local copies, waits for them, and re-layouts: 21 us -> 24.3 us
    ppermute x45 -> x31, waiting for transfers between devices: 71.2 us -> 68.1 us  [swap(): return lax.ppermute(array, axis, [(i, i ^ r) for i in range(size)])]
  transfers between devices with their start and end apart: 46 -> 32, of which waited for: 14 -> 14; matrix products, arithmetic and copies ran while one was open for 6% -> 4% of each run, Pallas kernels for 37% -> 36%
where the time goes in v3:
time: 325 us; the launch traced here: 323 us
  Pallas kernels  165 us (51%)
  waiting for transfers between devices  68.1 us (21%)
  local copies, waits for them, and re-layouts  35.9 us (11%)
  starting transfers between devices  33.1 us (10%)
  between operations  14.9 us (5%)
  other arithmetic  6.23 us (2%)
    pallas_call x16, Pallas kernels, call(): pl.pallas_call(body, grid=grid, out_shape=outs, in_specs=in_specs or [VME...  165 us
    ppermute x31, waiting for transfers between devices, swap(): return lax.ppermute(array, axis, [(i, i ^ r) for i in range(size)])  68.1 us
    ppermute x31, starting transfers between devices, swap(): return lax.ppermute(array, axis, [(i, i ^ r) for i in range(size)])  33.1 us
    unnamed x99, local copies, waits for them, and re-layouts  24.3 us
  transfers between devices with their start and end apart: 32, of which 14 were waited for; matrix products, arithmetic and copies ran while one was open for 4% of the time, Pallas kernels for 36%

profile of v3, /device:TPU:0, one launch (start us, length us, event | category | flops | bytes accessed | tf_op | source)
XLA Modules:
  0.0 323.2 jit_solution(2802975321441337414)
XLA Ops:
  10.3 5.1 %collective-permute-start.2 = (bf16[96,640]{1,0:T(8,128)(2,1)S(1)}, bf16[96,640]{1,0:T(8,128)(2,1)}, u32[]{:S(2)}, u32[]{:S(2)}) collective-permute-start(bf16[96,640]{1,0:T(8,128)(2,1)S(1)} %concatenate.15), channel_id=1, source_target_pairs={{0,24},{8,16},{16,8},{24,0},{1,25},{9,17},{17,9},{25,1},{2,26},{10... | collective-permute-start | bytes 368648 | tf_op jit(solution)/shard_map/ppermute | solution.py:70
  22.3 3.7 %collective-permute-done.1 = bf16[96,640]{1,0:T(8,128)(2,1)} collective-permute-done((bf16[96,640]{1,0:T(8,128)(2,1)S(1)}, bf16[96,640]{1,0:T(8,128)(2,1)}, u32[]{:S(2)}, u32[]{:S(2)}) %collective-permute-start.1) | collective-permute-done | bytes 122912 | tf_op jit(solution)/shard_map/ppermute | solution.py:70
  44.0 17.4 %collective-permute-done.9.refs_3_ = bf16[2,4,48,640]{3,2,1,0:T(8,128)(2,1)} collective-permute-done((bf16[2,4,48,640]{3,2,1,0:T(8,128)(2,1)}, bf16[2,4,48,640]{3,2,1,0:T(8,128)(2,1)}, u32[]{:S(2)}, u32[]{:S(2)}) %collective-permute-start.9) | collective-permute-done | bytes 491552 | tf_op jit(solution)/shard_map/ppermute | solution.py:70
  61.4 45.8 %heads_forward.1 = (bf16[2048,384]{1,0:T(8,128)(2,1)}, bf16[2048,384]{1,0:T(8,128)(2,1)}, bf16[2048,384]{1,0:T(8,128)(2,1)}, bf16[768,1152]{1,0:T(8,128)(2,1)}, ...) custom-call(s32[3]{0:T(128)} %copy-done.13, s32[8]{0:T(128)} %get-tuple-element.195.lows, ...), custom_call_target="tpu_custom_call" | custom-call | flops 10066329600 | bytes 13249612 | tf_op jit(solution)/shard_map/heads_forward/pallas_call | solution.py:33
  110.3 37.3 %rows_step.1 = (bf16[1024,768]{1,0:T(8,128)(2,1)}, f32[1024,768]{1,0:T(8,128)}, bf16[1024,768]{1,0:T(8,128)(2,1)}, bf16[1024,3072]{1,0:T(8,128)(2,1)}, bf16[1024...) custom-call(s32[3]{0:T(128)} %copy-done.13, ...), custom_call_target="tpu_custom_call" | custom-call | flops 20535312384 | bytes 38498316 | tf_op jit(solution)/shard_map/rows_step/pallas_call | solution.py:33
  148.0 2.8 copy-done
  153.6 8.0 %grad_for_partner.1 = (bf16[2,768,768]{2,1,0:T(8,128)(2,1)}, bf16[2,768,768]{2,1,0:T(8,128)(2,1)}) custom-call(bf16[768,1024]{1,0:T(8,128)(2,1)S(1)} %copy-done.2, bf16[768,1024]{1,0:T(8,128)(2,1)S(1)} %copy-done.4, bf16[1024,3072]{1,0:T(8,128)(2,1)S(1)} %copy-done, bf16[1024,3072]{1,0:T(8,128)(2,1)S(1)} %copy-done, ...), custom_call_target="tpu_custom_call" | custom-call | flops 4831838208 | bytes 33030144 | tf_op jit(solution)/shard_map/grad_for_partner/pallas_call | solution.py:33
  171.0 6.9 %heads_back_start.1 = (bf16[2048,384]{1,0:T(8,128)(2,1)S(1)}, f32[8,8,256]{2,1,0:T(8,128)S(1)}, f32[768,384]{1,0:T(8,128)S(1)}) custom-call(s32[3]{0:T(128)S(1)} %copy-done.14, bf16[1024,768]{1,0:T(8,128)(2,1)S(1)} %copy-done.17, bf16[1024,768]{1,0:T(8,128)(2,1)S(1)} %copy-done.19, bf16[1024,384]{1,0:T(8,128)(2,1)S(1)} %copy-done.27, ...), custom_call_target="tpu_custom_call" | custom-call | flops 2415919104 | bytes 8126476 | tf_op jit(solution)/shard_map/heads_back_start/pallas_call | solution.py:33
  179.0 8.8 %grad_for_chip.1 = (bf16[2,384,768]{2,1,0:T(8,128)(2,1)S(1)}, bf16[2,384,768]{2,1,0:T(8,128)(2,1)S(1)}, bf16[2,384,768]{2,1,0:T(8,128)(2,1)S(1)}, bf16[2,384,768]{2,1,0:T(8,128)(2,1)S(1)}) custom-call(s32[3]{0:T(128)S(1)} %copy-done.14, bf16[768,1024]{1,0:T(8,128)(2,1)S(1)} %copy-done.3, bf16[768,1024]{1,0:T(8,128)(2,1)S(1)} %copy-done.5, ...), custom_call_target="tpu_custom_call" | custom-call | flops 4831838208 | bytes 37748748 | tf_op jit(solution)/shard_map/grad_for_chip/pallas_call | solution.py:33
  189.4 19.1 %attention_backward.2 = (f32[3,128,2048]{2,1,0:T(8,128)S(1)}, bf16[1024,768]{1,0:T(8,128)(2,1)S(1)}) custom-call(s32[3]{0:T(128)S(1)} %copy-done.14, s32[8]{0:T(128)S(1)} %copy-done.16, s32[8]{0:T(128)S(1)} %copy-done.15, bf16[2048,384]{1,0:T(8,128)(2,1)S(1)} %copy-done.31, bf16[2048,384]{1,0:T(8,128)(2,1)S(1)} %copy-done.33, ...), custom_call_target="tpu_custom_call" | custom-call | flops 8053063680 | bytes 11149388 | tf_op jit(solution)/shard_map/attention_backward/pallas_call | solution.py:33
  210.2 5.7 %collective-permute-done.14.got_x = bf16[2,384,768]{2,1,0:T(8,128)(2,1)S(1)} collective-permute-done((bf16[2,384,768]{2,1,0:T(8,128)(2,1)S(1)}, bf16[2,384,768]{2,1,0:T(8,128)(2,1)S(1)}, u32[]{:S(2)}, u32[]{:S(2)}) %collective-permute-start.14) | collective-permute-done | bytes 1179680 | tf_op jit(solution)/shard_map/ppermute | solution.py:70
  220.3 21.2 %attention_backward.3 = (f32[3,128,2048]{2,1,0:T(8,128)S(1)}, bf16[1024,768]{1,0:T(8,128)(2,1)S(1)}) custom-call(s32[3]{0:T(128)S(1)} %copy-done.14, s32[8]{0:T(128)S(1)} %copy-done.16, s32[8]{0:T(128)S(1)} %copy-done.15, bf16[2048,384]{1,0:T(8,128)(2,1)S(1)} %copy-done.32, bf16[2048,384]{1,0:T(8,128)(2,1)S(1)} %copy-done.34, ...), custom_call_target="tpu_custom_call" | custom-call | flops 8053063680 | bytes 14295116 | tf_op jit(solution)/shard_map/attention_backward/pallas_call | solution.py:33
  243.3 7.2 %projection_grad.1 = (bf16[384,768]{1,0:T(8,128)(2,1)S(1)}, bf16[400,768]{1,0:T(8,128)(2,1)S(1)}, bf16[384,768]{1,0:T(8,128)(2,1)S(1)}, bf16[384,768]{1,0:T(8,12...) custom-call(s32[3]{0:T(128)S(1)} %copy-done.14, bf16[768,2048]{1,0:T(8,128)(2,1)S(1)} %transpose_tokens.1.token_t, ...), custom_call_target="tpu_custom_call" | custom-call | flops 3623878656 | bytes 17811468 | tf_op jit(solution)/shard_map/projection_grad/pallas_call | solution.py:33
  250.6 4.1 %collective-permute-start.21 = (bf16[384,768]{1,0:T(8,128)(2,1)S(1)}, bf16[384,768]{1,0:T(8,128)(2,1)S(1)}, u32[]{:S(2)}, u32[]{:S(2)}) collective-permute-start(bf16[384,768]{1,0:T(8,128)(2,1)S(1)} %get-tuple-element.142), channel_id=1, source_target_pairs={{0,4},{4,0},{1,5},{5,1},{2,6},{6,2},{3,7},{7,3},{8,12},{12,8},{9,1... | collective-permute-start | bytes 1769480 | tf_op jit(solution)/shard_map/ppermute | solution.py:70
  256.3 2.8 collective-permute-start.24
  259.1 8.0 %collective-permute-done.22 = bf16[2,96,768]{2,1,0:T(8,128)(2,1)S(1)} collective-permute-done((bf16[2,96,768]{2,1,0:T(8,128)(2,1)S(1)}, bf16[2,96,768]{2,1,0:T(8,128)(2,1)S(1)}, u32[]{:S(2)}, u32[]{:S(2)}) %collective-permute-start.22) | collective-permute-done | bytes 294944 | tf_op jit(solution)/shard_map/ppermute | solution.py:70
  267.1 11.1 %collective-permute-done.23 = bf16[2,96,768]{2,1,0:T(8,128)(2,1)S(1)} collective-permute-done((bf16[2,96,768]{2,1,0:T(8,128)(2,1)S(1)}, bf16[2,96,768]{2,1,0:T(8,128)(2,1)S(1)}, u32[]{:S(2)}, u32[]{:S(2)}) %collective-permute-start.23) | collective-permute-done | bytes 294944 | tf_op jit(solution)/shard_map/ppermute | solution.py:70
  279.8 2.8 input_grad_other.1
  283.4 2.7 collective-permute-done.25.arrived
  286.1 4.5 %input_grad_own.1 = f32[1024,768]{1,0:T(8,128)} custom-call(s32[3]{0:T(128)S(1)} %copy-done.14, bf16[2048,1152]{1,0:T(8,128)(2,1)S(1)} %get-tuple-element.153.dqkv, bf16[768,1152]{1,0:T(8,128)(2,1)S(1)} %copy-done.1, f32[1024,768]{1,0:T(8,128)S(1)} %copy-done.6, bf16[1024,768]{1,0:T(8,128)(2,1)S(1)} %collective-permute-done.25.arrived), custom_call_target="tpu_custom_call" | custom-call | flops 1811939328 | bytes 14352396 | tf_op jit(solution)/shard_map/input_grad_own/pallas_call | solution.py:33
  292.9 4.5 %collective-permute-start.28 = (bf16[112,768]{1,0:T(8,128)(2,1)S(1)}, bf16[112,768]{1,0:T(8,128)(2,1)S(1)}, u32[]{:S(2)}, u32[]{:S(2)}) collective-permute-start(bf16[112,768]{1,0:T(8,128)(2,1)S(1)} %get-tuple-element.158), channel_id=1, source_target_pairs={{0,8},{8,0},{16,24},{24,16},{1,9},{9,1},{17,25},{25,17},{2,10},{10... | collective-permute-start | bytes 516104 | tf_op jit(solution)/shard_map/ppermute | solution.py:70
  297.5 2.4 collective-permute-start.30
  300.7 3.2 %collective-permute-done.28.refs_0_ = bf16[112,768]{1,0:T(8,128)(2,1)S(1)} collective-permute-done((bf16[112,768]{1,0:T(8,128)(2,1)S(1)}, bf16[112,768]{1,0:T(8,128)(2,1)S(1)}, u32[]{:S(2)}, u32[]{:S(2)}) %collective-permute-start.28) | collective-permute-done | bytes 172064 | tf_op jit(solution)/shard_map/ppermute | solution.py:70
  303.9 8.8 %collective-permute-done.29.refs_1_ = bf16[112,768]{1,0:T(8,128)(2,1)S(1)} collective-permute-done((bf16[112,768]{1,0:T(8,128)(2,1)S(1)}, bf16[112,768]{1,0:T(8,128)(2,1)S(1)}, u32[]{:S(2)}, u32[]{:S(2)}) %collective-permute-start.29) | collective-permute-done | bytes 172064 | tf_op jit(solution)/shard_map/ppermute | solution.py:70
  (208 shorter events, 64.5 us)
Async XLA Ops:
  7.2 103.1 %all-gather.3.cloned.1.call-start = ((), (), s32[]{:S(2)}) async-start(), calls=%async_computation | async-start | bytes 11354112 | tf_op jit(solution)/shard_map/all_gather | solution.py:146
  10.3 11.1 %collective-permute-start.2 = (bf16[96,640]{1,0:T(8,128)(2,1)S(1)}, bf16[96,640]{1,0:T(8,128)(2,1)}, u32[]{:S(2)}, u32[]{:S(2)}) collective-permute-start(bf16[96,640]{1,0:T(8,128)(2,1)S(1)} %concatenate.15), channel_id=1, source_target_pairs={{0,24},{8,16},{16,8},{24,0},{1,25},{9,17},{17,9},{25,1},{2,26},{10... | collective-permute-start | bytes 368648 | tf_op jit(solution)/shard_map/ppermute | solution.py:70
  15.4 10.5 %collective-permute-start.1 = (bf16[96,640]{1,0:T(8,128)(2,1)S(1)}, bf16[96,640]{1,0:T(8,128)(2,1)}, u32[]{:S(2)}, u32[]{:S(2)}) collective-permute-start(bf16[96,640]{1,0:T(8,128)(2,1)S(1)} %concatenate.15), channel_id=1, source_target_pairs={{0,16},{8,24},{16,0},{24,8},{1,17},{9,25},{17,1},{25,9},{2,18},{10... | collective-permute-start | bytes 368648 | tf_op jit(solution)/shard_map/ppermute | solution.py:70
  15.4 11.4 %collective-permute-start = (bf16[96,640]{1,0:T(8,128)(2,1)S(1)}, bf16[96,640]{1,0:T(8,128)(2,1)S(1)}, u32[]{:S(2)}, u32[]{:S(2)}) collective-permute-start(bf16[96,640]{1,0:T(8,128)(2,1)S(1)} %concatenate.15), channel_id=1, source_target_pairs={{0,8},{8,0},{16,24},{24,16},{1,9},{9,1},{17,25},{25,17},{2,10},{10... | collective-permute-start | bytes 368648 | tf_op jit(solution)/shard_map/ppermute | solution.py:70
  17.9 14.3 %collective-permute-start.7 = (bf16[1024,768]{1,0:T(8,128)(2,1)S(1)}, bf16[1024,768]{1,0:T(8,128)(2,1)S(1)}, u32[]{:S(2)}, u32[]{:S(2)}) collective-permute-start(bf16[1024,768]{1,0:T(8,128)(2,1)S(1)} %copy-done.7), channel_id=1, source_target_pairs={{0,1},{1,0},{2,3},{3,2},{4,5},{5,4},{6,7},{7,6},{8,9},{9,8},{10,11... | collective-permute-start | bytes 4718600 | tf_op jit(solution)/shard_map/ppermute | solution.py:70
  39.6 21.8 %collective-permute-start.9 = (bf16[2,4,48,640]{3,2,1,0:T(8,128)(2,1)}, bf16[2,4,48,640]{3,2,1,0:T(8,128)(2,1)}, u32[]{:S(2)}, u32[]{:S(2)}) collective-permute-start(bf16[2,4,48,640]{3,2,1,0:T(8,128)(2,1)} %pad_maximum_fusion.1.refs_2_), channel_id=1, source_target_pairs={{0,2},{2,0},{1,3},{3,1},{4,6},{6,4},{5,7},{7,5},{8,10},{10,8},{9,1... | collective-permute-start | bytes 1474568 | tf_op jit(solution)/shard_map/ppermute | solution.py:70
  41.9 19.5 %collective-permute-start.8 = (bf16[2,4,48,640]{3,2,1,0:T(8,128)(2,1)}, bf16[2,4,48,640]{3,2,1,0:T(8,128)(2,1)}, u32[]{:S(2)}, u32[]{:S(2)}) collective-permute-start(bf16[2,4,48,640]{3,2,1,0:T(8,128)(2,1)} %pad_maximum_fusion.refs_0_), channel_id=1, source_target_pairs={{0,4},{4,0},{1,5},{5,1},{2,6},{6,2},{3,7},{7,3},{8,12},{12,8},{9,1... | collective-permute-start | bytes 1474568 | tf_op jit(solution)/shard_map/ppermute | solution.py:70
  147.6 14.0 %collective-permute-start.11 = (bf16[1024,768]{1,0:T(8,128)(2,1)}, bf16[1024,768]{1,0:T(8,128)(2,1)S(1)}, u32[]{:S(2)}, u32[]{:S(2)}) collective-permute-start(bf16[1024,768]{1,0:T(8,128)(2,1)} %get-tuple-element.96.da_own), channel_id=1, source_target_pairs={{0,1},{1,0},{2,3},{3,2},{4,5},{5,4},{6,7},{7,6},{8,9},{9,8},{10,11... | collective-permute-start | bytes 4718600 | tf_op jit(solution)/shard_map/ppermute | solution.py:70
  162.7 16.2 %collective-permute-start.12 = (bf16[2,768,768]{2,1,0:T(8,128)(2,1)}, bf16[2,768,768]{2,1,0:T(8,128)(2,1)}, u32[]{:S(2)}, u32[]{:S(2)}) collective-permute-start(bf16[2,768,768]{2,1,0:T(8,128)(2,1)} %get-tuple-element.110), channel_id=1, source_target_pairs={{0,1},{1,0},{2,3},{3,2},{4,5},{5,4},{6,7},{7,6},{8,9},{9,8},{10,11... | collective-permute-start | bytes 7077896 | tf_op jit(solution)/shard_map/ppermute | solution.py:70
  162.9 16.1 %collective-permute-start.13 = (bf16[2,768,768]{2,1,0:T(8,128)(2,1)}, bf16[2,768,768]{2,1,0:T(8,128)(2,1)}, u32[]{:S(2)}, u32[]{:S(2)}) collective-permute-start(bf16[2,768,768]{2,1,0:T(8,128)(2,1)} %get-tuple-element.111), channel_id=1, source_target_pairs={{0,1},{1,0},{2,3},{3,2},{4,5},{5,4},{6,7},{7,6},{8,9},{9,8},{10,11... | collective-permute-start | bytes 7077896 | tf_op jit(solution)/shard_map/ppermute | solution.py:70
  164.2 25.0 %collective-permute-start.19 = (f32[2,768]{1,0:T(2,128)S(1)}, f32[2,768]{1,0:T(2,128)S(1)}, u32[]{:S(2)}, u32[]{:S(2)}) collective-permute-start(f32[2,768]{1,0:T(2,128)S(1)} %bitcast.80), channel_id=1, source_target_pairs={{0,1},{1,0},{2,3},{3,2},{4,5},{5,4},{6,7},{7,6},{8,9},{9,8},{10,11... | collective-permute-start | bytes 18440 | tf_op jit(solution)/shard_map/ppermute | solution.py:70
  164.4 24.8 %collective-permute-start.18 = (f32[6,768]{1,0:T(8,128)S(1)}, f32[6,768]{1,0:T(8,128)S(1)}, u32[]{:S(2)}, u32[]{:S(2)}) collective-permute-start(f32[6,768]{1,0:T(8,128)S(1)} %bitcast.78), channel_id=1, source_target_pairs={{0,1},{1,0},{2,3},{3,2},{4,5},{5,4},{6,7},{7,6},{8,9},{9,8},{10,11... | collective-permute-start | bytes 55304 | tf_op jit(solution)/shard_map/ppermute | solution.py:70
  187.8 28.1 %collective-permute-start.14 = (bf16[2,384,768]{2,1,0:T(8,128)(2,1)S(1)}, bf16[2,384,768]{2,1,0:T(8,128)(2,1)S(1)}, u32[]{:S(2)}, u32[]{:S(2)}) collective-permute-start(bf16[2,384,768]{2,1,0:T(8,128)(2,1)S(1)} %get-tuple-element.113), channel_id=1, source_target_pairs={{0,2},{2,0},{1,3},{3,1},{4,6},{6,4},{5,7},{7,5},{8,10},{10,8},{9,1... | collective-permute-start | bytes 3538952 | tf_op jit(solution)/shard_map/ppermute | solution.py:70
  188.6 27.8 %collective-permute-start.15 = (bf16[2,384,768]{2,1,0:T(8,128)(2,1)S(1)}, bf16[2,384,768]{2,1,0:T(8,128)(2,1)S(1)}, u32[]{:S(2)}, u32[]{:S(2)}) collective-permute-start(bf16[2,384,768]{2,1,0:T(8,128)(2,1)S(1)} %get-tuple-element.114), channel_id=1, source_target_pairs={{0,4},{4,0},{1,5},{5,1},{2,6},{6,2},{3,7},{7,3},{8,12},{12,8},{9,1... | collective-permute-start | bytes 3538952 | tf_op jit(solution)/shard_map/ppermute | solution.py:70
  216.7 24.8 %collective-permute-start.16 = (bf16[2,192,768]{2,1,0:T(8,128)(2,1)S(1)}, bf16[2,192,768]{2,1,0:T(8,128)(2,1)S(1)}, u32[]{:S(2)}, u32[]{:S(2)}) collective-permute-start(bf16[2,192,768]{2,1,0:T(8,128)(2,1)S(1)} %get-tuple-element.122), channel_id=1, source_target_pairs={{0,4},{4,0},{1,5},{5,1},{2,6},{6,2},{3,7},{7,3},{8,12},{12,8},{9,1... | collective-permute-start | bytes 1769480 | tf_op jit(solution)/shard_map/ppermute | solution.py:70
  217.4 24.1 %collective-permute-start.17 = (bf16[2,192,768]{2,1,0:T(8,128)(2,1)S(1)}, bf16[2,192,768]{2,1,0:T(8,128)(2,1)S(1)}, u32[]{:S(2)}, u32[]{:S(2)}) collective-permute-start(bf16[2,192,768]{2,1,0:T(8,128)(2,1)S(1)} %get-tuple-element.123), channel_id=1, source_target_pairs={{0,2},{2,0},{1,3},{3,1},{4,6},{6,4},{5,7},{7,5},{8,10},{10,8},{9,1... | collective-permute-start | bytes 1769480 | tf_op jit(solution)/shard_map/ppermute | solution.py:70
  250.5 27.9 %collective-permute-start.20 = (bf16[400,768]{1,0:T(8,128)(2,1)S(1)}, bf16[400,768]{1,0:T(8,128)(2,1)S(1)}, u32[]{:S(2)}, u32[]{:S(2)}) collective-permute-start(bf16[400,768]{1,0:T(8,128)(2,1)S(1)} %get-tuple-element.141), channel_id=1, source_target_pairs={{0,2},{2,0},{1,3},{3,1},{4,6},{6,4},{5,7},{7,5},{8,10},{10,8},{9,1... | collective-permute-start | bytes 1843208 | tf_op jit(solution)/shard_map/ppermute | solution.py:70
  250.6 27.8 %collective-permute-start.21 = (bf16[384,768]{1,0:T(8,128)(2,1)S(1)}, bf16[384,768]{1,0:T(8,128)(2,1)S(1)}, u32[]{:S(2)}, u32[]{:S(2)}) collective-permute-start(bf16[384,768]{1,0:T(8,128)(2,1)S(1)} %get-tuple-element.142), channel_id=1, source_target_pairs={{0,4},{4,0},{1,5},{5,1},{2,6},{6,2},{3,7},{7,3},{8,12},{12,8},{9,1... | collective-permute-start | bytes 1769480 | tf_op jit(solution)/shard_map/ppermute | solution.py:70
  254.7 12.4 %collective-permute-start.22 = (bf16[2,96,768]{2,1,0:T(8,128)(2,1)S(1)}, bf16[2,96,768]{2,1,0:T(8,128)(2,1)S(1)}, u32[]{:S(2)}, u32[]{:S(2)}) collective-permute-start(bf16[2,96,768]{2,1,0:T(8,128)(2,1)S(1)} %get-tuple-element.131), channel_id=1, source_target_pairs={{0,8},{8,0},{16,24},{24,16},{1,9},{9,1},{17,25},{25,17},{2,10},{10... | collective-permute-start | bytes 884744 | tf_op jit(solution)/shard_map/ppermute | solution.py:70
  254.7 23.5 %collective-permute-start.23 = (bf16[2,96,768]{2,1,0:T(8,128)(2,1)S(1)}, bf16[2,96,768]{2,1,0:T(8,128)(2,1)S(1)}, u32[]{:S(2)}, u32[]{:S(2)}) collective-permute-start(bf16[2,96,768]{2,1,0:T(8,128)(2,1)S(1)} %get-tuple-element.132), channel_id=1, source_target_pairs={{0,16},{8,24},{16,0},{24,8},{1,17},{9,25},{17,1},{25,9},{2,18},{10... | collective-permute-start | bytes 884744 | tf_op jit(solution)/shard_map/ppermute | solution.py:70
  256.3 21.9 %collective-permute-start.24 = (bf16[2,96,768]{2,1,0:T(8,128)(2,1)S(1)}, bf16[2,96,768]{2,1,0:T(8,128)(2,1)S(1)}, u32[]{:S(2)}, u32[]{:S(2)}) collective-permute-start(bf16[2,96,768]{2,1,0:T(8,128)(2,1)S(1)} %get-tuple-element.133), channel_id=1, source_target_pairs={{0,24},{8,16},{16,8},{24,0},{1,25},{9,17},{17,9},{25,1},{2,26},{10... | collective-permute-start | bytes 884744 | tf_op jit(solution)/shard_map/ppermute | solution.py:70
  292.9 11.0 %collective-permute-start.28 = (bf16[112,768]{1,0:T(8,128)(2,1)S(1)}, bf16[112,768]{1,0:T(8,128)(2,1)S(1)}, u32[]{:S(2)}, u32[]{:S(2)}) collective-permute-start(bf16[112,768]{1,0:T(8,128)(2,1)S(1)} %get-tuple-element.158), channel_id=1, source_target_pairs={{0,8},{8,0},{16,24},{24,16},{1,9},{9,1},{17,25},{25,17},{2,10},{10... | collective-permute-start | bytes 516104 | tf_op jit(solution)/shard_map/ppermute | solution.py:70
  297.4 15.4 %collective-permute-start.29 = (bf16[112,768]{1,0:T(8,128)(2,1)S(1)}, bf16[112,768]{1,0:T(8,128)(2,1)S(1)}, u32[]{:S(2)}, u32[]{:S(2)}) collective-permute-start(bf16[112,768]{1,0:T(8,128)(2,1)S(1)} %get-tuple-element.159), channel_id=1, source_target_pairs={{0,16},{8,24},{16,0},{24,8},{1,17},{9,25},{17,1},{25,9},{2,18},{10... | collective-permute-start | bytes 516104 | tf_op jit(solution)/shard_map/ppermute | solution.py:70
  297.5 15.3 %collective-permute-start.30 = (bf16[112,768]{1,0:T(8,128)(2,1)S(1)}, bf16[112,768]{1,0:T(8,128)(2,1)S(1)}, u32[]{:S(2)}, u32[]{:S(2)}) collective-permute-start(bf16[112,768]{1,0:T(8,128)(2,1)S(1)} %get-tuple-element.160), channel_id=1, source_target_pairs={{0,24},{8,16},{16,8},{24,0},{1,25},{9,17},{17,9},{25,1},{2,26},{10... | collective-permute-start | bytes 516104 | tf_op jit(solution)/shard_map/ppermute | solution.py:70
  (56 other events, 603.4 us)
Sparse Core Ops, SparseCore 0:
  10.9 99.2 all-gather.2

commit v4 on v3

--- a/solution.py
+++ b/solution.py
@@ -229,6 +229,8 @@
 VM_HEADS = 60
 VM_ROWS = 60
 VM_GRAD = 40
+VM_PART = 60
+VM_START = 60
 VM_BACK = 36
 VM_PROJ = 36
 
@@ -534,7 +536,7 @@
 
 
 def finish_heads(count, near, vector, *refs):
-    arrived, (qkv_out, out_out, vector_out) = refs[:count], refs[count:]
+    arrived, (qkv_out, out_out, six_out, hidden_out, head_out) = refs[:count], refs[count:]
     total, sums = near[...], vector[...]
     rows = total.shape[0]
     for part in arrived:
@@ -548,7 +550,11 @@
             out_out[...] = value
         else:
             qkv_out[kind] = value
-    vector_out[...] = sums
+    lanes = heads * d
+    six_out[...] = sums[:6]
+    hidden_out[...] = sums[6:7]
+    head_out[0:1, :] = sums[7:8, :lanes]
+    head_out[1:2, :] = sums[7:8, lanes : 2 * lanes]
 
 
 def normalize(values):
@@ -814,7 +820,7 @@
         grid=(tiles,),
         flops=ffn,
         name="grad_for_partner",
-        vmem=VM_GRAD,
+        vmem=VM_PART,
     )
     dctx, delta, out_grad = call(
         heads_back_start,
@@ -824,7 +830,7 @@
         scratch=[pltpu.VMEM((width, rows), BF16)],
         flops=4 * seq * width * lanes,
         name="heads_back_start",
-        vmem=VM_PROJ,
+        vmem=VM_START,
     )
     received = [g.swap(a, "c") for a in after(for_partner, other_da)]
     leaving = Scatter.shapes(g, shard, hidden, weights=2)
@@ -882,17 +888,17 @@
     head_grad = Scatter(g, shard, arrays, (vector[0], vector[1]))
     ffn_parts = ffn_grad.third(arrays)
     ffn_share = ffn_parts[0] + sum(part.astype(F32) for part in ffn_parts[1:])
-    head_away = head_grad.first(ffn_share)
     (ig_other,) = call(
         input_grad_other,
         [shape_of((rows, width), BF16)],
-        [meta, after(dqkv, head_away), w],
+        [meta, dqkv, w],
         in_specs=[SMEM] + [VMEM] * 2,
         flops=seq * width * 3 * lanes,
         name="input_grad_other",
         vmem=VM_PROJ,
     )
-    ig_arrived = g.swap(ig_other, "c")
+    head_away = head_grad.first((ffn_share, ig_other))
+    ig_arrived = g.swap(after(ig_other, head_away), "c")
     (input_grad,) = call(
         input_grad_own,
         [shape_of((rows, width), F32)],
@@ -906,9 +912,10 @@
     down_share, up_share = ffn_share[0], ffn_share[1]
     parts = head_grad.third()
     if regular:
-        qkv_share, out_share, summed = call(
+        qkv_share, out_share, vectors_grad, up_bias_share, qv_share = call(
             partial(finish_heads, len(parts) - 2),
-            [shape_of((3, shard, local_width), F32), shape_of((shard, local_width), F32), shape_of((8, width), F32)],
+            [shape_of((3, shard, local_width), F32), shape_of((shard, local_width), F32), shape_of((6, width), F32)]
+            + [shape_of((1, width), F32), shape_of((2, local_width), F32)],
             parts,
             name="finish_heads",
             vmem=SUM_VMEM,
@@ -917,9 +924,10 @@
         shares, summed = parts
         shares = shares.reshape(shard, heads, 4, d).transpose(2, 0, 1, 3).reshape(4, shard, local_width)
         qkv_share, out_share = shares[:3], shares[3]
+        vectors_grad, up_bias_share = summed[:6], summed[6:7]
+        qv_share = summed[7, : 2 * local_width].reshape(2, local_width)
     qkv_share = qkv_share.transpose(1, 0, 2)
-    vectors_grad, up_bias_share = summed[:6], summed[6]
-    qv_share = summed[7, : 2 * local_width].reshape(2, local_width)
+    up_bias_share = up_bias_share.reshape(-1)
     return (output, input_grad, qkv_share, qv_share, out_share, up_share, up_bias_share, down_share, vectors_grad)
 
 

time: 325 us -> 296 us (0.911)
  local copies, waits for them, and re-layouts: 35.9 us -> 14.6 us
  waiting for transfers between devices: 68.1 us -> 54.7 us
  Pallas kernels: 165 us -> 173 us
    unnamed x99 -> x83, local copies, waits for them, and re-layouts: 24.3 us -> 5.63 us
    ppermute x31, waiting for transfers between devices: 68.1 us -> 54 us  [swap(): return lax.ppermute(array, axis, [(i, i ^ r) for i in range(size)])]
    pallas_call x16, Pallas kernels: 165 us -> 173 us  [call(): pl.pallas_call(body, grid=grid, out_shape=outs, in_specs=in_specs or [VME...]
  transfers between devices with their start and end apart: 32 -> 32, of which waited for: 14 -> 16; matrix products, arithmetic and copies ran while one was open for 4% -> 4% of each run, Pallas kernels for 36% -> 45%
where the time goes in v4:
time: 296 us; the launch traced here: 295 us
  Pallas kernels  173 us (58%)
  waiting for transfers between devices  54.7 us (18%)
  starting transfers between devices  32.6 us (11%)
  between operations  14.8 us (5%)
  local copies, waits for them, and re-layouts  14.6 us (5%)
  other arithmetic  5.2 us (2%)
    pallas_call x16, Pallas kernels, call(): pl.pallas_call(body, grid=grid, out_shape=outs, in_specs=in_specs or [VME...  173 us
    ppermute x31, waiting for transfers between devices, swap(): return lax.ppermute(array, axis, [(i, i ^ r) for i in range(size)])  54 us
    ppermute x31, starting transfers between devices, swap(): return lax.ppermute(array, axis, [(i, i ^ r) for i in range(size)])  32.6 us
  transfers between devices with their start and end apart: 32, of which 16 were waited for; matrix products, arithmetic and copies ran while one was open for 4% of the time, Pallas kernels for 45%

profile of v4, /device:TPU:0, one launch (start us, length us, event | category | flops | bytes accessed | tf_op | source)
XLA Modules:
  0.0 295.3 jit_solution(6633550515986480005)
XLA Ops:
  8.5 1.8 concatenate.16
  10.3 5.1 %collective-permute-start.2 = (bf16[96,640]{1,0:T(8,128)(2,1)S(1)}, bf16[96,640]{1,0:T(8,128)(2,1)}, u32[]{:S(2)}, u32[]{:S(2)}) collective-permute-start(bf16[96,640]{1,0:T(8,128)(2,1)S(1)} %concatenate.15), channel_id=1, source_target_pairs={{0,24},{8,16},{16,8},{24,0},{1,25},{9,17},{17,9},{25,1},{2,26},{10... | collective-permute-start | bytes 368648 | tf_op jit(solution)/shard_map/ppermute | solution.py:70
  17.9 2.0 collective-permute-done.3
  22.3 3.7 %collective-permute-done.1 = bf16[96,640]{1,0:T(8,128)(2,1)} collective-permute-done((bf16[96,640]{1,0:T(8,128)(2,1)S(1)}, bf16[96,640]{1,0:T(8,128)(2,1)}, u32[]{:S(2)}, u32[]{:S(2)}) %collective-permute-start.1) | collective-permute-done | bytes 122912 | tf_op jit(solution)/shard_map/ppermute | solution.py:70
  33.7 1.7 copy-done.3
  42.1 14.2 %collective-permute-done.9.refs_3_ = bf16[2,4,48,640]{3,2,1,0:T(8,128)(2,1)S(1)} collective-permute-done((bf16[2,4,48,640]{3,2,1,0:T(8,128)(2,1)S(1)}, bf16[2,4,48,640]{3,2,1,0:T(8,128)(2,1)S(1)}, u32[]{:S(2)}, u32[]{:S(2)}) %collective-permute-start.9) | collective-permute-done | bytes 491552 | tf_op jit(solution)/shard_map/ppermute | solution.py:70
  57.3 47.4 %heads_forward.1 = (bf16[2048,384]{1,0:T(8,128)(2,1)}, bf16[2048,384]{1,0:T(8,128)(2,1)}, bf16[2048,384]{1,0:T(8,128)(2,1)}, bf16[768,1152]{1,0:T(8,128)(2,1)}, ...) custom-call(s32[3]{0:T(128)} %copy-done.10, s32[8]{0:T(128)} %get-tuple-element.199.lows, ...), custom_call_target="tpu_custom_call" | custom-call | flops 10066329600 | bytes 13249612 | tf_op jit(solution)/shard_map/heads_forward/pallas_call | solution.py:33
  108.1 37.3 %rows_step.1 = (bf16[1024,768]{1,0:T(8,128)(2,1)}, f32[1024,768]{1,0:T(8,128)}, bf16[1024,768]{1,0:T(8,128)(2,1)}, bf16[1024,3072]{1,0:T(8,128)(2,1)}, bf16[1024...) custom-call(s32[3]{0:T(128)} %copy-done.10, ...), custom_call_target="tpu_custom_call" | custom-call | flops 20535312384 | bytes 38498316 | tf_op jit(solution)/shard_map/rows_step/pallas_call | solution.py:33
  145.7 9.3 %grad_for_partner.1 = (bf16[2,768,768]{2,1,0:T(8,128)(2,1)}, bf16[2,768,768]{2,1,0:T(8,128)(2,1)}) custom-call(bf16[768,1024]{1,0:T(8,128)(2,1)} %get-tuple-element.106.df_t, bf16[768,1024]{1,0:T(8,128)(2,1)} %get-tuple-element.107.low_t, bf16[1024,3072]{1,0:T(8,128)(2,1)} %get-tuple-element.108.act_one.act_two, ...), custom_call_target="tpu_custom_call" | custom-call | flops 4831838208 | bytes 33030144 | tf_op jit(solution)/shard_map/grad_for_partner/pallas_call | solution.py:33
  157.7 10.0 %heads_back_start.1 = (bf16[2048,384]{1,0:T(8,128)(2,1)}, f32[8,8,256]{2,1,0:T(8,128)}, f32[768,384]{1,0:T(8,128)}) custom-call(s32[3]{0:T(128)} %copy-done.10, bf16[1024,768]{1,0:T(8,128)(2,1)} %get-tuple-element.98.da_own, bf16[1024,768]{1,0:T(8,128)(2,1)} %copy-done.36, bf16[1024,384]{1,0:T(8,128)(2,1)} %get-tuple-element.95.ctx_own, ...), custom_call_target="tpu_custom_call" | custom-call | flops 2415919104 | bytes 8126476 | tf_op jit(solution)/shard_map/heads_back_start/pallas_call | solution.py:33
  167.8 8.3 %grad_for_chip.1 = (bf16[2,384,768]{2,1,0:T(8,128)(2,1)S(1)}, bf16[2,384,768]{2,1,0:T(8,128)(2,1)S(1)}, bf16[2,384,768]{2,1,0:T(8,128)(2,1)S(1)}, bf16[2,384,768]{2,1,0:T(8,128)(2,1)S(1)}) custom-call(s32[3]{0:T(128)S(1)} %copy-done.11, bf16[768,1024]{1,0:T(8,128)(2,1)S(1)} %copy-done.1, bf16[768,1024]{1,0:T(8,128)(2,1)S(1)} %copy-done.2, ...), custom_call_target="tpu_custom_call" | custom-call | flops 4831838208 | bytes 37748748 | tf_op jit(solution)/shard_map/grad_for_chip/pallas_call | solution.py:33
  179.9 19.4 %attention_backward.2 = (f32[3,128,2048]{2,1,0:T(8,128)S(1)}, bf16[1024,768]{1,0:T(8,128)(2,1)S(1)}) custom-call(s32[3]{0:T(128)S(1)} %copy-done.11, s32[8]{0:T(128)S(1)} %copy-done.13, s32[8]{0:T(128)S(1)} %copy-done.12, bf16[2048,384]{1,0:T(8,128)(2,1)S(1)} %copy-done.17, bf16[2048,384]{1,0:T(8,128)(2,1)S(1)} %copy-done.19, ...), custom_call_target="tpu_custom_call" | custom-call | flops 8053063680 | bytes 11149388 | tf_op jit(solution)/shard_map/attention_backward/pallas_call | solution.py:33
  199.3 5.1 %collective-permute-done.14.got_x = bf16[2,384,768]{2,1,0:T(8,128)(2,1)S(1)} collective-permute-done((bf16[2,384,768]{2,1,0:T(8,128)(2,1)S(1)}, bf16[2,384,768]{2,1,0:T(8,128)(2,1)S(1)}, u32[]{:S(2)}, u32[]{:S(2)}) %collective-permute-start.14) | collective-permute-done | bytes 1179680 | tf_op jit(solution)/shard_map/ppermute | solution.py:70
  208.1 23.7 %attention_backward.3 = (f32[3,128,2048]{2,1,0:T(8,128)S(1)}, bf16[1024,768]{1,0:T(8,128)(2,1)S(1)}) custom-call(s32[3]{0:T(128)S(1)} %copy-done.11, s32[8]{0:T(128)S(1)} %copy-done.13, s32[8]{0:T(128)S(1)} %copy-done.12, bf16[2048,384]{1,0:T(8,128)(2,1)S(1)} %copy-done.18, bf16[2048,384]{1,0:T(8,128)(2,1)S(1)} %copy-done.20, ...), custom_call_target="tpu_custom_call" | custom-call | flops 8053063680 | bytes 14295116 | tf_op jit(solution)/shard_map/attention_backward/pallas_call | solution.py:33
  232.3 4.3 %collective-permute-start.24 = (bf16[2,96,768]{2,1,0:T(8,128)(2,1)S(1)}, bf16[2,96,768]{2,1,0:T(8,128)(2,1)S(1)}, u32[]{:S(2)}, u32[]{:S(2)}) collective-permute-start(bf16[2,96,768]{2,1,0:T(8,128)(2,1)S(1)} %get-tuple-element.135), channel_id=1, source_target_pairs={{0,24},{8,16},{16,8},{24,0},{1,25},{9,17},{17,9},{25,1},{2,26},{10... | collective-permute-start | bytes 884744 | tf_op jit(solution)/shard_map/ppermute | solution.py:70
  236.6 7.3 %projection_grad.1 = (bf16[384,768]{1,0:T(8,128)(2,1)S(1)}, bf16[400,768]{1,0:T(8,128)(2,1)S(1)}, bf16[384,768]{1,0:T(8,128)(2,1)S(1)}, bf16[384,768]{1,0:T(8,12...) custom-call(s32[3]{0:T(128)S(1)} %copy-done.11, bf16[768,2048]{1,0:T(8,128)(2,1)S(1)} %copy-done.4, ...), custom_call_target="tpu_custom_call" | custom-call | flops 3623878656 | bytes 17811468 | tf_op jit(solution)/shard_map/projection_grad/pallas_call | solution.py:33
  244.0 2.0 collective-permute-start.20
  246.0 2.8 input_grad_other.1
  248.8 6.5 %collective-permute-done.23 = bf16[2,96,768]{2,1,0:T(8,128)(2,1)S(1)} collective-permute-done((bf16[2,96,768]{2,1,0:T(8,128)(2,1)S(1)}, bf16[2,96,768]{2,1,0:T(8,128)(2,1)S(1)}, u32[]{:S(2)}, u32[]{:S(2)}) %collective-permute-start.23) | collective-permute-done | bytes 294944 | tf_op jit(solution)/shard_map/ppermute | solution.py:70
  261.7 4.5 %input_grad_own.1 = f32[1024,768]{1,0:T(8,128)} custom-call(s32[3]{0:T(128)S(1)} %copy-done.11, bf16[2048,1152]{1,0:T(8,128)(2,1)S(1)} %get-tuple-element.139.dqkv, bf16[768,1152]{1,0:T(8,128)(2,1)S(1)} %copy-done, f32[1024,768]{1,0:T(8,128)S(1)} %copy-done.5, bf16[1024,768]{1,0:T(8,128)(2,1)S(1)} %collective-permute-done.25.arrived), custom_call_target="tpu_custom_call" | custom-call | flops 1811939328 | bytes 14352396 | tf_op jit(solution)/shard_map/input_grad_own/pallas_call | solution.py:33
  266.2 2.6 collective-permute-done.27.last_y
  269.0 2.4 collective-permute-start.28
  274.7 2.8 collective-permute-done.28.refs_0_
  277.5 9.4 %collective-permute-done.29.refs_1_ = bf16[112,768]{1,0:T(8,128)(2,1)S(1)} collective-permute-done((bf16[112,768]{1,0:T(8,128)(2,1)S(1)}, bf16[112,768]{1,0:T(8,128)(2,1)S(1)}, u32[]{:S(2)}, u32[]{:S(2)}) %collective-permute-start.29) | collective-permute-done | bytes 172064 | tf_op jit(solution)/shard_map/ppermute | solution.py:70
  (190 shorter events, 46.9 us)
Async XLA Ops:
  7.2 100.7 %all-gather.3.cloned.1.call-start = ((), (), s32[]{:S(2)}) async-start(), calls=%async_computation | async-start | bytes 11354112 | tf_op jit(solution)/shard_map/all_gather | solution.py:146
  10.3 11.1 %collective-permute-start.2 = (bf16[96,640]{1,0:T(8,128)(2,1)S(1)}, bf16[96,640]{1,0:T(8,128)(2,1)}, u32[]{:S(2)}, u32[]{:S(2)}) collective-permute-start(bf16[96,640]{1,0:T(8,128)(2,1)S(1)} %concatenate.15), channel_id=1, source_target_pairs={{0,24},{8,16},{16,8},{24,0},{1,25},{9,17},{17,9},{25,1},{2,26},{10... | collective-permute-start | bytes 368648 | tf_op jit(solution)/shard_map/ppermute | solution.py:70
  15.5 10.5 %collective-permute-start.1 = (bf16[96,640]{1,0:T(8,128)(2,1)S(1)}, bf16[96,640]{1,0:T(8,128)(2,1)}, u32[]{:S(2)}, u32[]{:S(2)}) collective-permute-start(bf16[96,640]{1,0:T(8,128)(2,1)S(1)} %concatenate.15), channel_id=1, source_target_pairs={{0,16},{8,24},{16,0},{24,8},{1,17},{9,25},{17,1},{25,9},{2,18},{10... | collective-permute-start | bytes 368648 | tf_op jit(solution)/shard_map/ppermute | solution.py:70
  15.5 11.4 %collective-permute-start = (bf16[96,640]{1,0:T(8,128)(2,1)S(1)}, bf16[96,640]{1,0:T(8,128)(2,1)S(1)}, u32[]{:S(2)}, u32[]{:S(2)}) collective-permute-start(bf16[96,640]{1,0:T(8,128)(2,1)S(1)} %concatenate.15), channel_id=1, source_target_pairs={{0,8},{8,0},{16,24},{24,16},{1,9},{9,1},{17,25},{25,17},{2,10},{10... | collective-permute-start | bytes 368648 | tf_op jit(solution)/shard_map/ppermute | solution.py:70
  17.9 14.3 %collective-permute-start.7 = (bf16[1024,768]{1,0:T(8,128)(2,1)S(1)}, bf16[1024,768]{1,0:T(8,128)(2,1)S(1)}, u32[]{:S(2)}, u32[]{:S(2)}) collective-permute-start(bf16[1024,768]{1,0:T(8,128)(2,1)S(1)} %copy-done.6), channel_id=1, source_target_pairs={{0,1},{1,0},{2,3},{3,2},{4,5},{5,4},{6,7},{7,6},{8,9},{9,8},{10,11... | collective-permute-start | bytes 4718600 | tf_op jit(solution)/shard_map/ppermute | solution.py:70
  37.3 19.0 %collective-permute-start.9 = (bf16[2,4,48,640]{3,2,1,0:T(8,128)(2,1)S(1)}, bf16[2,4,48,640]{3,2,1,0:T(8,128)(2,1)S(1)}, u32[]{:S(2)}, u32[]{:S(2)}) collective-permute-start(bf16[2,4,48,640]{3,2,1,0:T(8,128)(2,1)S(1)} %pad_maximum_fusion.1.refs_2_), channel_id=1, source_target_pairs={{0,2},{2,0},{1,3},{3,1},{4,6},{6,4},{5,7},{7,5},{8,10},{10,8},{9,1... | collective-permute-start | bytes 1474568 | tf_op jit(solution)/shard_map/ppermute | solution.py:70
  38.9 17.4 %collective-permute-start.8 = (bf16[2,4,48,640]{3,2,1,0:T(8,128)(2,1)S(1)}, bf16[2,4,48,640]{3,2,1,0:T(8,128)(2,1)S(1)}, u32[]{:S(2)}, u32[]{:S(2)}) collective-permute-start(bf16[2,4,48,640]{3,2,1,0:T(8,128)(2,1)S(1)} %pad_maximum_fusion.refs_0_), channel_id=1, source_target_pairs={{0,4},{4,0},{1,5},{5,1},{2,6},{6,2},{3,7},{7,3},{8,12},{12,8},{9,1... | collective-permute-start | bytes 1474568 | tf_op jit(solution)/shard_map/ppermute | solution.py:70
  145.4 9.6 %collective-permute-start.11 = (bf16[1024,768]{1,0:T(8,128)(2,1)}, bf16[1024,768]{1,0:T(8,128)(2,1)S(1)}, u32[]{:S(2)}, u32[]{:S(2)}) collective-permute-start(bf16[1024,768]{1,0:T(8,128)(2,1)} %get-tuple-element.98.da_own), channel_id=1, source_target_pairs={{0,1},{1,0},{2,3},{3,2},{4,5},{5,4},{6,7},{7,6},{8,9},{9,8},{10,11... | collective-permute-start | bytes 4718600 | tf_op jit(solution)/shard_map/ppermute | solution.py:70
  155.0 12.8 %collective-permute-start.12 = (bf16[2,768,768]{2,1,0:T(8,128)(2,1)}, bf16[2,768,768]{2,1,0:T(8,128)(2,1)}, u32[]{:S(2)}, u32[]{:S(2)}) collective-permute-start(bf16[2,768,768]{2,1,0:T(8,128)(2,1)} %get-tuple-element.112), channel_id=1, source_target_pairs={{0,1},{1,0},{2,3},{3,2},{4,5},{5,4},{6,7},{7,6},{8,9},{9,8},{10,11... | collective-permute-start | bytes 7077896 | tf_op jit(solution)/shard_map/ppermute | solution.py:70
  155.4 12.4 %collective-permute-start.13 = (bf16[2,768,768]{2,1,0:T(8,128)(2,1)}, bf16[2,768,768]{2,1,0:T(8,128)(2,1)}, u32[]{:S(2)}, u32[]{:S(2)}) collective-permute-start(bf16[2,768,768]{2,1,0:T(8,128)(2,1)} %get-tuple-element.113), channel_id=1, source_target_pairs={{0,1},{1,0},{2,3},{3,2},{4,5},{5,4},{6,7},{7,6},{8,9},{9,8},{10,11... | collective-permute-start | bytes 7077896 | tf_op jit(solution)/shard_map/ppermute | solution.py:70
  157.1 21.2 %collective-permute-start.19 = (f32[2,768]{1,0:T(2,128)S(1)}, f32[2,768]{1,0:T(2,128)S(1)}, u32[]{:S(2)}, u32[]{:S(2)}) collective-permute-start(f32[2,768]{1,0:T(2,128)S(1)} %bitcast.79), channel_id=1, source_target_pairs={{0,1},{1,0},{2,3},{3,2},{4,5},{5,4},{6,7},{7,6},{8,9},{9,8},{10,11... | collective-permute-start | bytes 18440 | tf_op jit(solution)/shard_map/ppermute | solution.py:70
  157.5 20.9 %collective-permute-start.18 = (f32[6,768]{1,0:T(8,128)S(1)}, f32[6,768]{1,0:T(8,128)S(1)}, u32[]{:S(2)}, u32[]{:S(2)}) collective-permute-start(f32[6,768]{1,0:T(8,128)S(1)} %bitcast.77), channel_id=1, source_target_pairs={{0,1},{1,0},{2,3},{3,2},{4,5},{5,4},{6,7},{7,6},{8,9},{9,8},{10,11... | collective-permute-start | bytes 55304 | tf_op jit(solution)/shard_map/ppermute | solution.py:70
  176.2 28.2 %collective-permute-start.14 = (bf16[2,384,768]{2,1,0:T(8,128)(2,1)S(1)}, bf16[2,384,768]{2,1,0:T(8,128)(2,1)S(1)}, u32[]{:S(2)}, u32[]{:S(2)}) collective-permute-start(bf16[2,384,768]{2,1,0:T(8,128)(2,1)S(1)} %get-tuple-element.115), channel_id=1, source_target_pairs={{0,2},{2,0},{1,3},{3,1},{4,6},{6,4},{5,7},{7,5},{8,10},{10,8},{9,1... | collective-permute-start | bytes 3538952 | tf_op jit(solution)/shard_map/ppermute | solution.py:70
  177.5 27.8 %collective-permute-start.15 = (bf16[2,384,768]{2,1,0:T(8,128)(2,1)S(1)}, bf16[2,384,768]{2,1,0:T(8,128)(2,1)S(1)}, u32[]{:S(2)}, u32[]{:S(2)}) collective-permute-start(bf16[2,384,768]{2,1,0:T(8,128)(2,1)S(1)} %get-tuple-element.116), channel_id=1, source_target_pairs={{0,4},{4,0},{1,5},{5,1},{2,6},{6,2},{3,7},{7,3},{8,12},{12,8},{9,1... | collective-permute-start | bytes 3538952 | tf_op jit(solution)/shard_map/ppermute | solution.py:70
  205.6 26.1 %collective-permute-start.16 = (bf16[2,192,768]{2,1,0:T(8,128)(2,1)S(1)}, bf16[2,192,768]{2,1,0:T(8,128)(2,1)S(1)}, u32[]{:S(2)}, u32[]{:S(2)}) collective-permute-start(bf16[2,192,768]{2,1,0:T(8,128)(2,1)S(1)} %get-tuple-element.124), channel_id=1, source_target_pairs={{0,4},{4,0},{1,5},{5,1},{2,6},{6,2},{3,7},{7,3},{8,12},{12,8},{9,1... | collective-permute-start | bytes 1769480 | tf_op jit(solution)/shard_map/ppermute | solution.py:70
  206.6 25.2 %collective-permute-start.17 = (bf16[2,192,768]{2,1,0:T(8,128)(2,1)S(1)}, bf16[2,192,768]{2,1,0:T(8,128)(2,1)S(1)}, u32[]{:S(2)}, u32[]{:S(2)}) collective-permute-start(bf16[2,192,768]{2,1,0:T(8,128)(2,1)S(1)} %get-tuple-element.125), channel_id=1, source_target_pairs={{0,2},{2,0},{1,3},{3,1},{4,6},{6,4},{5,7},{7,5},{8,10},{10,8},{9,1... | collective-permute-start | bytes 1769480 | tf_op jit(solution)/shard_map/ppermute | solution.py:70
  232.2 16.6 %collective-permute-start.22 = (bf16[2,96,768]{2,1,0:T(8,128)(2,1)S(1)}, bf16[2,96,768]{2,1,0:T(8,128)(2,1)S(1)}, u32[]{:S(2)}, u32[]{:S(2)}) collective-permute-start(bf16[2,96,768]{2,1,0:T(8,128)(2,1)S(1)} %get-tuple-element.133), channel_id=1, source_target_pairs={{0,8},{8,0},{16,24},{24,16},{1,9},{9,1},{17,25},{25,17},{2,10},{10... | collective-permute-start | bytes 884744 | tf_op jit(solution)/shard_map/ppermute | solution.py:70
  232.3 23.0 %collective-permute-start.23 = (bf16[2,96,768]{2,1,0:T(8,128)(2,1)S(1)}, bf16[2,96,768]{2,1,0:T(8,128)(2,1)S(1)}, u32[]{:S(2)}, u32[]{:S(2)}) collective-permute-start(bf16[2,96,768]{2,1,0:T(8,128)(2,1)S(1)} %get-tuple-element.134), channel_id=1, source_target_pairs={{0,16},{8,24},{16,0},{24,8},{1,17},{9,25},{17,1},{25,9},{2,18},{10... | collective-permute-start | bytes 884744 | tf_op jit(solution)/shard_map/ppermute | solution.py:70
  232.3 22.9 %collective-permute-start.24 = (bf16[2,96,768]{2,1,0:T(8,128)(2,1)S(1)}, bf16[2,96,768]{2,1,0:T(8,128)(2,1)S(1)}, u32[]{:S(2)}, u32[]{:S(2)}) collective-permute-start(bf16[2,96,768]{2,1,0:T(8,128)(2,1)S(1)} %get-tuple-element.135), channel_id=1, source_target_pairs={{0,24},{8,16},{16,8},{24,0},{1,25},{9,17},{17,9},{25,1},{2,26},{10... | collective-permute-start | bytes 884744 | tf_op jit(solution)/shard_map/ppermute | solution.py:70
  243.9 13.2 %collective-permute-start.21 = (bf16[384,768]{1,0:T(8,128)(2,1)S(1)}, bf16[384,768]{1,0:T(8,128)(2,1)S(1)}, u32[]{:S(2)}, u32[]{:S(2)}) collective-permute-start(bf16[384,768]{1,0:T(8,128)(2,1)S(1)} %get-tuple-element.144), channel_id=1, source_target_pairs={{0,4},{4,0},{1,5},{5,1},{2,6},{6,2},{3,7},{7,3},{8,12},{12,8},{9,1... | collective-permute-start | bytes 1769480 | tf_op jit(solution)/shard_map/ppermute | solution.py:70
  244.0 14.1 %collective-permute-start.20 = (bf16[400,768]{1,0:T(8,128)(2,1)S(1)}, bf16[400,768]{1,0:T(8,128)(2,1)S(1)}, u32[]{:S(2)}, u32[]{:S(2)}) collective-permute-start(bf16[400,768]{1,0:T(8,128)(2,1)S(1)} %get-tuple-element.143), channel_id=1, source_target_pairs={{0,2},{2,0},{1,3},{3,1},{4,6},{6,4},{5,7},{7,5},{8,10},{10,8},{9,1... | collective-permute-start | bytes 1843208 | tf_op jit(solution)/shard_map/ppermute | solution.py:70
  258.3 10.5 %collective-permute-start.26 = (bf16[208,768]{1,0:T(8,128)(2,1)S(1)}, bf16[208,768]{1,0:T(8,128)(2,1)S(1)}, u32[]{:S(2)}, u32[]{:S(2)}) collective-permute-start(bf16[208,768]{1,0:T(8,128)(2,1)S(1)} %get-tuple-element.152), channel_id=1, source_target_pairs={{0,4},{4,0},{1,5},{5,1},{2,6},{6,2},{3,7},{7,3},{8,12},{12,8},{9,1... | collective-permute-start | bytes 958472 | tf_op jit(solution)/shard_map/ppermute | solution.py:70
  271.4 15.5 %collective-permute-start.29 = (bf16[112,768]{1,0:T(8,128)(2,1)S(1)}, bf16[112,768]{1,0:T(8,128)(2,1)S(1)}, u32[]{:S(2)}, u32[]{:S(2)}) collective-permute-start(bf16[112,768]{1,0:T(8,128)(2,1)S(1)} %get-tuple-element.161), channel_id=1, source_target_pairs={{0,16},{8,24},{16,0},{24,8},{1,17},{9,25},{17,1},{25,9},{2,18},{10... | collective-permute-start | bytes 516104 | tf_op jit(solution)/shard_map/ppermute | solution.py:70
  272.5 14.4 %collective-permute-start.30 = (bf16[112,768]{1,0:T(8,128)(2,1)S(1)}, bf16[112,768]{1,0:T(8,128)(2,1)S(1)}, u32[]{:S(2)}, u32[]{:S(2)}) collective-permute-start(bf16[112,768]{1,0:T(8,128)(2,1)S(1)} %get-tuple-element.162), channel_id=1, source_target_pairs={{0,24},{8,16},{16,8},{24,0},{1,25},{9,17},{17,9},{25,1},{2,26},{10... | collective-permute-start | bytes 516104 | tf_op jit(solution)/shard_map/ppermute | solution.py:70
  (48 other events, 584.0 us)
Sparse Core Ops, SparseCore 0:
  10.9 96.9 all-gather.2

commit v5 on v4

--- a/solution.py
+++ b/solution.py
@@ -154,7 +154,7 @@
     return [
         pltpu.make_async_copy(
             source.at[block, t, :, lanes],
-            target.at[t ^ me, pl.ds(block * rows, rows)],
+            target.at[t ^ me, pl.ds(block * rows, rows), lanes],
             sems.at[block * places + t],
         )
         for block in range(blocks)
@@ -484,7 +484,7 @@
             out[:, pl.ds(pl.multiple_of(base + r, BLOCK), BLOCK)] = source[r : r + BLOCK, :].T
 
 
-def projection_grad(nz, meta, token_t, out_grad, dq_t, dkv_one, dkv_two, vector, *refs):
+def projection_grad(nz, meta, token_t, out_grad, dq_t, dkv_one, dkv_two, sums_own, sums_other, *refs):
     outs, dqkv, stage = refs[:-2], refs[-2], refs[-1]
     d = HEAD_DIM
     seq = token_t.shape[1]
@@ -510,8 +510,9 @@
         store_blocks(jnp.concatenate(lanes, axis=1), outs[:-1], stage, place, meta[1], nz)
         for total in (q_sum, v_sum):
             biases += [total[:, j * PAIR + place * d : j * PAIR + (place + 1) * d] for j in range(width // PAIR)]
-        biases.append(jnp.zeros((1, vector.shape[2] - len(biases) * d), F32))
-        vectors.append(jnp.concatenate([vector[place], jnp.concatenate(biases, axis=1)], axis=0))
+        biases.append(jnp.zeros((1, sums_own.shape[1] - len(biases) * d), F32))
+        hidden = sums_own[8 + 2 * place : 9 + 2 * place, :] + sums_other[9 + 2 * place : 10 + 2 * place, :]
+        vectors.append(jnp.concatenate([sums_own[:6, :] + sums_other[:6, :], hidden, jnp.concatenate(biases, axis=1)], axis=0))
     outs[-1][0] = vectors[0]
     outs[-1][1] = vectors[1]
     if len(outs) > 2:
@@ -577,21 +578,22 @@
 
 def rows_step(
     meta, everywhere, tokens, vectors, ctx_own, ctx_other, bias, out_grad,
-    output, dr1_out, da_out, act_out, du_out, df_t, low_t, sums, bias_sums, wo_own,
-    w_out, w_all, slope, sems,
+    output, dr1_out, da_out, act_out, du_out, df_t, low_t, sums, wo_own,
+    w_out, w_all, slope, sems_out, sems,
 ):
     hidden = tokens.shape[1]
     half = ctx_own.shape[1]
-    copies = everywhere_copies(everywhere, meta[2], w_all, sems, slice(None))
+    copies_out = everywhere_copies(everywhere, meta[2], w_all, sems_out, slice(2 * hidden, None))
+    copies = everywhere_copies(everywhere, meta[2], w_all, sems, slice(0, 2 * hidden))
     w_up = w_all.at[:, :, :hidden]
     w_down = w_all.at[:, :, hidden : 2 * hidden]
     start = pl.program_id(0) == 0
 
     @pl.when(start)
     def _():
-        for copy in copies:
+        for copy in copies_out + copies:
             copy.start()
-        for copy in copies:
+        for copy in copies_out:
             copy.wait()
         d = HEAD_DIM
         for core in range(2):
@@ -602,7 +604,6 @@
                 w_out[:, at : at + PAIR] = jnp.concatenate(pair, axis=1)
         wo_own[...] = w_out[:, :half]
         sums[...] = jnp.zeros_like(sums)
-        bias_sums[...] = jnp.zeros_like(bias_sums)
 
     out_bias, gain_one, shift_one, down_bias, gain_two, shift_two = (vectors[n : n + 1, :] for n in range(6))
     mixed = dot_nt(jnp.concatenate([ctx_own[...], ctx_other[...]], axis=1), w_out[...])
@@ -610,6 +611,11 @@
     first = normed_one * gain_one + shift_one
     low = first.astype(BF16)
     low_t[...] = low.T
+
+    @pl.when(start)
+    def _():
+        for copy in copies:
+            copy.wait()
 
     for t in range(4):
         for n in range(0, hidden, BLOCK):
@@ -636,7 +642,7 @@
             at = slice(t * hidden + n, t * hidden + n + BLOCK)
             du = (dot_nn(df, w_down[t, :, n : n + BLOCK]) * slope[:, at]).astype(BF16)
             du_out[:, at] = du
-            bias_sums[0:1, at] += column_sum(du.astype(F32))
+            sums[8 + t : 9 + t, n : n + BLOCK] += column_sum(du.astype(F32))
     incoming = dr2
     for t in range(4):
         incoming = incoming + dot_nt(du_out[:, t * hidden : (t + 1) * hidden], w_up[t])
@@ -768,10 +774,9 @@
         return pl.BlockSpec(array.shape, lambda i: (0,) * len(array.shape))
 
     ffn = 2 * rows * width * 4 * hidden
-    sums_shape = shape_of((8, width), F32)
-    bias_shape = shape_of((8, 4 * hidden), F32)
+    sums_shape = shape_of((16, width), F32)
     weight_sems = pltpu.SemaphoreType.DMA((both.shape[0] * both.shape[1],))
-    output, dr1, da, act, du, df_t, low_t, sums_rows, hidden_sums, wo = call(
+    output, dr1, da, act, du, df_t, low_t, sums, wo = call(
         rows_step,
         [
             shape_of((rows, width), BF16),
@@ -782,7 +787,6 @@
             shape_of((width, rows), BF16),
             shape_of((width, rows), BF16),
             sums_shape,
-            bias_shape,
             shape_of((width, lanes), BF16),
         ],
         [meta, both, tokens, vectors, ctx_own, ctx_other, hidden_bias, output_grad],
@@ -791,11 +795,12 @@
         out_specs=[by_rows(width)] * 3
         + [by_rows(4 * hidden)] * 2
         + [by_columns(width)] * 2
-        + [fixed(sums_shape), fixed(bias_shape), pl.BlockSpec((width, lanes), lambda i: (0, 0))],
+        + [fixed(sums_shape), pl.BlockSpec((width, lanes), lambda i: (0, 0))],
         scratch=[
             pltpu.VMEM((width, width), BF16),
             pltpu.VMEM((4, width, both.shape[3]), BF16),
             pltpu.VMEM((ROW_BLOCK, 4 * hidden), F32),
+            weight_sems,
             weight_sems,
         ],
         grid=(rows // ROW_BLOCK,),
@@ -870,16 +875,11 @@
     dq_t, dkv_two = attend_back(blocks // 2, blocks, after(dctx, ffn_away), dq_t)
     ffn_second = ffn_grad.second(dkv_two)
 
-    six = sums_rows[:6]
-    six = six + g.swap(six, "c")
-    hidden_sums = hidden_sums[0].reshape(2, 2, hidden)
-    hidden_sums = hidden_sums[:, 0] + g.swap(hidden_sums[:, 1], "c")
-    vector = jnp.concatenate([jnp.stack([six, six]), hidden_sums[:, None]], axis=1)
     *arrays, vector, dqkv = call(
         partial(projection_grad, g.nz),
         Scatter.shapes(g, shard, 2 * lanes, SPARE) + [shape_of((2, 8, width), F32), shape_of((seq, 3 * lanes), BF16)],
-        [meta, token_t, out_grad, after(dq_t, ffn_second), dkv_one, dkv_two, vector],
-        in_specs=[SMEM] + [VMEM] * 6,
+        [meta, token_t, out_grad, after(dq_t, ffn_second), dkv_one, dkv_two, sums, g.swap(sums, "c")],
+        in_specs=[SMEM] + [VMEM] * 7,
         scratch=[pltpu.VMEM((2, width // 2, 2 * lanes), BF16)],
         flops=2 * seq * width * 3 * lanes,
         name="projection_grad",

time: 296 us -> 293 us (0.990)
    ppermute x31 -> x30, starting transfers between devices: 32.6 us -> 29.8 us  [swap(): return lax.ppermute(array, axis, [(i, i ^ r) for i in range(size)])]
    ppermute x31 -> x30, waiting for transfers between devices: 54 us -> 56.6 us  [swap(): return lax.ppermute(array, axis, [(i, i ^ r) for i in range(size)])]
  transfers between devices with their start and end apart: 32 -> 31, of which waited for: 16 -> 16; matrix products, arithmetic and copies ran while one was open for 4% -> 3% of each run, Pallas kernels for 45% -> 43%
where the time goes in v5:
time: 293 us
  Pallas kernels  172 us (59%)
  waiting for transfers between devices  57.3 us (20%)
  starting transfers between devices  29.9 us (10%)
  between operations  14.8 us (5%)
  local copies, waits for them, and re-layouts  13.6 us (5%)
  other arithmetic  5.18 us (2%)
    pallas_call x16, Pallas kernels, call(): pl.pallas_call(body, grid=grid, out_shape=outs, in_specs=in_specs or [VME...  172 us
    ppermute x30, waiting for transfers between devices, swap(): return lax.ppermute(array, axis, [(i, i ^ r) for i in range(size)])  56.6 us
    ppermute x30, starting transfers between devices, swap(): return lax.ppermute(array, axis, [(i, i ^ r) for i in range(size)])  29.8 us
  transfers between devices with their start and end apart: 31, of which 16 were waited for; matrix products, arithmetic and copies ran while one was open for 3% of the time, Pallas kernels for 43%

profile of v5, /device:TPU:0, one launch (start us, length us, event | category | flops | bytes accessed | tf_op | source)
XLA Modules:
  0.0 293.1 jit_solution(13971141433437016806)
XLA Ops:
  8.5 1.8 concatenate.13
  10.4 5.1 %collective-permute-start.2 = (bf16[96,640]{1,0:T(8,128)(2,1)S(1)}, bf16[96,640]{1,0:T(8,128)(2,1)}, u32[]{:S(2)}, u32[]{:S(2)}) collective-permute-start(bf16[96,640]{1,0:T(8,128)(2,1)S(1)} %concatenate.12), channel_id=1, source_target_pairs={{0,24},{8,16},{16,8},{24,0},{1,25},{9,17},{17,9},{25,1},{2,26},{10... | collective-permute-start | bytes 368648 | tf_op jit(solution)/shard_map/ppermute | solution.py:70
  18.0 2.0 collective-permute-done.3
  22.3 3.7 %collective-permute-done.1 = bf16[96,640]{1,0:T(8,128)(2,1)} collective-permute-done((bf16[96,640]{1,0:T(8,128)(2,1)S(1)}, bf16[96,640]{1,0:T(8,128)(2,1)}, u32[]{:S(2)}, u32[]{:S(2)}) %collective-permute-start.1) | collective-permute-done | bytes 122912 | tf_op jit(solution)/shard_map/ppermute | solution.py:70
  33.7 1.7 copy-done.3
  42.1 14.2 %collective-permute-done.9.refs_3_ = bf16[2,4,48,640]{3,2,1,0:T(8,128)(2,1)S(1)} collective-permute-done((bf16[2,4,48,640]{3,2,1,0:T(8,128)(2,1)S(1)}, bf16[2,4,48,640]{3,2,1,0:T(8,128)(2,1)S(1)}, u32[]{:S(2)}, u32[]{:S(2)}) %collective-permute-start.9) | collective-permute-done | bytes 491552 | tf_op jit(solution)/shard_map/ppermute | solution.py:70
  57.3 47.4 %heads_forward.1 = (bf16[2048,384]{1,0:T(8,128)(2,1)}, bf16[2048,384]{1,0:T(8,128)(2,1)}, bf16[2048,384]{1,0:T(8,128)(2,1)}, bf16[768,1152]{1,0:T(8,128)(2,1)}, ...) custom-call(s32[3]{0:T(128)} %copy-done.10, s32[8]{0:T(128)} %get-tuple-element.195.lows, ...), custom_call_target="tpu_custom_call" | custom-call | flops 10066329600 | bytes 13249612 | tf_op jit(solution)/shard_map/heads_forward/pallas_call | solution.py:33
  108.1 36.9 %rows_step.1 = (bf16[1024,768]{1,0:T(8,128)(2,1)}, f32[1024,768]{1,0:T(8,128)}, bf16[1024,768]{1,0:T(8,128)(2,1)}, bf16[1024,3072]{1,0:T(8,128)(2,1)}, bf16[1024...) custom-call(s32[3]{0:T(128)} %copy-done.10, ...), custom_call_target="tpu_custom_call" | custom-call | flops 20535312384 | bytes 38424588 | tf_op jit(solution)/shard_map/rows_step/pallas_call | solution.py:33
  145.3 9.2 %grad_for_partner.1 = (bf16[2,768,768]{2,1,0:T(8,128)(2,1)}, bf16[2,768,768]{2,1,0:T(8,128)(2,1)}) custom-call(bf16[768,1024]{1,0:T(8,128)(2,1)} %get-tuple-element.105.df_t, bf16[768,1024]{1,0:T(8,128)(2,1)} %get-tuple-element.106.low_t, bf16[1024,3072]{1,0:T(8,128)(2,1)} %get-tuple-element.107.act_one.act_two, ...), custom_call_target="tpu_custom_call" | custom-call | flops 4831838208 | bytes 33030144 | tf_op jit(solution)/shard_map/grad_for_partner/pallas_call | solution.py:33
  155.7 10.0 %heads_back_start.1 = (bf16[2048,384]{1,0:T(8,128)(2,1)}, f32[8,8,256]{2,1,0:T(8,128)}, f32[768,384]{1,0:T(8,128)}) custom-call(s32[3]{0:T(128)} %copy-done.10, bf16[1024,768]{1,0:T(8,128)(2,1)} %get-tuple-element.97.da_own, bf16[1024,768]{1,0:T(8,128)(2,1)} %copy-done.36, bf16[1024,384]{1,0:T(8,128)(2,1)} %get-tuple-element.94.ctx_own, ...), custom_call_target="tpu_custom_call" | custom-call | flops 2415919104 | bytes 8126476 | tf_op jit(solution)/shard_map/heads_back_start/pallas_call | solution.py:33
  165.8 8.3 %grad_for_chip.1 = (bf16[2,384,768]{2,1,0:T(8,128)(2,1)S(1)}, bf16[2,384,768]{2,1,0:T(8,128)(2,1)S(1)}, bf16[2,384,768]{2,1,0:T(8,128)(2,1)S(1)}, bf16[2,384,768]{2,1,0:T(8,128)(2,1)S(1)}) custom-call(s32[3]{0:T(128)S(1)} %copy-done.11, bf16[768,1024]{1,0:T(8,128)(2,1)S(1)} %copy-done.1, bf16[768,1024]{1,0:T(8,128)(2,1)S(1)} %copy-done.2, ...), custom_call_target="tpu_custom_call" | custom-call | flops 4831838208 | bytes 37748748 | tf_op jit(solution)/shard_map/grad_for_chip/pallas_call | solution.py:33
  177.8 19.1 %attention_backward.2 = (f32[3,128,2048]{2,1,0:T(8,128)S(1)}, bf16[1024,768]{1,0:T(8,128)(2,1)S(1)}) custom-call(s32[3]{0:T(128)S(1)} %copy-done.11, s32[8]{0:T(128)S(1)} %copy-done.13, s32[8]{0:T(128)S(1)} %copy-done.12, bf16[2048,384]{1,0:T(8,128)(2,1)S(1)} %copy-done.18, bf16[2048,384]{1,0:T(8,128)(2,1)S(1)} %copy-done.20, ...), custom_call_target="tpu_custom_call" | custom-call | flops 8053063680 | bytes 11149388 | tf_op jit(solution)/shard_map/attention_backward/pallas_call | solution.py:33
  196.9 5.5 %collective-permute-done.14.got_x = bf16[2,384,768]{2,1,0:T(8,128)(2,1)S(1)} collective-permute-done((bf16[2,384,768]{2,1,0:T(8,128)(2,1)S(1)}, bf16[2,384,768]{2,1,0:T(8,128)(2,1)S(1)}, u32[]{:S(2)}, u32[]{:S(2)}) %collective-permute-start.14) | collective-permute-done | bytes 1179680 | tf_op jit(solution)/shard_map/ppermute | solution.py:70
  206.1 23.3 %attention_backward.3 = (f32[3,128,2048]{2,1,0:T(8,128)S(1)}, bf16[1024,768]{1,0:T(8,128)(2,1)S(1)}) custom-call(s32[3]{0:T(128)S(1)} %copy-done.11, s32[8]{0:T(128)S(1)} %copy-done.13, s32[8]{0:T(128)S(1)} %copy-done.12, bf16[2048,384]{1,0:T(8,128)(2,1)S(1)} %copy-done.19, bf16[2048,384]{1,0:T(8,128)(2,1)S(1)} %copy-done.21, ...), custom_call_target="tpu_custom_call" | custom-call | flops 8053063680 | bytes 14295116 | tf_op jit(solution)/shard_map/attention_backward/pallas_call | solution.py:33
  230.2 4.1 %collective-permute-start.23 = (bf16[2,96,768]{2,1,0:T(8,128)(2,1)S(1)}, bf16[2,96,768]{2,1,0:T(8,128)(2,1)S(1)}, u32[]{:S(2)}, u32[]{:S(2)}) collective-permute-start(bf16[2,96,768]{2,1,0:T(8,128)(2,1)S(1)} %get-tuple-element.134), channel_id=1, source_target_pairs={{0,24},{8,16},{16,8},{24,0},{1,25},{9,17},{17,9},{25,1},{2,26},{10... | collective-permute-start | bytes 884744 | tf_op jit(solution)/shard_map/ppermute | solution.py:70
  234.3 7.3 %projection_grad.1 = (bf16[384,768]{1,0:T(8,128)(2,1)S(1)}, bf16[400,768]{1,0:T(8,128)(2,1)S(1)}, bf16[384,768]{1,0:T(8,128)(2,1)S(1)}, bf16[384,768]{1,0:T(8,12...) custom-call(s32[3]{0:T(128)S(1)} %copy-done.11, bf16[768,2048]{1,0:T(8,128)(2,1)S(1)} %copy-done.4, ...), custom_call_target="tpu_custom_call" | custom-call | flops 3623878656 | bytes 17866764 | tf_op jit(solution)/shard_map/projection_grad/pallas_call | solution.py:33
  241.8 2.8 input_grad_other.1
  244.6 8.8 %collective-permute-done.22 = bf16[2,96,768]{2,1,0:T(8,128)(2,1)S(1)} collective-permute-done((bf16[2,96,768]{2,1,0:T(8,128)(2,1)S(1)}, bf16[2,96,768]{2,1,0:T(8,128)(2,1)S(1)}, u32[]{:S(2)}, u32[]{:S(2)}) %collective-permute-start.22) | collective-permute-done | bytes 294944 | tf_op jit(solution)/shard_map/ppermute | solution.py:70
  255.7 1.7 collective-permute-start.25
  259.1 4.6 %input_grad_own.1 = f32[1024,768]{1,0:T(8,128)} custom-call(s32[3]{0:T(128)S(1)} %copy-done.11, bf16[2048,1152]{1,0:T(8,128)(2,1)S(1)} %get-tuple-element.137.dqkv, bf16[768,1152]{1,0:T(8,128)(2,1)S(1)} %copy-done, f32[1024,768]{1,0:T(8,128)S(1)} %copy-done.5, bf16[1024,768]{1,0:T(8,128)(2,1)S(1)} %collective-permute-done.24.arrived), custom_call_target="tpu_custom_call" | custom-call | flops 1811939328 | bytes 14352396 | tf_op jit(solution)/shard_map/input_grad_own/pallas_call | solution.py:33
  263.7 2.9 collective-permute-done.26.last_y
  266.8 2.4 collective-permute-start.27
  272.5 2.9 collective-permute-done.27.refs_0_
  275.4 9.3 %collective-permute-done.28.refs_1_ = bf16[112,768]{1,0:T(8,128)(2,1)S(1)} collective-permute-done((bf16[112,768]{1,0:T(8,128)(2,1)S(1)}, bf16[112,768]{1,0:T(8,128)(2,1)S(1)}, u32[]{:S(2)}, u32[]{:S(2)}) %collective-permute-start.28) | collective-permute-done | bytes 172064 | tf_op jit(solution)/shard_map/ppermute | solution.py:70
  (180 shorter events, 43.2 us)
Async XLA Ops:
  7.2 100.7 %all-gather.3.cloned.1.call-start = ((), (), s32[]{:S(2)}) async-start(), calls=%async_computation | async-start | bytes 11354112 | tf_op jit(solution)/shard_map/all_gather | solution.py:146
  10.4 11.1 %collective-permute-start.2 = (bf16[96,640]{1,0:T(8,128)(2,1)S(1)}, bf16[96,640]{1,0:T(8,128)(2,1)}, u32[]{:S(2)}, u32[]{:S(2)}) collective-permute-start(bf16[96,640]{1,0:T(8,128)(2,1)S(1)} %concatenate.12), channel_id=1, source_target_pairs={{0,24},{8,16},{16,8},{24,0},{1,25},{9,17},{17,9},{25,1},{2,26},{10... | collective-permute-start | bytes 368648 | tf_op jit(solution)/shard_map/ppermute | solution.py:70
  15.5 10.5 %collective-permute-start.1 = (bf16[96,640]{1,0:T(8,128)(2,1)S(1)}, bf16[96,640]{1,0:T(8,128)(2,1)}, u32[]{:S(2)}, u32[]{:S(2)}) collective-permute-start(bf16[96,640]{1,0:T(8,128)(2,1)S(1)} %concatenate.12), channel_id=1, source_target_pairs={{0,16},{8,24},{16,0},{24,8},{1,17},{9,25},{17,1},{25,9},{2,18},{10... | collective-permute-start | bytes 368648 | tf_op jit(solution)/shard_map/ppermute | solution.py:70
  15.5 11.4 %collective-permute-start = (bf16[96,640]{1,0:T(8,128)(2,1)S(1)}, bf16[96,640]{1,0:T(8,128)(2,1)S(1)}, u32[]{:S(2)}, u32[]{:S(2)}) collective-permute-start(bf16[96,640]{1,0:T(8,128)(2,1)S(1)} %concatenate.12), channel_id=1, source_target_pairs={{0,8},{8,0},{16,24},{24,16},{1,9},{9,1},{17,25},{25,17},{2,10},{10... | collective-permute-start | bytes 368648 | tf_op jit(solution)/shard_map/ppermute | solution.py:70
  17.9 14.3 %collective-permute-start.7 = (bf16[1024,768]{1,0:T(8,128)(2,1)S(1)}, bf16[1024,768]{1,0:T(8,128)(2,1)S(1)}, u32[]{:S(2)}, u32[]{:S(2)}) collective-permute-start(bf16[1024,768]{1,0:T(8,128)(2,1)S(1)} %copy-done.6), channel_id=1, source_target_pairs={{0,1},{1,0},{2,3},{3,2},{4,5},{5,4},{6,7},{7,6},{8,9},{9,8},{10,11... | collective-permute-start | bytes 4718600 | tf_op jit(solution)/shard_map/ppermute | solution.py:70
  37.3 19.0 %collective-permute-start.9 = (bf16[2,4,48,640]{3,2,1,0:T(8,128)(2,1)S(1)}, bf16[2,4,48,640]{3,2,1,0:T(8,128)(2,1)S(1)}, u32[]{:S(2)}, u32[]{:S(2)}) collective-permute-start(bf16[2,4,48,640]{3,2,1,0:T(8,128)(2,1)S(1)} %pad_maximum_fusion.1.refs_2_), channel_id=1, source_target_pairs={{0,2},{2,0},{1,3},{3,1},{4,6},{6,4},{5,7},{7,5},{8,10},{10,8},{9,1... | collective-permute-start | bytes 1474568 | tf_op jit(solution)/shard_map/ppermute | solution.py:70
  38.9 17.4 %collective-permute-start.8 = (bf16[2,4,48,640]{3,2,1,0:T(8,128)(2,1)S(1)}, bf16[2,4,48,640]{3,2,1,0:T(8,128)(2,1)S(1)}, u32[]{:S(2)}, u32[]{:S(2)}) collective-permute-start(bf16[2,4,48,640]{3,2,1,0:T(8,128)(2,1)S(1)} %pad_maximum_fusion.refs_0_), channel_id=1, source_target_pairs={{0,4},{4,0},{1,5},{5,1},{2,6},{6,2},{3,7},{7,3},{8,12},{12,8},{9,1... | collective-permute-start | bytes 1474568 | tf_op jit(solution)/shard_map/ppermute | solution.py:70
  145.1 9.5 %collective-permute-start.11 = (bf16[1024,768]{1,0:T(8,128)(2,1)}, bf16[1024,768]{1,0:T(8,128)(2,1)S(1)}, u32[]{:S(2)}, u32[]{:S(2)}) collective-permute-start(bf16[1024,768]{1,0:T(8,128)(2,1)} %get-tuple-element.97.da_own), channel_id=1, source_target_pairs={{0,1},{1,0},{2,3},{3,2},{4,5},{5,4},{6,7},{7,6},{8,9},{9,8},{10,11... | collective-permute-start | bytes 4718600 | tf_op jit(solution)/shard_map/ppermute | solution.py:70
  154.5 11.2 %collective-permute-start.12 = (bf16[2,768,768]{2,1,0:T(8,128)(2,1)}, bf16[2,768,768]{2,1,0:T(8,128)(2,1)}, u32[]{:S(2)}, u32[]{:S(2)}) collective-permute-start(bf16[2,768,768]{2,1,0:T(8,128)(2,1)} %get-tuple-element.111), channel_id=1, source_target_pairs={{0,1},{1,0},{2,3},{3,2},{4,5},{5,4},{6,7},{7,6},{8,9},{9,8},{10,11... | collective-permute-start | bytes 7077896 | tf_op jit(solution)/shard_map/ppermute | solution.py:70
  154.9 10.9 %collective-permute-start.13 = (bf16[2,768,768]{2,1,0:T(8,128)(2,1)}, bf16[2,768,768]{2,1,0:T(8,128)(2,1)}, u32[]{:S(2)}, u32[]{:S(2)}) collective-permute-start(bf16[2,768,768]{2,1,0:T(8,128)(2,1)} %get-tuple-element.112), channel_id=1, source_target_pairs={{0,1},{1,0},{2,3},{3,2},{4,5},{5,4},{6,7},{7,6},{8,9},{9,8},{10,11... | collective-permute-start | bytes 7077896 | tf_op jit(solution)/shard_map/ppermute | solution.py:70
  174.2 28.2 %collective-permute-start.14 = (bf16[2,384,768]{2,1,0:T(8,128)(2,1)S(1)}, bf16[2,384,768]{2,1,0:T(8,128)(2,1)S(1)}, u32[]{:S(2)}, u32[]{:S(2)}) collective-permute-start(bf16[2,384,768]{2,1,0:T(8,128)(2,1)S(1)} %get-tuple-element.114), channel_id=1, source_target_pairs={{0,2},{2,0},{1,3},{3,1},{4,6},{6,4},{5,7},{7,5},{8,10},{10,8},{9,1... | collective-permute-start | bytes 3538952 | tf_op jit(solution)/shard_map/ppermute | solution.py:70
  175.5 27.9 %collective-permute-start.15 = (bf16[2,384,768]{2,1,0:T(8,128)(2,1)S(1)}, bf16[2,384,768]{2,1,0:T(8,128)(2,1)S(1)}, u32[]{:S(2)}, u32[]{:S(2)}) collective-permute-start(bf16[2,384,768]{2,1,0:T(8,128)(2,1)S(1)} %get-tuple-element.115), channel_id=1, source_target_pairs={{0,4},{4,0},{1,5},{5,1},{2,6},{6,2},{3,7},{7,3},{8,12},{12,8},{9,1... | collective-permute-start | bytes 3538952 | tf_op jit(solution)/shard_map/ppermute | solution.py:70
  176.3 58.0 %collective-permute-start.18 = (f32[16,768]{1,0:T(8,128)S(1)}, f32[16,768]{1,0:T(8,128)S(1)}, u32[]{:S(2)}, u32[]{:S(2)}) collective-permute-start(f32[16,768]{1,0:T(8,128)S(1)} %copy-done.14), channel_id=1, source_target_pairs={{0,1},{1,0},{2,3},{3,2},{4,5},{5,4},{6,7},{7,6},{8,9},{9,8},{10,11... | collective-permute-start | bytes 147464 | tf_op jit(solution)/shard_map/ppermute | solution.py:70
  203.6 25.8 %collective-permute-start.16 = (bf16[2,192,768]{2,1,0:T(8,128)(2,1)S(1)}, bf16[2,192,768]{2,1,0:T(8,128)(2,1)S(1)}, u32[]{:S(2)}, u32[]{:S(2)}) collective-permute-start(bf16[2,192,768]{2,1,0:T(8,128)(2,1)S(1)} %get-tuple-element.123), channel_id=1, source_target_pairs={{0,4},{4,0},{1,5},{5,1},{2,6},{6,2},{3,7},{7,3},{8,12},{12,8},{9,1... | collective-permute-start | bytes 1769480 | tf_op jit(solution)/shard_map/ppermute | solution.py:70
  204.5 24.9 %collective-permute-start.17 = (bf16[2,192,768]{2,1,0:T(8,128)(2,1)S(1)}, bf16[2,192,768]{2,1,0:T(8,128)(2,1)S(1)}, u32[]{:S(2)}, u32[]{:S(2)}) collective-permute-start(bf16[2,192,768]{2,1,0:T(8,128)(2,1)S(1)} %get-tuple-element.124), channel_id=1, source_target_pairs={{0,2},{2,0},{1,3},{3,1},{4,6},{6,4},{5,7},{7,5},{8,10},{10,8},{9,1... | collective-permute-start | bytes 1769480 | tf_op jit(solution)/shard_map/ppermute | solution.py:70
  229.8 14.8 %collective-permute-start.21 = (bf16[2,96,768]{2,1,0:T(8,128)(2,1)S(1)}, bf16[2,96,768]{2,1,0:T(8,128)(2,1)S(1)}, u32[]{:S(2)}, u32[]{:S(2)}) collective-permute-start(bf16[2,96,768]{2,1,0:T(8,128)(2,1)S(1)} %get-tuple-element.132), channel_id=1, source_target_pairs={{0,8},{8,0},{16,24},{24,16},{1,9},{9,1},{17,25},{25,17},{2,10},{10... | collective-permute-start | bytes 884744 | tf_op jit(solution)/shard_map/ppermute | solution.py:70
  230.2 23.2 %collective-permute-start.22 = (bf16[2,96,768]{2,1,0:T(8,128)(2,1)S(1)}, bf16[2,96,768]{2,1,0:T(8,128)(2,1)S(1)}, u32[]{:S(2)}, u32[]{:S(2)}) collective-permute-start(bf16[2,96,768]{2,1,0:T(8,128)(2,1)S(1)} %get-tuple-element.133), channel_id=1, source_target_pairs={{0,16},{8,24},{16,0},{24,8},{1,17},{9,25},{17,1},{25,9},{2,18},{10... | collective-permute-start | bytes 884744 | tf_op jit(solution)/shard_map/ppermute | solution.py:70
  230.2 23.2 %collective-permute-start.23 = (bf16[2,96,768]{2,1,0:T(8,128)(2,1)S(1)}, bf16[2,96,768]{2,1,0:T(8,128)(2,1)S(1)}, u32[]{:S(2)}, u32[]{:S(2)}) collective-permute-start(bf16[2,96,768]{2,1,0:T(8,128)(2,1)S(1)} %get-tuple-element.134), channel_id=1, source_target_pairs={{0,24},{8,16},{16,8},{24,0},{1,25},{9,17},{17,9},{25,1},{2,26},{10... | collective-permute-start | bytes 884744 | tf_op jit(solution)/shard_map/ppermute | solution.py:70
  241.7 13.2 %collective-permute-start.20 = (bf16[384,768]{1,0:T(8,128)(2,1)S(1)}, bf16[384,768]{1,0:T(8,128)(2,1)S(1)}, u32[]{:S(2)}, u32[]{:S(2)}) collective-permute-start(bf16[384,768]{1,0:T(8,128)(2,1)S(1)} %get-tuple-element.142), channel_id=1, source_target_pairs={{0,4},{4,0},{1,5},{5,1},{2,6},{6,2},{3,7},{7,3},{8,12},{12,8},{9,1... | collective-permute-start | bytes 1769480 | tf_op jit(solution)/shard_map/ppermute | solution.py:70
  241.7 13.8 %collective-permute-start.19 = (bf16[400,768]{1,0:T(8,128)(2,1)S(1)}, bf16[400,768]{1,0:T(8,128)(2,1)S(1)}, u32[]{:S(2)}, u32[]{:S(2)}) collective-permute-start(bf16[400,768]{1,0:T(8,128)(2,1)S(1)} %get-tuple-element.141), channel_id=1, source_target_pairs={{0,2},{2,0},{1,3},{3,1},{4,6},{6,4},{5,7},{7,5},{8,10},{10,8},{9,1... | collective-permute-start | bytes 1843208 | tf_op jit(solution)/shard_map/ppermute | solution.py:70
  255.7 10.8 %collective-permute-start.25 = (bf16[208,768]{1,0:T(8,128)(2,1)S(1)}, bf16[208,768]{1,0:T(8,128)(2,1)S(1)}, u32[]{:S(2)}, u32[]{:S(2)}) collective-permute-start(bf16[208,768]{1,0:T(8,128)(2,1)S(1)} %get-tuple-element.150), channel_id=1, source_target_pairs={{0,4},{4,0},{1,5},{5,1},{2,6},{6,2},{3,7},{7,3},{8,12},{12,8},{9,1... | collective-permute-start | bytes 958472 | tf_op jit(solution)/shard_map/ppermute | solution.py:70
  257.5 9.1 %collective-permute-start.26 = (bf16[192,768]{1,0:T(8,128)(2,1)S(1)}, bf16[192,768]{1,0:T(8,128)(2,1)S(1)}, u32[]{:S(2)}, u32[]{:S(2)}) collective-permute-start(bf16[192,768]{1,0:T(8,128)(2,1)S(1)} %get-tuple-element.151), channel_id=1, source_target_pairs={{0,2},{2,0},{1,3},{3,1},{4,6},{6,4},{5,7},{7,5},{8,10},{10,8},{9,1... | collective-permute-start | bytes 884744 | tf_op jit(solution)/shard_map/ppermute | solution.py:70
  269.2 15.5 %collective-permute-start.28 = (bf16[112,768]{1,0:T(8,128)(2,1)S(1)}, bf16[112,768]{1,0:T(8,128)(2,1)S(1)}, u32[]{:S(2)}, u32[]{:S(2)}) collective-permute-start(bf16[112,768]{1,0:T(8,128)(2,1)S(1)} %get-tuple-element.159), channel_id=1, source_target_pairs={{0,16},{8,24},{16,0},{24,8},{1,17},{9,25},{17,1},{25,9},{2,18},{10... | collective-permute-start | bytes 516104 | tf_op jit(solution)/shard_map/ppermute | solution.py:70
  270.2 14.5 %collective-permute-start.29 = (bf16[112,768]{1,0:T(8,128)(2,1)S(1)}, bf16[112,768]{1,0:T(8,128)(2,1)S(1)}, u32[]{:S(2)}, u32[]{:S(2)}) collective-permute-start(bf16[112,768]{1,0:T(8,128)(2,1)S(1)} %get-tuple-element.160), channel_id=1, source_target_pairs={{0,24},{8,16},{16,8},{24,0},{1,25},{9,17},{17,9},{25,1},{2,26},{10... | collective-permute-start | bytes 516104 | tf_op jit(solution)/shard_map/ppermute | solution.py:70
  (47 other events, 570.6 us)
Sparse Core Ops, SparseCore 0:
  10.9 96.9 all-gather.2

commit v6 on v5

--- a/solution.py
+++ b/solution.py
@@ -228,7 +228,7 @@
 SUM_VMEM = 12
 VM_HEADS = 60
 VM_ROWS = 60
-VM_GRAD = 40
+VM_GRAD = 28
 VM_PART = 60
 VM_START = 60
 VM_BACK = 36

time: 293 us -> 300 us (1.024)
  waiting for transfers between devices: 57.3 us -> 47.6 us
  local copies, waits for them, and re-layouts: 13.6 us -> 21.9 us
  starting transfers between devices: 29.9 us -> 36.3 us
    ppermute x30, waiting for transfers between devices: 56.6 us -> 47.6 us  [swap(): return lax.ppermute(array, axis, [(i, i ^ r) for i in range(size)])]
    ppermute x30, starting transfers between devices: 29.8 us -> 36.2 us  [swap(): return lax.ppermute(array, axis, [(i, i ^ r) for i in range(size)])]
    unnamed x82 -> x84, local copies, waits for them, and re-layouts: 5.61 us -> 11.8 us
  transfers between devices with their start and end apart: 31 -> 31, of which waited for: 16 -> 14; matrix products, arithmetic and copies ran while one was open for 3% -> 4% of each run, Pallas kernels for 43% -> 43%
where the time goes in v6:
time: 300 us
  Pallas kernels  174 us (58%)
  waiting for transfers between devices  47.6 us (16%)
  starting transfers between devices  36.3 us (12%)
  local copies, waits for them, and re-layouts  21.9 us (7%)
  between operations  14.7 us (5%)
  other arithmetic  5.17 us (2%)
    pallas_call x16, Pallas kernels, call(): pl.pallas_call(body, grid=grid, out_shape=outs, in_specs=in_specs or [VME...  174 us
    ppermute x30, waiting for transfers between devices, swap(): return lax.ppermute(array, axis, [(i, i ^ r) for i in range(size)])  47.6 us
    ppermute x30, starting transfers between devices, swap(): return lax.ppermute(array, axis, [(i, i ^ r) for i in range(size)])  36.2 us
    unnamed x84, local copies, waits for them, and re-layouts  11.8 us
  transfers between devices with their start and end apart: 31, of which 14 were waited for; matrix products, arithmetic and copies ran while one was open for 4% of the time, Pallas kernels for 43%

profile of v6, /device:TPU:0, one launch (start us, length us, event | category | flops | bytes accessed | tf_op | source)
XLA Modules:
  0.0 299.8 jit_solution(16743250553865957817)
XLA Ops:
  10.4 5.1 %collective-permute-start.2 = (bf16[96,640]{1,0:T(8,128)(2,1)S(1)}, bf16[96,640]{1,0:T(8,128)(2,1)}, u32[]{:S(2)}, u32[]{:S(2)}) collective-permute-start(bf16[96,640]{1,0:T(8,128)(2,1)S(1)} %concatenate.12), channel_id=1, source_target_pairs={{0,24},{8,16},{16,8},{24,0},{1,25},{9,17},{17,9},{25,1},{2,26},{10... | collective-permute-start | bytes 368648 | tf_op jit(solution)/shard_map/ppermute | solution.py:70
  42.0 15.2 %collective-permute-done.9.refs_3_ = bf16[2,4,48,640]{3,2,1,0:T(8,128)(2,1)S(1)} collective-permute-done((bf16[2,4,48,640]{3,2,1,0:T(8,128)(2,1)S(1)}, bf16[2,4,48,640]{3,2,1,0:T(8,128)(2,1)S(1)}, u32[]{:S(2)}, u32[]{:S(2)}) %collective-permute-start.9) | collective-permute-done | bytes 491552 | tf_op jit(solution)/shard_map/ppermute | solution.py:70
  58.2 47.3 %heads_forward.1 = (bf16[2048,384]{1,0:T(8,128)(2,1)}, bf16[2048,384]{1,0:T(8,128)(2,1)}, bf16[2048,384]{1,0:T(8,128)(2,1)}, bf16[768,1152]{1,0:T(8,128)(2,1)}, ...) custom-call(s32[3]{0:T(128)} %copy-done.12, s32[8]{0:T(128)} %get-tuple-element.195.lows, ...), custom_call_target="tpu_custom_call" | custom-call | flops 10066329600 | bytes 13249612 | tf_op jit(solution)/shard_map/heads_forward/pallas_call | solution.py:33
  109.1 36.9 %rows_step.1 = (bf16[1024,768]{1,0:T(8,128)(2,1)}, f32[1024,768]{1,0:T(8,128)}, bf16[1024,768]{1,0:T(8,128)(2,1)}, bf16[1024,3072]{1,0:T(8,128)(2,1)}, bf16[1024...) custom-call(s32[3]{0:T(128)} %copy-done.12, ...), custom_call_target="tpu_custom_call" | custom-call | flops 20535312384 | bytes 38424588 | tf_op jit(solution)/shard_map/rows_step/pallas_call | solution.py:33
  146.5 9.5 %grad_for_partner.1 = (bf16[2,768,768]{2,1,0:T(8,128)(2,1)}, bf16[2,768,768]{2,1,0:T(8,128)(2,1)}) custom-call(bf16[768,1024]{1,0:T(8,128)(2,1)} %get-tuple-element.105.df_t, bf16[768,1024]{1,0:T(8,128)(2,1)} %get-tuple-element.106.low_t, bf16[1024,3072]{1,0:T(8,128)(2,1)} %get-tuple-element.107.act_one.act_two, ...), custom_call_target="tpu_custom_call" | custom-call | flops 4831838208 | bytes 33030144 | tf_op jit(solution)/shard_map/grad_for_partner/pallas_call | solution.py:33
  157.2 10.0 %heads_back_start.1 = (bf16[2048,384]{1,0:T(8,128)(2,1)}, f32[8,8,256]{2,1,0:T(8,128)}, f32[768,384]{1,0:T(8,128)}) custom-call(s32[3]{0:T(128)} %copy-done.12, bf16[1024,768]{1,0:T(8,128)(2,1)} %get-tuple-element.97.da_own, bf16[1024,768]{1,0:T(8,128)(2,1)} %copy-done.37, bf16[1024,384]{1,0:T(8,128)(2,1)} %get-tuple-element.94.ctx_own, ...), custom_call_target="tpu_custom_call" | custom-call | flops 2415919104 | bytes 8126476 | tf_op jit(solution)/shard_map/heads_back_start/pallas_call | solution.py:33
  167.2 2.8 copy-done
  170.0 2.8 copy-done.1
  172.8 8.3 %grad_for_chip.1 = (bf16[2,384,768]{2,1,0:T(8,128)(2,1)S(1)}, bf16[2,384,768]{2,1,0:T(8,128)(2,1)S(1)}, bf16[2,384,768]{2,1,0:T(8,128)(2,1)S(1)}, bf16[2,384,768]{2,1,0:T(8,128)(2,1)S(1)}) custom-call(s32[3]{0:T(128)S(1)} %copy-done.13, bf16[768,1024]{1,0:T(8,128)(2,1)S(1)} %copy-done.3, bf16[768,1024]{1,0:T(8,128)(2,1)S(1)} %copy-done.4, ...), custom_call_target="tpu_custom_call" | custom-call | flops 4831838208 | bytes 37748748 | tf_op jit(solution)/shard_map/grad_for_chip/pallas_call | solution.py:33
  183.4 24.4 %attention_backward.2 = (f32[3,128,2048]{2,1,0:T(8,128)S(1)}, bf16[1024,768]{1,0:T(8,128)(2,1)S(1)}) custom-call(s32[3]{0:T(128)S(1)} %copy-done.13, s32[8]{0:T(128)S(1)} %copy-done.15, s32[8]{0:T(128)S(1)} %copy-done.14, bf16[2048,384]{1,0:T(8,128)(2,1)S(1)} %copy-done.20, bf16[2048,384]{1,0:T(8,128)(2,1)S(1)} %copy-done.22, ...), custom_call_target="tpu_custom_call" | custom-call | flops 8053063680 | bytes 11149388 | tf_op jit(solution)/shard_map/attention_backward/pallas_call | solution.py:33
  212.1 19.6 %attention_backward.3 = (f32[3,128,2048]{2,1,0:T(8,128)S(1)}, bf16[1024,768]{1,0:T(8,128)(2,1)S(1)}) custom-call(s32[3]{0:T(128)S(1)} %copy-done.13, s32[8]{0:T(128)S(1)} %copy-done.15, s32[8]{0:T(128)S(1)} %copy-done.14, bf16[2048,384]{1,0:T(8,128)(2,1)S(1)} %copy-done.21, bf16[2048,384]{1,0:T(8,128)(2,1)S(1)} %copy-done.23, ...), custom_call_target="tpu_custom_call" | custom-call | flops 8053063680 | bytes 14295116 | tf_op jit(solution)/shard_map/attention_backward/pallas_call | solution.py:33
  232.3 2.8 collective-permute-start.22
  236.7 7.3 %projection_grad.1 = (bf16[384,768]{1,0:T(8,128)(2,1)S(1)}, bf16[400,768]{1,0:T(8,128)(2,1)S(1)}, bf16[384,768]{1,0:T(8,128)(2,1)S(1)}, bf16[384,768]{1,0:T(8,12...) custom-call(s32[3]{0:T(128)S(1)} %copy-done.13, bf16[768,2048]{1,0:T(8,128)(2,1)S(1)} %copy-done.6, ...), custom_call_target="tpu_custom_call" | custom-call | flops 3623878656 | bytes 17866764 | tf_op jit(solution)/shard_map/projection_grad/pallas_call | solution.py:33
  244.0 3.5 %collective-permute-start.20 = (bf16[384,768]{1,0:T(8,128)(2,1)S(1)}, bf16[384,768]{1,0:T(8,128)(2,1)S(1)}, u32[]{:S(2)}, u32[]{:S(2)}) collective-permute-start(bf16[384,768]{1,0:T(8,128)(2,1)S(1)} %get-tuple-element.142), channel_id=1, source_target_pairs={{0,4},{4,0},{1,5},{5,1},{2,6},{6,2},{3,7},{7,3},{8,12},{12,8},{9,1... | collective-permute-start | bytes 1769480 | tf_op jit(solution)/shard_map/ppermute | solution.py:70
  247.5 2.5 collective-permute-start.19
  250.1 2.8 input_grad_other.1
  252.9 3.0 collective-permute-done.22
  256.0 3.2 %collective-permute-done.20.got_y = bf16[384,768]{1,0:T(8,128)(2,1)S(1)} collective-permute-done((bf16[384,768]{1,0:T(8,128)(2,1)S(1)}, bf16[384,768]{1,0:T(8,128)(2,1)S(1)}, u32[]{:S(2)}, u32[]{:S(2)}) %collective-permute-start.20) | collective-permute-done | bytes 589856 | tf_op jit(solution)/shard_map/ppermute | solution.py:70
  259.2 2.8 collective-permute-done.19.got_x
  265.5 4.6 %input_grad_own.1 = f32[1024,768]{1,0:T(8,128)} custom-call(s32[3]{0:T(128)S(1)} %copy-done.13, bf16[2048,1152]{1,0:T(8,128)(2,1)S(1)} %get-tuple-element.137.dqkv, bf16[768,1152]{1,0:T(8,128)(2,1)S(1)} %copy-done.2, f32[1024,768]{1,0:T(8,128)S(1)} %copy-done.7, bf16[1024,768]{1,0:T(8,128)(2,1)S(1)} %collective-permute-done.24.arrived), custom_call_target="tpu_custom_call" | custom-call | flops 1811939328 | bytes 14352396 | tf_op jit(solution)/shard_map/input_grad_own/pallas_call | solution.py:33
  270.1 2.4 collective-permute-done.26.last_y
  272.7 3.1 %collective-permute-start.27 = (bf16[112,768]{1,0:T(8,128)(2,1)S(1)}, bf16[112,768]{1,0:T(8,128)(2,1)S(1)}, u32[]{:S(2)}, u32[]{:S(2)}) collective-permute-start(bf16[112,768]{1,0:T(8,128)(2,1)S(1)} %get-tuple-element.158), channel_id=1, source_target_pairs={{0,8},{8,0},{16,24},{24,16},{1,9},{9,1},{17,25},{25,17},{2,10},{10... | collective-permute-start | bytes 516104 | tf_op jit(solution)/shard_map/ppermute | solution.py:70
  279.1 3.4 %collective-permute-done.27.refs_0_ = bf16[112,768]{1,0:T(8,128)(2,1)S(1)} collective-permute-done((bf16[112,768]{1,0:T(8,128)(2,1)S(1)}, bf16[112,768]{1,0:T(8,128)(2,1)S(1)}, u32[]{:S(2)}, u32[]{:S(2)}) %collective-permute-start.27) | collective-permute-done | bytes 172064 | tf_op jit(solution)/shard_map/ppermute | solution.py:70
  282.6 8.9 %collective-permute-done.28.refs_1_ = bf16[112,768]{1,0:T(8,128)(2,1)S(1)} collective-permute-done((bf16[112,768]{1,0:T(8,128)(2,1)S(1)}, bf16[112,768]{1,0:T(8,128)(2,1)S(1)}, u32[]{:S(2)}, u32[]{:S(2)}) %collective-permute-start.28) | collective-permute-done | bytes 172064 | tf_op jit(solution)/shard_map/ppermute | solution.py:70
  (182 shorter events, 52.9 us)
Async XLA Ops:
  7.2 101.1 %all-gather.3.cloned.1.call-start = ((), (), s32[]{:S(2)}) async-start(), calls=%async_computation | async-start | bytes 11354112 | tf_op jit(solution)/shard_map/all_gather | solution.py:146
  10.4 12.4 %collective-permute-start.2 = (bf16[96,640]{1,0:T(8,128)(2,1)S(1)}, bf16[96,640]{1,0:T(8,128)(2,1)}, u32[]{:S(2)}, u32[]{:S(2)}) collective-permute-start(bf16[96,640]{1,0:T(8,128)(2,1)S(1)} %concatenate.12), channel_id=1, source_target_pairs={{0,24},{8,16},{16,8},{24,0},{1,25},{9,17},{17,9},{25,1},{2,26},{10... | collective-permute-start | bytes 368648 | tf_op jit(solution)/shard_map/ppermute | solution.py:70
  15.5 10.5 %collective-permute-start.1 = (bf16[96,640]{1,0:T(8,128)(2,1)S(1)}, bf16[96,640]{1,0:T(8,128)(2,1)}, u32[]{:S(2)}, u32[]{:S(2)}) collective-permute-start(bf16[96,640]{1,0:T(8,128)(2,1)S(1)} %concatenate.12), channel_id=1, source_target_pairs={{0,16},{8,24},{16,0},{24,8},{1,17},{9,25},{17,1},{25,9},{2,18},{10... | collective-permute-start | bytes 368648 | tf_op jit(solution)/shard_map/ppermute | solution.py:70
  15.5 11.4 %collective-permute-start = (bf16[96,640]{1,0:T(8,128)(2,1)S(1)}, bf16[96,640]{1,0:T(8,128)(2,1)S(1)}, u32[]{:S(2)}, u32[]{:S(2)}) collective-permute-start(bf16[96,640]{1,0:T(8,128)(2,1)S(1)} %concatenate.12), channel_id=1, source_target_pairs={{0,8},{8,0},{16,24},{24,16},{1,9},{9,1},{17,25},{25,17},{2,10},{10... | collective-permute-start | bytes 368648 | tf_op jit(solution)/shard_map/ppermute | solution.py:70
  17.9 15.0 %collective-permute-start.7 = (bf16[1024,768]{1,0:T(8,128)(2,1)S(1)}, bf16[1024,768]{1,0:T(8,128)(2,1)S(1)}, u32[]{:S(2)}, u32[]{:S(2)}) collective-permute-start(bf16[1024,768]{1,0:T(8,128)(2,1)S(1)} %copy-done.8), channel_id=1, source_target_pairs={{0,1},{1,0},{2,3},{3,2},{4,5},{5,4},{6,7},{7,6},{8,9},{9,8},{10,11... | collective-permute-start | bytes 4718600 | tf_op jit(solution)/shard_map/ppermute | solution.py:70
  37.3 20.0 %collective-permute-start.9 = (bf16[2,4,48,640]{3,2,1,0:T(8,128)(2,1)S(1)}, bf16[2,4,48,640]{3,2,1,0:T(8,128)(2,1)S(1)}, u32[]{:S(2)}, u32[]{:S(2)}) collective-permute-start(bf16[2,4,48,640]{3,2,1,0:T(8,128)(2,1)S(1)} %pad_maximum_fusion.1.refs_2_), channel_id=1, source_target_pairs={{0,2},{2,0},{1,3},{3,1},{4,6},{6,4},{5,7},{7,5},{8,10},{10,8},{9,1... | collective-permute-start | bytes 1474568 | tf_op jit(solution)/shard_map/ppermute | solution.py:70
  38.9 18.3 %collective-permute-start.8 = (bf16[2,4,48,640]{3,2,1,0:T(8,128)(2,1)S(1)}, bf16[2,4,48,640]{3,2,1,0:T(8,128)(2,1)S(1)}, u32[]{:S(2)}, u32[]{:S(2)}) collective-permute-start(bf16[2,4,48,640]{3,2,1,0:T(8,128)(2,1)S(1)} %pad_maximum_fusion.refs_0_), channel_id=1, source_target_pairs={{0,4},{4,0},{1,5},{5,1},{2,6},{6,2},{3,7},{7,3},{8,12},{12,8},{9,1... | collective-permute-start | bytes 1474568 | tf_op jit(solution)/shard_map/ppermute | solution.py:70
  146.1 9.9 %collective-permute-start.11 = (bf16[1024,768]{1,0:T(8,128)(2,1)}, bf16[1024,768]{1,0:T(8,128)(2,1)S(1)}, u32[]{:S(2)}, u32[]{:S(2)}) collective-permute-start(bf16[1024,768]{1,0:T(8,128)(2,1)} %get-tuple-element.97.da_own), channel_id=1, source_target_pairs={{0,1},{1,0},{2,3},{3,2},{4,5},{5,4},{6,7},{7,6},{8,9},{9,8},{10,11... | collective-permute-start | bytes 4718600 | tf_op jit(solution)/shard_map/ppermute | solution.py:70
  156.0 11.2 %collective-permute-start.12 = (bf16[2,768,768]{2,1,0:T(8,128)(2,1)}, bf16[2,768,768]{2,1,0:T(8,128)(2,1)}, u32[]{:S(2)}, u32[]{:S(2)}) collective-permute-start(bf16[2,768,768]{2,1,0:T(8,128)(2,1)} %get-tuple-element.111), channel_id=1, source_target_pairs={{0,1},{1,0},{2,3},{3,2},{4,5},{5,4},{6,7},{7,6},{8,9},{9,8},{10,11... | collective-permute-start | bytes 7077896 | tf_op jit(solution)/shard_map/ppermute | solution.py:70
  156.2 11.0 %collective-permute-start.13 = (bf16[2,768,768]{2,1,0:T(8,128)(2,1)}, bf16[2,768,768]{2,1,0:T(8,128)(2,1)}, u32[]{:S(2)}, u32[]{:S(2)}) collective-permute-start(bf16[2,768,768]{2,1,0:T(8,128)(2,1)} %get-tuple-element.112), channel_id=1, source_target_pairs={{0,1},{1,0},{2,3},{3,2},{4,5},{5,4},{6,7},{7,6},{8,9},{9,8},{10,11... | collective-permute-start | bytes 7077896 | tf_op jit(solution)/shard_map/ppermute | solution.py:70
  181.2 28.1 %collective-permute-start.14 = (bf16[2,384,768]{2,1,0:T(8,128)(2,1)S(1)}, bf16[2,384,768]{2,1,0:T(8,128)(2,1)S(1)}, u32[]{:S(2)}, u32[]{:S(2)}) collective-permute-start(bf16[2,384,768]{2,1,0:T(8,128)(2,1)S(1)} %get-tuple-element.114), channel_id=1, source_target_pairs={{0,2},{2,0},{1,3},{3,1},{4,6},{6,4},{5,7},{7,5},{8,10},{10,8},{9,1... | collective-permute-start | bytes 3538952 | tf_op jit(solution)/shard_map/ppermute | solution.py:70
  181.2 28.1 %collective-permute-start.15 = (bf16[2,384,768]{2,1,0:T(8,128)(2,1)S(1)}, bf16[2,384,768]{2,1,0:T(8,128)(2,1)S(1)}, u32[]{:S(2)}, u32[]{:S(2)}) collective-permute-start(bf16[2,384,768]{2,1,0:T(8,128)(2,1)S(1)} %get-tuple-element.115), channel_id=1, source_target_pairs={{0,4},{4,0},{1,5},{5,1},{2,6},{6,2},{3,7},{7,3},{8,12},{12,8},{9,1... | collective-permute-start | bytes 3538952 | tf_op jit(solution)/shard_map/ppermute | solution.py:70
  181.9 54.8 %collective-permute-start.18 = (f32[16,768]{1,0:T(8,128)S(1)}, f32[16,768]{1,0:T(8,128)S(1)}, u32[]{:S(2)}, u32[]{:S(2)}) collective-permute-start(f32[16,768]{1,0:T(8,128)S(1)} %copy-done.16), channel_id=1, source_target_pairs={{0,1},{1,0},{2,3},{3,2},{4,5},{5,4},{6,7},{7,6},{8,9},{9,8},{10,11... | collective-permute-start | bytes 147464 | tf_op jit(solution)/shard_map/ppermute | solution.py:70
  209.6 22.2 %collective-permute-start.16 = (bf16[2,192,768]{2,1,0:T(8,128)(2,1)S(1)}, bf16[2,192,768]{2,1,0:T(8,128)(2,1)S(1)}, u32[]{:S(2)}, u32[]{:S(2)}) collective-permute-start(bf16[2,192,768]{2,1,0:T(8,128)(2,1)S(1)} %get-tuple-element.123), channel_id=1, source_target_pairs={{0,4},{4,0},{1,5},{5,1},{2,6},{6,2},{3,7},{7,3},{8,12},{12,8},{9,1... | collective-permute-start | bytes 1769480 | tf_op jit(solution)/shard_map/ppermute | solution.py:70
  210.4 21.3 %collective-permute-start.17 = (bf16[2,192,768]{2,1,0:T(8,128)(2,1)S(1)}, bf16[2,192,768]{2,1,0:T(8,128)(2,1)S(1)}, u32[]{:S(2)}, u32[]{:S(2)}) collective-permute-start(bf16[2,192,768]{2,1,0:T(8,128)(2,1)S(1)} %get-tuple-element.124), channel_id=1, source_target_pairs={{0,2},{2,0},{1,3},{3,1},{4,6},{6,4},{5,7},{7,5},{8,10},{10,8},{9,1... | collective-permute-start | bytes 1769480 | tf_op jit(solution)/shard_map/ppermute | solution.py:70
  232.2 20.6 %collective-permute-start.21 = (bf16[2,96,768]{2,1,0:T(8,128)(2,1)S(1)}, bf16[2,96,768]{2,1,0:T(8,128)(2,1)S(1)}, u32[]{:S(2)}, u32[]{:S(2)}) collective-permute-start(bf16[2,96,768]{2,1,0:T(8,128)(2,1)S(1)} %get-tuple-element.132), channel_id=1, source_target_pairs={{0,8},{8,0},{16,24},{24,16},{1,9},{9,1},{17,25},{25,17},{2,10},{10... | collective-permute-start | bytes 884744 | tf_op jit(solution)/shard_map/ppermute | solution.py:70
  232.3 23.6 %collective-permute-start.22 = (bf16[2,96,768]{2,1,0:T(8,128)(2,1)S(1)}, bf16[2,96,768]{2,1,0:T(8,128)(2,1)S(1)}, u32[]{:S(2)}, u32[]{:S(2)}) collective-permute-start(bf16[2,96,768]{2,1,0:T(8,128)(2,1)S(1)} %get-tuple-element.133), channel_id=1, source_target_pairs={{0,16},{8,24},{16,0},{24,8},{1,17},{9,25},{17,1},{25,9},{2,18},{10... | collective-permute-start | bytes 884744 | tf_op jit(solution)/shard_map/ppermute | solution.py:70
  235.1 20.8 %collective-permute-start.23 = (bf16[2,96,768]{2,1,0:T(8,128)(2,1)S(1)}, bf16[2,96,768]{2,1,0:T(8,128)(2,1)S(1)}, u32[]{:S(2)}, u32[]{:S(2)}) collective-permute-start(bf16[2,96,768]{2,1,0:T(8,128)(2,1)S(1)} %get-tuple-element.134), channel_id=1, source_target_pairs={{0,24},{8,16},{16,8},{24,0},{1,25},{9,17},{17,9},{25,1},{2,26},{10... | collective-permute-start | bytes 884744 | tf_op jit(solution)/shard_map/ppermute | solution.py:70
  244.0 15.1 %collective-permute-start.20 = (bf16[384,768]{1,0:T(8,128)(2,1)S(1)}, bf16[384,768]{1,0:T(8,128)(2,1)S(1)}, u32[]{:S(2)}, u32[]{:S(2)}) collective-permute-start(bf16[384,768]{1,0:T(8,128)(2,1)S(1)} %get-tuple-element.142), channel_id=1, source_target_pairs={{0,4},{4,0},{1,5},{5,1},{2,6},{6,2},{3,7},{7,3},{8,12},{12,8},{9,1... | collective-permute-start | bytes 1769480 | tf_op jit(solution)/shard_map/ppermute | solution.py:70
  247.5 14.4 %collective-permute-start.19 = (bf16[400,768]{1,0:T(8,128)(2,1)S(1)}, bf16[400,768]{1,0:T(8,128)(2,1)S(1)}, u32[]{:S(2)}, u32[]{:S(2)}) collective-permute-start(bf16[400,768]{1,0:T(8,128)(2,1)S(1)} %get-tuple-element.141), channel_id=1, source_target_pairs={{0,2},{2,0},{1,3},{3,1},{4,6},{6,4},{5,7},{7,5},{8,10},{10,8},{9,1... | collective-permute-start | bytes 1843208 | tf_op jit(solution)/shard_map/ppermute | solution.py:70
  262.1 10.4 %collective-permute-start.25 = (bf16[208,768]{1,0:T(8,128)(2,1)S(1)}, bf16[208,768]{1,0:T(8,128)(2,1)S(1)}, u32[]{:S(2)}, u32[]{:S(2)}) collective-permute-start(bf16[208,768]{1,0:T(8,128)(2,1)S(1)} %get-tuple-element.150), channel_id=1, source_target_pairs={{0,4},{4,0},{1,5},{5,1},{2,6},{6,2},{3,7},{7,3},{8,12},{12,8},{9,1... | collective-permute-start | bytes 958472 | tf_op jit(solution)/shard_map/ppermute | solution.py:70
  272.7 9.8 %collective-permute-start.27 = (bf16[112,768]{1,0:T(8,128)(2,1)S(1)}, bf16[112,768]{1,0:T(8,128)(2,1)S(1)}, u32[]{:S(2)}, u32[]{:S(2)}) collective-permute-start(bf16[112,768]{1,0:T(8,128)(2,1)S(1)} %get-tuple-element.158), channel_id=1, source_target_pairs={{0,8},{8,0},{16,24},{24,16},{1,9},{9,1},{17,25},{25,17},{2,10},{10... | collective-permute-start | bytes 516104 | tf_op jit(solution)/shard_map/ppermute | solution.py:70
  275.9 15.6 %collective-permute-start.28 = (bf16[112,768]{1,0:T(8,128)(2,1)S(1)}, bf16[112,768]{1,0:T(8,128)(2,1)S(1)}, u32[]{:S(2)}, u32[]{:S(2)}) collective-permute-start(bf16[112,768]{1,0:T(8,128)(2,1)S(1)} %get-tuple-element.159), channel_id=1, source_target_pairs={{0,16},{8,24},{16,0},{24,8},{1,17},{9,25},{17,1},{25,9},{2,18},{10... | collective-permute-start | bytes 516104 | tf_op jit(solution)/shard_map/ppermute | solution.py:70
  276.9 14.5 %collective-permute-start.29 = (bf16[112,768]{1,0:T(8,128)(2,1)S(1)}, bf16[112,768]{1,0:T(8,128)(2,1)S(1)}, u32[]{:S(2)}, u32[]{:S(2)}) collective-permute-start(bf16[112,768]{1,0:T(8,128)(2,1)S(1)} %get-tuple-element.160), channel_id=1, source_target_pairs={{0,24},{8,16},{16,8},{24,0},{1,25},{9,17},{17,9},{25,1},{2,26},{10... | collective-permute-start | bytes 516104 | tf_op jit(solution)/shard_map/ppermute | solution.py:70
  (48 other events, 576.2 us)
Sparse Core Ops, SparseCore 0:
  10.9 96.7 all-gather.2
